TPU v7x, 32 devices: a whole 2x2x4 slice. The times are simulated.
32 devices in a mesh: group: 2 (over y), seq: 4 (over z), head: 4 (over x, core).
Axes of the slice: x: 2, y: 2, z: 4, core: 2. Of those that a mesh axis runs over, the one named last changes fastest.
Arguments:
- tokens: bfloat16 [4096, 768], P(('group', 'seq')), parts along dimension 0, may hold values from -40 to 40
- w_qkv: bfloat16 [3, 768, 768], P(None, None, 'head'), may hold values from -1 to 1
- w_out: bfloat16 [768, 768], P('head'), may hold values from -0.75 to 0.75
- gain: float32 [768], P('head'), may hold values from 0.5 to 1.5
- bias: float32 [768], P('head'), may hold values from -3 to 3
- mid_offset: int32 [12], P('head'), may hold values from 0 to 7
- far_offset: int32 [12], P('head'), may hold values from 0 to 31
Outputs:
- encoded: bfloat16 [4096, 768], P(('group', 'seq'), 'head'), parts along dimension 0
There are 2 independent parts, one for each index of `group`. A program takes and returns all parts, laid end to end along the dimension named above; an argument that names none is the same for every part. Nothing has to cross between parts.
All inputs are finite; a program needn't handle non-finite values.
Results may differ from a plain program's by a relative error of at most 0.0085.
Values may be sent and summed in bfloat16 or wider, within the bound.
No kernel may reach another device: no remote copies, remote signals or barrier semaphores. Data moves between devices by JAX's collectives and lax.ppermute only.
A program may use at most 64 MiB of HBM per device.

v0:
```python
from functools import partial
import math

import jax
import jax.numpy as jnp
from jax import lax
from jax.sharding import PartitionSpec as P

HEADS = 12
SEG0 = 128
R1 = 8
R2 = 32


epsilon = 1e-05


def attend(queries, keys_in, values_in, scale):
    scores = (
        jnp.einsum("qhd,khd->hqk", queries, keys_in, preferred_element_type=jnp.float32) * scale
    )
    peaks = jnp.max(scores, axis=-1)
    shifted = jnp.exp(scores - peaks[..., None])
    masses = jnp.sum(shifted, axis=-1)
    weights = shifted.astype(jnp.bfloat16)
    summed = jnp.einsum("hqk,khd->qhd", weights, values_in, preferred_element_type=jnp.float32)
    result = summed / jnp.transpose(masses)[:, :, None]
    log_mass = jnp.transpose(peaks + jnp.log(masses))
    return (result, log_mass)


def pick(source, offset, rate):
    folded = source.reshape(source.shape[0] // rate, rate, source.shape[1], source.shape[2])
    chosen = lax.broadcasted_iota(jnp.int32, (rate, source.shape[1]), 0) == offset[None, :]
    kept = jnp.where(chosen[None, :, :, None], folded, jnp.zeros((), source.dtype))
    return jnp.sum(kept, axis=1)


def spread(result, log_mass, offset, rate):
    count = result.shape[0]
    chosen = lax.broadcasted_iota(jnp.int32, (rate, result.shape[1]), 0) == offset[None, :]
    full = jnp.where(chosen[None, :, :, None], result[:, None], 0.0)
    full = full.reshape(count * rate, result.shape[1], result.shape[2])
    mass_full = jnp.where(chosen[None], log_mass[:, None, :], -1e30).reshape(
        count * rate, result.shape[1]
    )
    return (full, mass_full)


def local(tokens, w_qkv, w_out, gain, bias, mid_offset, far_offset):
    rows_here = tokens.shape[0]
    width = tokens.shape[1]
    heads_here = mid_offset.shape[0]
    head_size = width // HEADS
    cols_here = heads_here * head_size
    scale = 1.0 / math.sqrt(head_size)
    projected = jnp.einsum("td,sde->ste", tokens, w_qkv, preferred_element_type=jnp.float32).astype(
        jnp.bfloat16
    )
    query = projected[0].reshape(rows_here, heads_here, head_size)
    keyed = projected[1].reshape(rows_here, heads_here, head_size)
    value = projected[2].reshape(rows_here, heads_here, head_size)
    blocks = rows_here // SEG0
    near_out, near_mass = jax.vmap(partial(attend, scale=scale))(
        query.reshape(blocks, SEG0, heads_here, head_size),
        keyed.reshape(blocks, SEG0, heads_here, head_size),
        value.reshape(blocks, SEG0, heads_here, head_size),
    )
    near_out = near_out.reshape(rows_here, heads_here, head_size)
    near_mass = near_mass.reshape(rows_here, heads_here)
    mid_count = rows_here // R1
    far_count = rows_here // R2
    mid_query = pick(query, mid_offset, R1)
    mid_stack = jnp.stack(
        [
            pick(keyed, mid_offset, R1).reshape(mid_count, cols_here),
            pick(value, mid_offset, R1).reshape(mid_count, cols_here),
        ]
    )
    far_query = pick(query, far_offset, R2)
    far_stack = jnp.stack(
        [
            pick(keyed, far_offset, R2).reshape(far_count, cols_here),
            pick(value, far_offset, R2).reshape(far_count, cols_here),
        ]
    )
    mid_devs = min(8, lax.axis_size("seq"))
    place = lax.axis_index("seq")
    gathered_mid, far_all = (
        lax.all_gather(mid_stack, "seq", axis=1, tiled=True),
        lax.all_gather(far_stack, "seq", axis=1, tiled=True),
    )
    first_row = place // mid_devs * (mid_devs * mid_count)
    mid_all = lax.dynamic_slice_in_dim(gathered_mid, first_row, mid_devs * mid_count, 1)
    mid_out, mid_mass = attend(
        mid_query,
        mid_all[0].reshape(-1, heads_here, head_size),
        mid_all[1].reshape(-1, heads_here, head_size),
        scale,
    )
    far_out, far_mass = attend(
        far_query,
        far_all[0].reshape(-1, heads_here, head_size),
        far_all[1].reshape(-1, heads_here, head_size),
        scale,
    )
    mid_full, mid_mfull = spread(mid_out, mid_mass, mid_offset, R1)
    far_full, far_mfull = spread(far_out, far_mass, far_offset, R2)
    top = jnp.maximum(jnp.maximum(near_mass, mid_mfull), far_mfull)
    near_weight = jnp.exp(near_mass - top)
    mid_weight = jnp.exp(mid_mfull - top)
    far_weight = jnp.exp(far_mfull - top)
    mixed = (
        near_weight[..., None] * near_out
        + mid_weight[..., None] * mid_full
        + far_weight[..., None] * far_full
    )
    mixed = mixed / (near_weight + mid_weight + far_weight)[..., None]
    attn = mixed.reshape(rows_here, cols_here).astype(jnp.bfloat16)
    head_count = lax.axis_size("head")
    head_place = lax.axis_index("head")
    piece_cols = width // head_count
    weight_cols = lax.all_to_all(w_out, "head", split_axis=1, concat_axis=0, tiled=True)
    summed = jnp.dot(
        lax.all_gather(attn, "head", axis=1, tiled=True),
        weight_cols,
        preferred_element_type=jnp.float32,
    )
    resid = (
        lax.dynamic_slice_in_dim(tokens, head_place * piece_cols, piece_cols, 1).astype(jnp.float32)
        + summed
    )
    totals, squares = lax.psum((jnp.sum(resid, axis=1), jnp.sum(resid * resid, axis=1)), "head")
    mean = totals / width
    var = squares / width - mean * mean
    normed_cols = (resid - mean[:, None]) * lax.rsqrt(var + epsilon)[:, None]
    return (normed_cols * gain + bias).astype(jnp.bfloat16)


def solution(mesh):
    in_specs = (
        P(("group", "seq"), None),
        P(None, None, "head"),
        P("head", None),
        P("head"),
        P("head"),
        P("head"),
        P("head"),
    )
    out_specs = P(("group", "seq"), "head")
    return jax.shard_map(local, mesh=mesh, in_specs=in_specs, out_specs=out_specs, check_vma=False)
```

profile of v0, /device:TPU:0, one launch (start us, length us, event | category | flops | bytes accessed | tf_op | source)
XLA Modules:
  0.0 76.6 jit_solution(17679054772339913622)
XLA Ops:
  0.0 2.0 %copy.128 = bf16[192,768]{0,1:T(8,128)(2,1)} copy(bf16[192,768]{1,0:T(8,128)(2,1)} %param.9) | data formatting | bytes 589824 | tf_op args[2]
  2.0 4.2 %all-to-all-start = ((bf16[192,4,192]{0,2,1:T(8,128)(2,1)}), bf16[192,4,192]{0,2,1:T(8,128)(2,1)}, u32[]{:S(2)}, u32[]{:S(2)}) async-start(bf16[192,4,192]{0,2,1:T(8,128)(2,1)} %bitcast.24), calls=%async_computation | async-start | bytes 786432 | tf_op jit(solution)/shard_map/all_to_all | solution.py:123
  6.2 0.7 fusion
  7.7 1.0 %reshape_reshape_squeeze.30 = bf16[64,8,3,64]{3,2,1,0:T(4,128)(2,1)} reshape(bf16[1,512,192]{2,1,0:T(8,128)(2,1)S(1)} %copy.104) | data formatting | bytes 393216 | tf_op jit(solution)/shard_map/reshape;reshape;squeeze | solution.py:33
  9.0 0.9 %reshape_reshape_squeeze.31 = bf16[64,8,3,64]{3,2,1,0:T(4,128)(2,1)} reshape(bf16[1,512,192]{2,1,0:T(8,128)(2,1)S(1)} %copy.106) | data formatting | bytes 393216 | tf_op jit(solution)/shard_map/reshape;reshape;squeeze | solution.py:33
  10.1 1.7 %reshape_reshape_squeeze.27 = bf16[4,128,3,64]{1,0,3,2:T(4,128)(2,1)} reshape(bf16[1,512,192]{1,2,0:T(8,128)(2,1)} %copy-done.4) | data formatting | bytes 393216 | tf_op jit(solution)/shard_map/reshape;reshape;squeeze | solution.py:65
  11.8 1.7 %reshape_reshape_squeeze.28 = bf16[4,128,3,64]{1,0,3,2:T(4,128)(2,1)} reshape(bf16[1,512,192]{1,2,0:T(8,128)(2,1)} %copy-done.3) | data formatting | bytes 393216 | tf_op jit(solution)/shard_map/reshape;reshape;squeeze | solution.py:66
  13.4 1.7 %reshape_reshape_squeeze.35 = bf16[4,128,3,64]{1,0,3,2:T(4,128)(2,1)} reshape(bf16[1,512,192]{1,2,0:T(8,128)(2,1)} %copy-done.2) | data formatting | bytes 393216 | tf_op jit(solution)/shard_map/reshape;reshape;squeeze | solution.py:67
  15.2 3.4 %select_reduce_fusion.5 = (bf16[64,3,64]{2,1,0:T(4,128)(2,1)}, bf16[64,3,64]{2,1,0:T(4,128)(2,1)}, bf16[64,3,64]{2,1,0:T(4,128)(2,1)}) fusion(bf16[64,8,3,64]{3,2,1,0:T(4,128)(2,1)S(1)} %reshape_reshape_squeeze.29, pred[8,3]{1,0:T(8,128)(4,1)S(1)} %iota_compare_fusion.1, bf16[64,8,3,64]{3,2,1,0:T(4,128)(2,1)S(1)} %copy-done.1, ...), kind=kLoop, calls=%fused_computation.21 | loop fusion | flops 552960 | bytes 663576 | tf_op jit(solution)/shard_map/reduce_sum | solution.py:36
  18.6 0.9 %copy.105 = bf16[64,3,64]{0,2,1:T(8,128)(2,1)S(1)} copy(bf16[64,3,64]{2,1,0:T(4,128)(2,1)} %get-tuple-element.11) | data formatting | bytes 49152 | tf_op jit(solution)/shard_map/reduce_sum | solution.py:36
  19.5 0.9 %copy.107 = bf16[64,3,64]{0,2,1:T(8,128)(2,1)S(1)} copy(bf16[64,3,64]{2,1,0:T(4,128)(2,1)} %get-tuple-element.12) | data formatting | bytes 49152 | tf_op jit(solution)/shard_map/reduce_sum | solution.py:36
  20.6 15.6 %all_gather.9 = bf16[2,256,192]{2,0,1:T(2,128)(2,1)S(1)} all-gather(bf16[2,64,192]{2,0,1:T(2,128)(2,1)S(1)} %copy.108), channel_id=1, replica_groups=mesh['group'=2,'seq'=4,'head'=4] {'seq'}, dimensions={1}, use_global_device_ids=true | all-gather | bytes 245760 | tf_op jit(solution)/shard_map/all_gather | solution.py:90
  36.2 0.4 fusion.31
  36.8 0.2 fusion.34
  37.5 1.1 %select_reduce_fusion.2 = (bf16[16,3,64]{2,1,0:T(4,128)(2,1)S(1)}, bf16[16,3,64]{2,1,0:T(4,128)(2,1)S(1)}, bf16[16,3,64]{2,1,0:T(4,128)(2,1)S(1)}) fusion(bf16[16,32,3,64]{3,2,1,0:T(4,128)(2,1)S(1)} %reshape_reshape_squeeze.32, pred[32,3]{1,0:T(8,128)(4,1)S(1)} %iota_compare_fusion, bf16[16,32,3,64]{3,2,1,0:T(4,128)(2,1)S(1)} %reshape_reshape_squeeze.33, ...), kind=kLoop, calls=%fused_computation.18 | loop fusion | flops 580608 | bytes 608352 | tf_op jit(solution)/shard_map/reduce_sum | solution.py:36
  38.9 13.3 %all_gather.10 = bf16[2,64,192]{2,1,0:T(8,128)(2,1)S(1)} all-gather(bf16[2,16,192]{2,1,0:T(8,128)(2,1)S(1)} %pad_maximum_fusion.1), channel_id=1, replica_groups=mesh['group'=2,'seq'=4,'head'=4] {'seq'}, dimensions={1}, use_global_device_ids=true | all-gather | bytes 61440 | tf_op jit(solution)/shard_map/all_gather | solution.py:91
  52.3 0.2 fusion.33
  53.3 0.2 fusion.2
  53.8 0.6 broadcast_in_dim.184
  54.6 0.2 fusion.3
  55.0 0.6 broadcast_in_dim.189
  56.1 0.3 fusion.35
  56.5 0.5 copy-done.8
  57.0 0.3 fusion.1
  57.2 0.3 copy.120
  57.5 1.1 %constant_dynamic-slice_fusion = bf16[512,192]{1,0:T(8,128)(2,1)S(1)} fusion(bf16[512,768]{1,0:T(8,128)(2,1)} %param.7, s32[]{:T(128)S(6)} %select_n.99), kind=kLoop, calls=%fused_computation.61 | loop fusion | bytes 393220 | tf_op jit(solution)/shard_map/dynamic_slice | solution.py:130
  59.0 8.8 %all_gather.11 = bf16[512,768]{0,1:T(8,128)(2,1)S(1)} all-gather(bf16[512,192]{0,1:T(8,128)(2,1)S(1)} %fusion.12), channel_id=1, replica_groups=mesh['group'=2,'seq'=4,'head'=4] {'head'}, dimensions={1}, use_global_device_ids=true | all-gather | bytes 983040 | tf_op jit(solution)/shard_map/all_gather | solution.py:125
  67.8 1.3 %copy.129 = bf16[4,192,192]{1,0,2:T(4,128)(2,1)S(1)} copy(bf16[4,192,192]{1,2,0:T(8,128)(2,1)} %bitcast.25) | data formatting | bytes 589824 | tf_op jit(solution)/shard_map/all_to_all | solution.py:123
  69.1 0.3 all_to_all.17
  69.4 0.3 fusion.28
  69.8 6.0 %all-reduce = (f32[512]{0:T(512)S(1)}, f32[512]{0:T(512)S(1)}) all-reduce(f32[512]{0:T(512)S(1)} %get-tuple-element.6, f32[512]{0:T(512)S(1)} %get-tuple-element.5), channel_id=1, replica_groups=mesh['group'=2,'seq'=4,'head'=4] {'head'}, use_global_device_ids=true, to_apply=%region_15.16 | all-reduce | flops 1024 | bytes 8192 | tf_op jit(solution)/shard_map/psum | solution.py:133
  75.8 0.8 %add_convert_fusion = bf16[512,192]{0,1:T(8,128)(2,1)} fusion(f32[512,192]{0,1:T(8,128)S(1)} %get-tuple-element.34, f32[192]{0:T(256)S(1)} %copy-done.10, f32[192]{0:T(256)S(1)} %copy-done.11, f32[512]{0:T(512)S(1)} %get-tuple-element.27, f32[512]{0:T(512)S(1)} %get-tuple-element.26), kind=kLoop, calls=%fused_computation.28 | loop fusion | flops 491520 | bytes 595456 | tf_op jit(solution)/shard_map/convert_element_type | solution.py:137
  (73 shorter events, 4.7 us)
Async XLA Ops:
  0.0 6.2 %copy-start = (bf16[3,768,192]{1,2,0:T(8,128)(2,1)S(1)}, bf16[3,768,192]{1,2,0:T(8,128)(2,1)}, u32[]{:S(2)}) copy-start(bf16[3,768,192]{1,2,0:T(8,128)(2,1)} %param.8) | copy-start | bytes 2654212
  0.0 6.2 %copy-start.9 = (bf16[512,768]{1,0:T(8,128)(2,1)S(1)}, bf16[512,768]{1,0:T(8,128)(2,1)}, u32[]{:S(2)}) copy-start(bf16[512,768]{1,0:T(8,128)(2,1)} %param.7) | copy-start | bytes 2359300
  2.0 65.7 %all-to-all-start = ((bf16[192,4,192]{0,2,1:T(8,128)(2,1)}), bf16[192,4,192]{0,2,1:T(8,128)(2,1)}, u32[]{:S(2)}, u32[]{:S(2)}) async-start(bf16[192,4,192]{0,2,1:T(8,128)(2,1)} %bitcast.24), calls=%async_computation | async-start | bytes 786432 | tf_op jit(solution)/shard_map/all_to_all | solution.py:123
  6.9 0.7 copy-start.3
  7.0 0.7 copy-start.4
  7.0 1.8 %copy-start.2 = (bf16[1,512,192]{1,2,0:T(8,128)(2,1)}, bf16[1,512,192]{1,2,0:T(8,128)(2,1)S(1)}, u32[]{:S(2)}) copy-start(bf16[1,512,192]{1,2,0:T(8,128)(2,1)S(1)} %get-tuple-element.19) | copy-start | bytes 589828
  9.9 5.2 %copy-start.13 = (s32[3]{0:T(128)S(1)}, s32[3]{0:T(128)}, u32[]{:S(2)}) copy-start(s32[3]{0:T(128)} %param.12) | copy-start | bytes 40
  10.0 5.1 %copy-start.1 = (bf16[64,8,3,64]{3,2,1,0:T(4,128)(2,1)S(1)}, bf16[64,8,3,64]{3,2,1,0:T(4,128)(2,1)}, u32[]{:S(2)}) copy-start(bf16[64,8,3,64]{3,2,1,0:T(4,128)(2,1)} %reshape_reshape_squeeze.30) | copy-start | bytes 589828
  20.5 16.3 %copy-start.7 = (bf16[64,3,64]{2,1,0:T(4,128)(2,1)S(1)}, bf16[64,3,64]{2,1,0:T(4,128)(2,1)}, u32[]{:S(2)}) copy-start(bf16[64,3,64]{2,1,0:T(4,128)(2,1)} %get-tuple-element.10) | copy-start | bytes 73732
  36.2 1.2 %copy-start.12 = (s32[3]{0:T(128)S(1)}, s32[3]{0:T(128)}, u32[]{:S(2)}) copy-start(s32[3]{0:T(128)} %param.13) | copy-start | bytes 40
  55.0 0.9 %copy-start.5 = (bf16[4,128,3,64]{1,0,3,2:T(4,128)(2,1)S(1)}, bf16[4,128,3,64]{1,0,3,2:T(4,128)(2,1)}, u32[]{:S(2)}) copy-start(bf16[4,128,3,64]{1,0,3,2:T(4,128)(2,1)} %reshape_reshape_squeeze.27) | copy-start | bytes 589828
  55.0 1.0 %copy-start.6 = (bf16[4,128,3,64]{1,0,3,2:T(4,128)(2,1)S(1)}, bf16[4,128,3,64]{1,0,3,2:T(4,128)(2,1)}, u32[]{:S(2)}) copy-start(bf16[4,128,3,64]{1,0,3,2:T(4,128)(2,1)} %reshape_reshape_squeeze.28) | copy-start | bytes 589828
  56.0 0.9 %copy-start.8 = (bf16[4,128,3,64]{1,0,3,2:T(4,128)(2,1)S(1)}, bf16[4,128,3,64]{1,0,3,2:T(4,128)(2,1)}, u32[]{:S(2)}) copy-start(bf16[4,128,3,64]{1,0,3,2:T(4,128)(2,1)} %reshape_reshape_squeeze.35) | copy-start | bytes 589828
  69.1 6.7 %copy-start.10 = (f32[192]{0:T(256)S(1)}, f32[192]{0:T(256)}, u32[]{:S(2)}) copy-start(f32[192]{0:T(256)} %param.11) | copy-start | bytes 2308
  69.1 6.7 %copy-start.11 = (f32[192]{0:T(256)S(1)}, f32[192]{0:T(256)}, u32[]{:S(2)}) copy-start(f32[192]{0:T(256)} %param.10) | copy-start | bytes 2308
where the time goes:
time: 77.2 us; the launch traced here: 76.6 us
  blocking collectives  43.7 us (57%)
  local copies, waits for them, and re-layouts  19.7 us (26%)
  other arithmetic  6.08 us (8%)
  starting transfers between devices  4.21 us (5%)
  matrix products  2.49 us (3%)
    all_gather x1, blocking collectives, local(): lax.all_gather(mid_stack, 'seq', axis=1, tiled=True)  15.6 us
    all_gather x1, blocking collectives, local(): lax.all_gather(far_stack, 'seq', axis=1, tiled=True)  13.3 us
    all_gather x1, blocking collectives, local(): lax.all_gather(attn, 'head', axis=1, tiled=True)  8.79 us
    psum x1, blocking collectives, local(): lax.psum((jnp.sum(resid, axis=1), jnp.sum(resid * resid, axis=1)), 'head')  6.01 us
    reduce_sum x2, other arithmetic, pick(): return jnp.sum(kept, axis=1)  4.51 us
    all_to_all x1, starting transfers between devices, local(): lax.all_to_all(w_out, 'head', split_axis=1, concat_axis=0, tiled=True)  4.21 us
    unnamed x30, local copies, waits for them, and re-layouts  3.03 us
    another operation x6, local copies, waits for them, and re-layouts, pick(): source.reshape(source.shape[0] // rate, rate, source.shape[1], source.sha...  2.48 us
  transfers between devices with their start and end apart: 1, of which 0 were waited for; matrix products, arithmetic and copies ran while one was open for 29% of the time, Pallas kernels for 0%

commit v1 on v0

v1 whole, which is shorter than its diff:
```python
from functools import partial
import math

import jax
import jax.numpy as jnp
from jax import lax
from jax.experimental import pallas as pl
from jax.experimental.pallas import tpu as pltpu
from jax.sharding import PartitionSpec as P

HEADS = 12
SEG0 = 128
R1 = 8
R2 = 32
LANES = 128
HALF = 64

epsilon = 1e-05
f32 = jnp.float32
bf16 = jnp.bfloat16

NT = (((1,), (1,)), ((), ()))


def lane_half(shape):
    return lax.broadcasted_iota(jnp.int32, shape, 1) < HALF


def acc_low(head):
    return head % 2 == 0


def project_kernel(mo, fo, x_ref, w_ref, qkv_ref, kvp_ref, qp_ref, scr):
    rows = x_ref.shape[0]
    mid, far = rows // R1, rows // R2
    per = mid + far
    q = [w_ref[0, h * HALF : (h + 1) * HALF] for h in range(3)]
    k = [w_ref[1, h * HALF : (h + 1) * HALF] for h in range(3)]
    v = [w_ref[2, h * HALF : (h + 1) * HALF] for h in range(3)]
    w = jnp.concatenate(
        [v[0], k[0], k[1], v[1], v[2], k[2], q[1], q[0], q[2], q[2]], axis=0
    )
    y = lax.dot_general(x_ref[...], w, NT, preferred_element_type=f32).astype(bf16)
    qkv_ref[...] = y
    for i in range(5):
        scr[i] = y[:, i * LANES : (i + 1) * LANES].astype(f32)
    for h in range(3):
        asked = 3 + h // 2
        low = lane_half((mid, LANES))
        keep = jnp.logical_not(low) if acc_low(h) else low
        mid_rows = pl.ds(mo[h], mid, stride=R1)
        far_rows = pl.ds(fo[h], far, stride=R2)
        kvp_ref[h * per : h * per + mid] = scr[h, mid_rows].astype(bf16)
        kvp_ref[h * per + mid : (h + 1) * per] = scr[h, far_rows].astype(bf16)
        qp_ref[h * per : h * per + mid] = jnp.where(keep, scr[asked, mid_rows], 0.0).astype(bf16)
        qp_ref[h * per + mid : (h + 1) * per] = jnp.where(
            keep[:far], scr[asked, far_rows], 0.0
        ).astype(bf16)


def soft(queries, keys_values, head, factor):
    s = lax.dot_general(queries, keys_values, NT, preferred_element_type=f32)
    peak = jnp.max(s, axis=1, keepdims=True)
    p = jnp.exp2((s - peak) * factor).astype(bf16)
    low = lane_half(keys_values.shape)
    is_value = low if acc_low(head) else jnp.logical_not(low)
    values = jnp.where(is_value, keys_values, jnp.ones((), bf16))
    return peak, jnp.dot(p, values, preferred_element_type=f32)


def near_kernel(factor, mo, fo, qkv_ref, near_ref, am_ref, pk_ref, am_scr, pk_scr):
    rows = qkv_ref.shape[0]
    mid, far = rows // R1, rows // R2
    per = mid + far
    low = lane_half((SEG0, LANES))
    for b in range(rows // SEG0):
        at = slice(b * SEG0, (b + 1) * SEG0)
        done = []
        for h in range(3):
            keep = jnp.logical_not(low) if acc_low(h) else low
            first = (3 + h // 2) * LANES
            queries = jnp.where(keep, qkv_ref[at, first : first + LANES], jnp.zeros((), bf16))
            peak, am = soft(queries, qkv_ref[at, h * LANES : (h + 1) * LANES], h, factor)
            am_scr[h, at] = am
            pk_scr[h, at] = jnp.broadcast_to(peak, am.shape)
            done.append(am / pltpu.roll(am, HALF, 1))
        near_ref[at, :LANES] = jnp.where(low, done[0], done[1]).astype(bf16)
        near_ref[at, LANES:] = jnp.where(low, done[2], 0.0).astype(bf16)
    for h in range(3):
        for first, picked in (
            (h * per, pl.ds(mo[h], mid, stride=R1)),
            (h * per + mid, pl.ds(fo[h], far, stride=R2)),
        ):
            count = mid if first == h * per else far
            am_ref[first : first + count] = am_scr[h, picked]
            pk_ref[first : first + count] = pk_scr[h, picked]


def merge_kernel(factor, mid_n, far_n, mo, fo, qp_ref, am_ref, pk_ref, *rest):
    mids, fars = rest[:mid_n], rest[mid_n : mid_n + far_n]
    corr_ref, am_scr, pk_scr = rest[mid_n + far_n :]
    mid, far = corr_ref.shape[0] * 4 // 5, corr_ref.shape[0] // 5
    per = mid + far
    out_mid, out_far = [], []
    for h in range(3):
        own = slice(h * per, h * per + mid)
        own_far = slice(h * per + mid, (h + 1) * per)
        kv_mid = jnp.concatenate([m[h] for m in mids], axis=0)
        kv_far = jnp.concatenate([m[h] for m in fars], axis=0)
        peak_mid, am_mid = soft(qp_ref[own], kv_mid, h, factor)
        peak_far, am_far = soft(qp_ref[own_far], kv_far, h, factor)
        peak_mid = jnp.broadcast_to(peak_mid, am_mid.shape)
        am_scr[h] = am_mid
        pk_scr[h] = peak_mid
        near_peak, near_am = pk_ref[own], am_ref[own]
        top = jnp.maximum(near_peak, peak_mid)
        total = (
            jnp.exp2((near_peak - top) * factor) * near_am
            + jnp.exp2((peak_mid - top) * factor) * am_mid
        )
        out_mid.append(total / pltpu.roll(total, HALF, 1))
        shared = pl.ds(fo[h] // R1, far, stride=R2 // R1)
        also = fo[h] % R1 == mo[h]
        both_peak = jnp.where(also, pk_scr[h, shared], -1e30)
        both_am = am_scr[h, shared]
        near_peak, near_am = pk_ref[own_far], am_ref[own_far]
        top = jnp.maximum(jnp.maximum(near_peak, both_peak), peak_far)
        total = (
            jnp.exp2((near_peak - top) * factor) * near_am
            + jnp.exp2((both_peak - top) * factor) * both_am
            + jnp.exp2((peak_far - top) * factor) * am_far
        )
        out_far.append(total / pltpu.roll(total, HALF, 1))
    for first, out in ((0, out_mid), (mid, out_far)):
        at = slice(first, first + out[0].shape[0])
        low = lane_half(out[0].shape)
        corr_ref[at, :LANES] = jnp.where(low, out[0], out[1]).astype(bf16)
        corr_ref[at, LANES:] = jnp.where(low, out[2], 0.0).astype(bf16)


def output_kernel(head_count, place, mo, fo, x_ref, gain_ref, bias_ref, *rest):
    near, corr, weights = (rest[i * head_count : (i + 1) * head_count] for i in range(3))
    out_ref, attn_scr, resid_scr = rest[3 * head_count :]
    rows, width = x_ref.shape
    mid, far = rows // R1, rows // R2
    cols = width // head_count
    resid = x_ref[...].astype(f32)
    low = lane_half((rows, LANES))
    for r in range(head_count):
        for h in range(3):
            tile = slice(h // 2 * LANES, (h // 2 + 1) * LANES)
            attn_scr[r, h] = near[r][:, tile].astype(f32)
            attn_scr[r, h, pl.ds(mo[r, h], mid, stride=R1)] = corr[r][:mid, tile].astype(f32)
            attn_scr[r, h, pl.ds(fo[r, h], far, stride=R2)] = corr[r][mid:, tile].astype(f32)
        pair = jnp.where(low, attn_scr[r, 0], attn_scr[r, 1]).astype(bf16)
        attn = jnp.concatenate([pair, attn_scr[r, 2].astype(bf16)[:, :HALF]], axis=1)
        resid += jnp.dot(attn, weights[r][...], preferred_element_type=f32)
    mean = jnp.sum(resid, axis=1, keepdims=True) / width
    var = jnp.sum(resid * resid, axis=1, keepdims=True) / width - mean * mean
    inv = lax.rsqrt(var + epsilon)
    resid_scr[...] = resid
    for i in range(head_count):

        @pl.when(place[0] == i)
        def _():
            mine = resid_scr[:, i * cols : (i + 1) * cols]
            normed = (mine - mean) * inv * gain_ref[...] + bias_ref[...]
            out_ref[...] = normed.T.astype(bf16)


def vmem(*shape_dtypes):
    return [pltpu.VMEM(shape, dtype) for shape, dtype in shape_dtypes]


IN_VMEM = pl.BlockSpec(memory_space=pltpu.VMEM)
IN_SMEM = pl.BlockSpec(memory_space=pltpu.SMEM)


def call(kernel, outs, scratch, scalars, arrays, name):
    return pl.pallas_call(
        kernel,
        out_shape=outs,
        in_specs=[IN_SMEM] * len(scalars) + [IN_VMEM] * len(arrays),
        out_specs=jax.tree.map(lambda _: IN_VMEM, outs),
        scratch_shapes=vmem(*scratch),
        compiler_params=pltpu.CompilerParams(vmem_limit_bytes=48 << 20),
        name=name,
    )(*scalars, *arrays)


def local(tokens, w_qkv, w_out, gain, bias, mid_offset, far_offset):
    rows, width = tokens.shape
    heads_here = mid_offset.shape[0]
    head_size = width // HEADS
    cols = heads_here * head_size
    factor = math.log2(math.e) / math.sqrt(head_size)
    mid, far = rows // R1, rows // R2
    per = mid + far
    shape = jax.ShapeDtypeStruct

    qkv, kvp, qp = call(
        project_kernel,
        (
            shape((rows, 5 * LANES), bf16),
            shape((3 * per, LANES), bf16),
            shape((3 * per, LANES), bf16),
        ),
        [((5, rows, LANES), f32)],
        (mid_offset, far_offset),
        (tokens, jnp.swapaxes(w_qkv, 1, 2)),
        "project",
    )

    seq_count = lax.axis_size("seq")
    mid_devs = min(8, seq_count)

    def within(step):
        return [
            (i, i // mid_devs * mid_devs + (i + step) % mid_devs) for i in range(seq_count)
        ]

    if mid_devs == seq_count:
        pieces = [kvp] + [lax.ppermute(kvp, "seq", within(s)) for s in range(1, mid_devs)]
        pieces = [p.reshape(3, per, LANES) for p in pieces]
        mids = [p[:, :mid] for p in pieces]
        fars = [p[:, mid:] for p in pieces]
    else:
        split = kvp.reshape(3, per, LANES)
        piece = split[:, :mid]
        mids = [piece] + [lax.ppermute(piece, "seq", within(s)) for s in range(1, mid_devs)]
        fars = [lax.all_gather(split[:, mid:], "seq", axis=1, tiled=True)]

    head_count = lax.axis_size("head")
    if head_count & (head_count - 1) == 0:
        paths = [[(i, i ^ r) for i in range(head_count)] for r in range(head_count)]
    else:
        paths = [[(i, (i + r) % head_count) for i in range(head_count)] for r in range(head_count)]

    def spread(array):
        return [array] + [lax.ppermute(array, "head", paths[r]) for r in range(1, head_count)]

    def relay(array):
        if head_count != 4:
            return spread(array)
        across = lax.ppermute(array, "head", paths[2])
        beside = lax.ppermute(array, "head", paths[1])
        return [array, beside, across, lax.ppermute(across, "head", paths[1])]

    weights = relay(w_out)
    offsets = spread(jnp.concatenate([mid_offset, far_offset]))
    offsets = jnp.stack(offsets)

    near, am, pk = call(
        partial(near_kernel, factor),
        (
            shape((rows, 2 * LANES), bf16),
            shape((3 * per, LANES), f32),
            shape((3 * per, LANES), f32),
        ),
        [((3, rows, LANES), f32)] * 2,
        (mid_offset, far_offset),
        (qkv,),
        "near",
    )
    nears = relay(near)

    corr = call(
        partial(merge_kernel, factor, len(mids), len(fars)),
        shape((per, 2 * LANES), bf16),
        [((3, mid, LANES), f32)] * 2,
        (mid_offset, far_offset),
        (qp, am, pk, *mids, *fars),
        "merge",
    )
    corrs = spread(corr)

    out = call(
        partial(output_kernel, head_count),
        shape((cols, rows), bf16),
        [((head_count, 3, rows, LANES), f32), ((rows, width), f32)],
        (
            lax.axis_index("head").reshape(1),
            offsets[:, :heads_here],
            offsets[:, heads_here:],
        ),
        (tokens, gain.reshape(1, cols), bias.reshape(1, cols), *nears, *corrs, *weights),
        "output",
    )
    return out.T


def solution(mesh):
    in_specs = (
        P(("group", "seq"), None),
        P(None, None, "head"),
        P("head", None),
        P("head"),
        P("head"),
        P("head"),
        P("head"),
    )
    out_specs = P(("group", "seq"), "head")
    return jax.shard_map(local, mesh=mesh, in_specs=in_specs, out_specs=out_specs, check_vma=False)
```

time: 77.2 us -> 37.3 us (0.48)
  blocking collectives: 43.7 us -> 0 us
  local copies, waits for them, and re-layouts: 19.7 us -> 3.08 us
  starting transfers between devices: 4.21 us -> 14.5 us
  waiting for transfers between devices: 0.01 us -> 9.74 us
  Pallas kernels: 0 us -> 9.67 us
  other arithmetic: 6.08 us -> 0.09 us
  matrix products: 2.49 us -> 0 us
    all_gather x3 -> x0, blocking collectives: 37.7 us -> none  [the longest x1 15.6 us: local(): lax.all_gather(mid_stack, 'seq', axis=1, tiled=True)]
    ppermute x0 -> x15, starting transfers between devices: none -> 14.5 us  [the longest x6 5.16 us: spread(): lax.ppermute(array, 'head', paths[r])]
    ppermute x0 -> x15, waiting for transfers between devices: none -> 9.74 us  [the longest x3 4.99 us: local(): lax.ppermute(kvp, 'seq', within(s))]
    pallas_call x0 -> x4, Pallas kernels: none -> 9.67 us  [call(): pl.pallas_call(kernel, out_shape=outs, in_specs=[IN_SMEM] * len(scalars)...]
    another operation x12 -> x0, local copies, waits for them, and re-layouts: 7.78 us -> none  [the longest x6 2.48 us: pick(): source.reshape(source.shape[0] // rate, rate, source.shape[1], source.sha...]
    psum x1 -> x0, blocking collectives: 6.01 us -> none  [local(): lax.psum((jnp.sum(resid, axis=1), jnp.sum(resid * resid, axis=1)), 'head')]
    reduce_sum x5 -> x0, other arithmetic: 5.01 us -> none  [the longest x2 4.51 us: pick(): return jnp.sum(kept, axis=1)]
    all_to_all x1 -> x0, starting transfers between devices: 4.21 us -> none  [local(): lax.all_to_all(w_out, 'head', split_axis=1, concat_axis=0, tiled=True)]
  transfers between devices with their start and end apart: 1 -> 15, of which waited for: 0 -> 7; matrix products, arithmetic and copies ran while one was open for 29% -> 0% of each run, Pallas kernels for 0% -> 18%
where the time goes in v1:
time: 37.3 us; the launch traced here: 37.1 us
  starting transfers between devices  14.5 us (39%)
  waiting for transfers between devices  9.74 us (26%)
  Pallas kernels  9.67 us (26%)
  local copies, waits for them, and re-layouts  3.08 us (8%)
    pallas_call x4, Pallas kernels, call(): pl.pallas_call(kernel, out_shape=outs, in_specs=[IN_SMEM] * len(scalars)...  9.67 us
    ppermute x6, starting transfers between devices, spread(): lax.ppermute(array, 'head', paths[r])  5.16 us
    ppermute x3, waiting for transfers between devices, local(): lax.ppermute(kvp, 'seq', within(s))  4.99 us
    ppermute x6, waiting for transfers between devices, spread(): lax.ppermute(array, 'head', paths[r])  4.74 us
    ppermute x3, starting transfers between devices, local(): lax.ppermute(kvp, 'seq', within(s))  4.61 us
    ppermute x2, starting transfers between devices, relay(): across = lax.ppermute(array, 'head', paths[2])  3.67 us
    unnamed x16, local copies, waits for them, and re-layouts  2.98 us
  transfers between devices with their start and end apart: 15, of which 7 were waited for; matrix products, arithmetic and copies ran while one was open for 0% of the time, Pallas kernels for 18%

profile of v1, /device:TPU:0, one launch (start us, length us, event | category | flops | bytes accessed | tf_op | source)
XLA Modules:
  0.0 37.1 jit_solution(15177680033673595793)
XLA Ops:
  0.0 2.9 %collective-permute-start.13 = (bf16[192,768]{1,0:T(8,128)(2,1)}, bf16[192,768]{1,0:T(8,128)(2,1)S(1)}, u32[]{:S(2)}, u32[]{:S(2)}) collective-permute-start(bf16[192,768]{1,0:T(8,128)(2,1)} %rest_8_.1), channel_id=1, source_target_pairs={{0,2},{1,3},{2,0},{3,1},{4,6},{5,7},{6,4},{7,5},{8,10},{9,11},{10,... | collective-permute-start | bytes 884744 | tf_op jit(solution)/shard_map/ppermute | solution.py:245
  3.0 1.1 %copy-done = bf16[512,768]{1,0:T(8,128)(2,1)S(1)} copy-done((bf16[512,768]{1,0:T(8,128)(2,1)S(1)}, bf16[512,768]{1,0:T(8,128)(2,1)}, u32[]{:S(2)}) %copy-start) | copy-done | bytes 786456
  4.1 1.2 %copy-done.2 = bf16[3,768,192]{1,2,0:T(8,128)(2,1)S(1)} copy-done((bf16[3,768,192]{1,2,0:T(8,128)(2,1)S(1)}, bf16[3,768,192]{1,2,0:T(8,128)(2,1)}, u32[]{:S(2)}) %copy-start.2) | copy-done | bytes 884760
  5.3 1.5 %project.1 = (bf16[512,640]{1,0:T(8,128)(2,1)S(1)}, bf16[240,128]{1,0:T(8,128)(2,1)S(1)}, bf16[240,128]{1,0:T(8,128)(2,1)S(1)}) custom-call(s32[3]{0:T(128)S(1)} %copy-done.5, s32[3]{0:T(128)S(1)} %copy-done.4, bf16[512,768]{1,0:T(8,128)(2,1)S(1)} %copy-done, bf16[3,192,768]{2,1,0:T(8,128)(2,1)S(1)} %bitcast.13), custom_call_target="tpu_custom_call" | custom-call | tf_op jit(solution)/shard_map/project/pallas_call | solution.py:180
  6.7 0.0 copy-start.1
  6.7 3.6 %near.1 = (bf16[512,256]{1,0:T(8,128)(2,1)S(1)}, f32[240,128]{1,0:T(8,128)S(1)}, f32[240,128]{1,0:T(8,128)S(1)}) custom-call(s32[3]{0:T(128)S(1)} %copy-done.5, s32[3]{0:T(128)S(1)} %copy-done.4, bf16[512,640]{1,0:T(8,128)(2,1)S(1)} %get-tuple-element.11.qkv_ref), custom_call_target="tpu_custom_call" | custom-call | tf_op jit(solution)/shard_map/near/pallas_call | solution.py:180
  10.3 0.7 %collective-permute-start.4 = (bf16[512,256]{1,0:T(8,128)(2,1)S(1)}, bf16[512,256]{1,0:T(8,128)(2,1)S(1)}, u32[]{:S(2)}, u32[]{:S(2)}) collective-permute-start(bf16[512,256]{1,0:T(8,128)(2,1)S(1)} %get-tuple-element.12.rest_0_), channel_id=1, source_target_pairs={{0,2},{1,3},{2,0},{3,1},{4,6},{5,7},{6,4},{7,5},{8,10},{9,11},{10,... | collective-permute-start | bytes 786440 | tf_op jit(solution)/shard_map/ppermute | solution.py:245
  11.0 3.6 %collective-permute-start.8 = (bf16[240,128]{1,0:T(8,128)(2,1)S(1)}, bf16[240,128]{1,0:T(8,128)(2,1)S(1)}, u32[]{:S(2)}, u32[]{:S(2)}) collective-permute-start(bf16[240,128]{1,0:T(8,128)(2,1)S(1)} %get-tuple-element.16), channel_id=1, source_target_pairs={{0,12},{4,0},{8,4},{12,8},{1,13},{5,1},{9,5},{13,9},{2,14},{6,2},{... | collective-permute-start | bytes 184328 | tf_op jit(solution)/shard_map/ppermute | solution.py:223
  14.6 0.0 collective-permute-start.7
  14.6 1.0 %collective-permute-start.6 = (bf16[240,128]{1,0:T(8,128)(2,1)S(1)}, bf16[240,128]{1,0:T(8,128)(2,1)S(1)}, u32[]{:S(2)}, u32[]{:S(2)}) collective-permute-start(bf16[240,128]{1,0:T(8,128)(2,1)S(1)} %get-tuple-element.16), channel_id=1, source_target_pairs={{0,4},{4,8},{8,12},{12,0},{1,5},{5,9},{9,13},{13,1},{2,6},{6,10},{... | collective-permute-start | bytes 184328 | tf_op jit(solution)/shard_map/ppermute | solution.py:223
  15.7 1.3 %collective-permute-done.8 = bf16[240,128]{1,0:T(8,128)(2,1)S(1)} collective-permute-done((bf16[240,128]{1,0:T(8,128)(2,1)S(1)}, bf16[240,128]{1,0:T(8,128)(2,1)S(1)}, u32[]{:S(2)}, u32[]{:S(2)}) %collective-permute-start.8) | collective-permute-done | bytes 61472 | tf_op jit(solution)/shard_map/ppermute | solution.py:223
  17.0 3.0 %collective-permute-done.7 = bf16[240,128]{1,0:T(8,128)(2,1)S(1)} collective-permute-done((bf16[240,128]{1,0:T(8,128)(2,1)S(1)}, bf16[240,128]{1,0:T(8,128)(2,1)S(1)}, u32[]{:S(2)}, u32[]{:S(2)}) %collective-permute-start.7) | collective-permute-done | bytes 61472 | tf_op jit(solution)/shard_map/ppermute | solution.py:223
  19.9 0.7 %collective-permute-done.6 = bf16[240,128]{1,0:T(8,128)(2,1)S(1)} collective-permute-done((bf16[240,128]{1,0:T(8,128)(2,1)S(1)}, bf16[240,128]{1,0:T(8,128)(2,1)S(1)}, u32[]{:S(2)}, u32[]{:S(2)}) %collective-permute-start.6) | collective-permute-done | bytes 61472 | tf_op jit(solution)/shard_map/ppermute | solution.py:223
  20.7 1.7 %merge.1.rest_4_ = bf16[80,256]{1,0:T(8,128)(2,1)S(1)} custom-call(s32[3]{0:T(128)S(1)} %copy-done.5, s32[3]{0:T(128)S(1)} %copy-done.4, bf16[240,128]{1,0:T(8,128)(2,1)S(1)} %get-tuple-element.13.qp_ref, f32[240,128]{1,0:T(8,128)S(1)} %get-tuple-element.14.am_ref, f32[240,128]{1,0:T(8,128)S(1)} %get-tuple-element.15.pk_ref, ...), custom_call_target="tpu_custom_call" | custom-call | tf_op jit(solution)/shard_map/merge/pallas_call | solution.py:180
  22.3 0.0 collective-permute-start.11
  22.4 0.0 copy-start.7
  22.4 0.1 pad_add_fusion.1
  22.5 1.7 %collective-permute-start.2 = (s32[6]{0:T(128)S(1)}, s32[6]{0:T(128)S(1)}, u32[]{:S(2)}, u32[]{:S(2)}) collective-permute-start(s32[6]{0:T(128)S(1)} %pad_add_fusion.1), channel_id=1, source_target_pairs={{0,3},{1,2},{2,1},{3,0},{4,7},{5,6},{6,5},{7,4},{8,11},{9,10},{10,... | collective-permute-start | bytes 80 | tf_op jit(solution)/shard_map/ppermute | solution.py:240
  24.2 1.4 %collective-permute-start.1 = (s32[6]{0:T(128)S(1)}, s32[6]{0:T(128)S(1)}, u32[]{:S(2)}, u32[]{:S(2)}) collective-permute-start(s32[6]{0:T(128)S(1)} %pad_add_fusion.1), channel_id=1, source_target_pairs={{0,2},{1,3},{2,0},{3,1},{4,6},{5,7},{6,4},{7,5},{8,10},{9,11},{10,... | collective-permute-start | bytes 80 | tf_op jit(solution)/shard_map/ppermute | solution.py:240
  25.6 0.7 %collective-permute-done.2 = s32[6]{0:T(128)S(1)} collective-permute-done((s32[6]{0:T(128)S(1)}, s32[6]{0:T(128)S(1)}, u32[]{:S(2)}, u32[]{:S(2)}) %collective-permute-start.2) | collective-permute-done | bytes 56 | tf_op jit(solution)/shard_map/ppermute | solution.py:240
  26.2 0.7 %collective-permute-start = (s32[6]{0:T(128)S(1)}, s32[6]{0:T(128)S(1)}, u32[]{:S(2)}, u32[]{:S(2)}) collective-permute-start(s32[6]{0:T(128)S(1)} %pad_add_fusion.1), channel_id=1, source_target_pairs={{0,1},{1,0},{2,3},{3,2},{4,5},{5,4},{6,7},{7,6},{8,9},{9,8},{10,11... | collective-permute-start | bytes 80 | tf_op jit(solution)/shard_map/ppermute | solution.py:240
  26.9 0.8 %collective-permute-done.1 = s32[6]{0:T(128)S(1)} collective-permute-done((s32[6]{0:T(128)S(1)}, s32[6]{0:T(128)S(1)}, u32[]{:S(2)}, u32[]{:S(2)}) %collective-permute-start.1) | collective-permute-done | bytes 56 | tf_op jit(solution)/shard_map/ppermute | solution.py:240
  27.7 0.0 collective-permute-start.12
  27.7 0.5 %collective-permute-start.3 = (bf16[512,256]{1,0:T(8,128)(2,1)S(1)}, bf16[512,256]{1,0:T(8,128)(2,1)S(1)}, u32[]{:S(2)}, u32[]{:S(2)}) collective-permute-start(bf16[512,256]{1,0:T(8,128)(2,1)S(1)} %get-tuple-element.12.rest_0_), channel_id=1, source_target_pairs={{0,1},{1,0},{2,3},{3,2},{4,5},{5,4},{6,7},{7,6},{8,9},{9,8},{10,11... | collective-permute-start | bytes 786440 | tf_op jit(solution)/shard_map/ppermute | solution.py:246
  28.2 1.4 %collective-permute-start.10 = (bf16[80,256]{1,0:T(8,128)(2,1)S(1)}, bf16[80,256]{1,0:T(8,128)(2,1)S(1)}, u32[]{:S(2)}, u32[]{:S(2)}) collective-permute-start(bf16[80,256]{1,0:T(8,128)(2,1)S(1)} %merge.1.rest_4_), channel_id=1, source_target_pairs={{0,2},{1,3},{2,0},{3,1},{4,6},{5,7},{6,4},{7,5},{8,10},{9,11},{10,... | collective-permute-start | bytes 122888 | tf_op jit(solution)/shard_map/ppermute | solution.py:240
  29.6 0.5 %collective-permute-start.14 = (bf16[192,768]{1,0:T(8,128)(2,1)S(1)}, bf16[192,768]{1,0:T(8,128)(2,1)S(1)}, u32[]{:S(2)}, u32[]{:S(2)}) collective-permute-start(bf16[192,768]{1,0:T(8,128)(2,1)S(1)} %collective-permute-done.13.rest_10_), channel_id=1, source_target_pairs={{0,1},{1,0},{2,3},{3,2},{4,5},{5,4},{6,7},{7,6},{8,9},{9,8},{10,11... | collective-permute-start | bytes 884744 | tf_op jit(solution)/shard_map/ppermute | solution.py:247
  30.1 2.1 %collective-permute-done.10.rest_6_ = bf16[80,256]{1,0:T(8,128)(2,1)S(1)} collective-permute-done((bf16[80,256]{1,0:T(8,128)(2,1)S(1)}, bf16[80,256]{1,0:T(8,128)(2,1)S(1)}, u32[]{:S(2)}, u32[]{:S(2)}) %collective-permute-start.10) | collective-permute-done | bytes 40992 | tf_op jit(solution)/shard_map/ppermute | solution.py:240
  32.3 0.1 fusion
  32.3 1.1 %collective-permute-done.9.rest_5_ = bf16[80,256]{1,0:T(8,128)(2,1)S(1)} collective-permute-done((bf16[80,256]{1,0:T(8,128)(2,1)S(1)}, bf16[80,256]{1,0:T(8,128)(2,1)S(1)}, u32[]{:S(2)}, u32[]{:S(2)}) %collective-permute-start.9) | collective-permute-done | bytes 40992 | tf_op jit(solution)/shard_map/ppermute | solution.py:240
  33.5 0.0 copy-start.6
  33.5 0.7 %copy-done.6 = f32[192]{0:T(256)S(1)} copy-done((f32[192]{0:T(256)S(1)}, f32[192]{0:T(256)}, u32[]{:S(2)}) %copy-start.6) | copy-done | bytes 792
  34.2 3.0 %output.1 = bf16[192,512]{1,0:T(8,128)(2,1)} custom-call(s32[1]{0:T(128)} %bitcast.place, s32[4,3]{1,0:T(4,128)S(1)} %get-tuple-element.18.mo, s32[4,3]{1,0:T(4,128)S(1)} %get-tuple-element.17.fo, bf16[512,768]{1,0:T(8,128)(2,1)S(1)} %copy-done.1, f32[1,192]{1,0:T(1,128)S(1)} %bitcast.16, f32[1,192]{1,0:T(1,128)S(1)} %bitcast.17, ...), custom_call_target="tpu_custom_call" | custom-call | tf_op jit(solution)/shard_map/output/pallas_call | solution.py:180
  (29 shorter events, 0.1 us)
Async XLA Ops:
  0.0 2.9 %copy-start.4 = (s32[3]{0:T(128)S(1)}, s32[3]{0:T(128)}, u32[]{:S(2)}) copy-start(s32[3]{0:T(128)} %fo.5) | copy-start | bytes 40
  0.0 2.9 %copy-start.5 = (s32[3]{0:T(128)S(1)}, s32[3]{0:T(128)}, u32[]{:S(2)}) copy-start(s32[3]{0:T(128)} %mo.5) | copy-start | bytes 40
  0.0 29.6 %collective-permute-start.13 = (bf16[192,768]{1,0:T(8,128)(2,1)}, bf16[192,768]{1,0:T(8,128)(2,1)S(1)}, u32[]{:S(2)}, u32[]{:S(2)}) collective-permute-start(bf16[192,768]{1,0:T(8,128)(2,1)} %rest_8_.1), channel_id=1, source_target_pairs={{0,2},{1,3},{2,0},{3,1},{4,6},{5,7},{6,4},{7,5},{8,10},{9,11},{10,... | collective-permute-start | bytes 884744 | tf_op jit(solution)/shard_map/ppermute | solution.py:245
  2.9 1.1 %copy-start = (bf16[512,768]{1,0:T(8,128)(2,1)S(1)}, bf16[512,768]{1,0:T(8,128)(2,1)}, u32[]{:S(2)}) copy-start(bf16[512,768]{1,0:T(8,128)(2,1)} %x_ref.3) | copy-start | bytes 2359300
  4.1 1.2 %copy-start.2 = (bf16[3,768,192]{1,2,0:T(8,128)(2,1)S(1)}, bf16[3,768,192]{1,2,0:T(8,128)(2,1)}, u32[]{:S(2)}) copy-start(bf16[3,768,192]{1,2,0:T(8,128)(2,1)} %param.8) | copy-start | bytes 2654212
  6.7 26.8 %copy-start.1 = (bf16[512,768]{1,0:T(8,128)(2,1)S(1)}, bf16[512,768]{1,0:T(8,128)(2,1)}, u32[]{:S(2)}) copy-start(bf16[512,768]{1,0:T(8,128)(2,1)} %x_ref.3) | copy-start | bytes 2359300
  10.3 19.3 %collective-permute-start.4 = (bf16[512,256]{1,0:T(8,128)(2,1)S(1)}, bf16[512,256]{1,0:T(8,128)(2,1)S(1)}, u32[]{:S(2)}, u32[]{:S(2)}) collective-permute-start(bf16[512,256]{1,0:T(8,128)(2,1)S(1)} %get-tuple-element.12.rest_0_), channel_id=1, source_target_pairs={{0,2},{1,3},{2,0},{3,1},{4,6},{5,7},{6,4},{7,5},{8,10},{9,11},{10,... | collective-permute-start | bytes 786440 | tf_op jit(solution)/shard_map/ppermute | solution.py:245
  11.0 5.9 %collective-permute-start.8 = (bf16[240,128]{1,0:T(8,128)(2,1)S(1)}, bf16[240,128]{1,0:T(8,128)(2,1)S(1)}, u32[]{:S(2)}, u32[]{:S(2)}) collective-permute-start(bf16[240,128]{1,0:T(8,128)(2,1)S(1)} %get-tuple-element.16), channel_id=1, source_target_pairs={{0,12},{4,0},{8,4},{12,8},{1,13},{5,1},{9,5},{13,9},{2,14},{6,2},{... | collective-permute-start | bytes 184328 | tf_op jit(solution)/shard_map/ppermute | solution.py:223
  14.6 5.3 %collective-permute-start.7 = (bf16[240,128]{1,0:T(8,128)(2,1)S(1)}, bf16[240,128]{1,0:T(8,128)(2,1)S(1)}, u32[]{:S(2)}, u32[]{:S(2)}) collective-permute-start(bf16[240,128]{1,0:T(8,128)(2,1)S(1)} %get-tuple-element.16), channel_id=1, source_target_pairs={{0,8},{4,12},{8,0},{12,4},{1,9},{5,13},{9,1},{13,5},{2,10},{6,14},... | collective-permute-start | bytes 184328 | tf_op jit(solution)/shard_map/ppermute | solution.py:223
  14.6 6.0 %collective-permute-start.6 = (bf16[240,128]{1,0:T(8,128)(2,1)S(1)}, bf16[240,128]{1,0:T(8,128)(2,1)S(1)}, u32[]{:S(2)}, u32[]{:S(2)}) collective-permute-start(bf16[240,128]{1,0:T(8,128)(2,1)S(1)} %get-tuple-element.16), channel_id=1, source_target_pairs={{0,4},{4,8},{8,12},{12,0},{1,5},{5,9},{9,13},{13,1},{2,6},{6,10},{... | collective-permute-start | bytes 184328 | tf_op jit(solution)/shard_map/ppermute | solution.py:223
  20.7 7.1 %copy-start.3 = (bf16[192,768]{1,0:T(8,128)(2,1)S(1)}, bf16[192,768]{1,0:T(8,128)(2,1)}, u32[]{:S(2)}) copy-start(bf16[192,768]{1,0:T(8,128)(2,1)} %rest_8_.1) | copy-start | bytes 884740
  22.3 5.9 %collective-permute-start.11 = (bf16[80,256]{1,0:T(8,128)(2,1)S(1)}, bf16[80,256]{1,0:T(8,128)(2,1)S(1)}, u32[]{:S(2)}, u32[]{:S(2)}) collective-permute-start(bf16[80,256]{1,0:T(8,128)(2,1)S(1)} %merge.1.rest_4_), channel_id=1, source_target_pairs={{0,3},{1,2},{2,1},{3,0},{4,7},{5,6},{6,5},{7,4},{8,11},{9,10},{10,... | collective-permute-start | bytes 122888 | tf_op jit(solution)/shard_map/ppermute | solution.py:240
  22.4 11.1 %copy-start.7 = (f32[192]{0:T(256)S(1)}, f32[192]{0:T(256)}, u32[]{:S(2)}) copy-start(f32[192]{0:T(256)} %param.11) | copy-start | bytes 2308
  22.5 3.8 %collective-permute-start.2 = (s32[6]{0:T(128)S(1)}, s32[6]{0:T(128)S(1)}, u32[]{:S(2)}, u32[]{:S(2)}) collective-permute-start(s32[6]{0:T(128)S(1)} %pad_add_fusion.1), channel_id=1, source_target_pairs={{0,3},{1,2},{2,1},{3,0},{4,7},{5,6},{6,5},{7,4},{8,11},{9,10},{10,... | collective-permute-start | bytes 80 | tf_op jit(solution)/shard_map/ppermute | solution.py:240
  24.2 3.5 %collective-permute-start.1 = (s32[6]{0:T(128)S(1)}, s32[6]{0:T(128)S(1)}, u32[]{:S(2)}, u32[]{:S(2)}) collective-permute-start(s32[6]{0:T(128)S(1)} %pad_add_fusion.1), channel_id=1, source_target_pairs={{0,2},{1,3},{2,0},{3,1},{4,6},{5,7},{6,4},{7,5},{8,10},{9,11},{10,... | collective-permute-start | bytes 80 | tf_op jit(solution)/shard_map/ppermute | solution.py:240
  26.2 1.5 %collective-permute-start = (s32[6]{0:T(128)S(1)}, s32[6]{0:T(128)S(1)}, u32[]{:S(2)}, u32[]{:S(2)}) collective-permute-start(s32[6]{0:T(128)S(1)} %pad_add_fusion.1), channel_id=1, source_target_pairs={{0,1},{1,0},{2,3},{3,2},{4,5},{5,4},{6,7},{7,6},{8,9},{9,8},{10,11... | collective-permute-start | bytes 80 | tf_op jit(solution)/shard_map/ppermute | solution.py:240
  27.7 5.7 %collective-permute-start.12 = (bf16[192,768]{1,0:T(8,128)(2,1)S(1)}, bf16[192,768]{1,0:T(8,128)(2,1)S(1)}, u32[]{:S(2)}, u32[]{:S(2)}) collective-permute-start(bf16[192,768]{1,0:T(8,128)(2,1)S(1)} %copy-done.3), channel_id=1, source_target_pairs={{0,1},{1,0},{2,3},{3,2},{4,5},{5,4},{6,7},{7,6},{8,9},{9,8},{10,11... | collective-permute-start | bytes 884744 | tf_op jit(solution)/shard_map/ppermute | solution.py:246
  27.7 5.7 %collective-permute-start.3 = (bf16[512,256]{1,0:T(8,128)(2,1)S(1)}, bf16[512,256]{1,0:T(8,128)(2,1)S(1)}, u32[]{:S(2)}, u32[]{:S(2)}) collective-permute-start(bf16[512,256]{1,0:T(8,128)(2,1)S(1)} %get-tuple-element.12.rest_0_), channel_id=1, source_target_pairs={{0,1},{1,0},{2,3},{3,2},{4,5},{5,4},{6,7},{7,6},{8,9},{9,8},{10,11... | collective-permute-start | bytes 786440 | tf_op jit(solution)/shard_map/ppermute | solution.py:246
  28.2 4.0 %collective-permute-start.10 = (bf16[80,256]{1,0:T(8,128)(2,1)S(1)}, bf16[80,256]{1,0:T(8,128)(2,1)S(1)}, u32[]{:S(2)}, u32[]{:S(2)}) collective-permute-start(bf16[80,256]{1,0:T(8,128)(2,1)S(1)} %merge.1.rest_4_), channel_id=1, source_target_pairs={{0,2},{1,3},{2,0},{3,1},{4,6},{5,7},{6,4},{7,5},{8,10},{9,11},{10,... | collective-permute-start | bytes 122888 | tf_op jit(solution)/shard_map/ppermute | solution.py:240
  29.6 3.9 %collective-permute-start.5 = (bf16[512,256]{1,0:T(8,128)(2,1)S(1)}, bf16[512,256]{1,0:T(8,128)(2,1)S(1)}, u32[]{:S(2)}, u32[]{:S(2)}) collective-permute-start(bf16[512,256]{1,0:T(8,128)(2,1)S(1)} %collective-permute-done.4.rest_2_), channel_id=1, source_target_pairs={{0,1},{1,0},{2,3},{3,2},{4,5},{5,4},{6,7},{7,6},{8,9},{9,8},{10,11... | collective-permute-start | bytes 786440 | tf_op jit(solution)/shard_map/ppermute | solution.py:247
  29.6 3.9 %collective-permute-start.14 = (bf16[192,768]{1,0:T(8,128)(2,1)S(1)}, bf16[192,768]{1,0:T(8,128)(2,1)S(1)}, u32[]{:S(2)}, u32[]{:S(2)}) collective-permute-start(bf16[192,768]{1,0:T(8,128)(2,1)S(1)} %collective-permute-done.13.rest_10_), channel_id=1, source_target_pairs={{0,1},{1,0},{2,3},{3,2},{4,5},{5,4},{6,7},{7,6},{8,9},{9,8},{10,11... | collective-permute-start | bytes 884744 | tf_op jit(solution)/shard_map/ppermute | solution.py:247
  32.2 1.2 %collective-permute-start.9 = (bf16[80,256]{1,0:T(8,128)(2,1)S(1)}, bf16[80,256]{1,0:T(8,128)(2,1)S(1)}, u32[]{:S(2)}, u32[]{:S(2)}) collective-permute-start(bf16[80,256]{1,0:T(8,128)(2,1)S(1)} %merge.1.rest_4_), channel_id=1, source_target_pairs={{0,1},{1,0},{2,3},{3,2},{4,5},{5,4},{6,7},{7,6},{8,9},{9,8},{10,11... | collective-permute-start | bytes 122888 | tf_op jit(solution)/shard_map/ppermute | solution.py:240
  33.5 0.7 %copy-start.6 = (f32[192]{0:T(256)S(1)}, f32[192]{0:T(256)}, u32[]{:S(2)}) copy-start(f32[192]{0:T(256)} %param.10) | copy-start | bytes 2308

commit v2 on v1

v2 whole, which is shorter than its diff:
```python
from functools import partial
import math

import jax
import jax.numpy as jnp
from jax import lax
from jax.experimental import pallas as pl
from jax.experimental.pallas import tpu as pltpu
from jax.sharding import PartitionSpec as P

HEADS = 12
SEG0 = 128
R1 = 8
R2 = 32
LANES = 128
HALF = 64

epsilon = 1e-05
f32 = jnp.float32
bf16 = jnp.bfloat16

NT = (((1,), (1,)), ((), ()))


def lane_half(shape):
    return lax.broadcasted_iota(jnp.int32, shape, 1) < HALF


def acc_low(head):
    return head % 2 == 0


def project_kernel(mo, fo, x_hbm, w_hbm, qkv_ref, kvp_ref, qp_ref, x_ref, w_ref, scr, x_sem, w_sem):
    rows = x_ref.shape[0]
    mid, far = rows // R1, rows // R2
    per = mid + far
    pieces, piece = x_sem.shape[0], rows // x_sem.shape[0]
    w_pieces, w_piece = w_sem.shape[1], w_ref.shape[1] // w_sem.shape[1]

    def w_copy(i, j):
        at = pl.ds(j * w_piece, w_piece)
        return pltpu.make_async_copy(w_hbm.at[i, at], w_ref.at[i, at], w_sem.at[i, j])

    def x_copy(i):
        at = pl.ds(i * piece, piece)
        return pltpu.make_async_copy(x_hbm.at[at], x_ref.at[at], x_sem.at[i])

    copies = [w_copy(i, j) for i in range(3) for j in range(w_pieces)]
    copies += [x_copy(i) for i in range(pieces)]
    for copy in copies:
        copy.start()
    for copy in copies:
        copy.wait()
    q = [w_ref[0, h * HALF : (h + 1) * HALF] for h in range(3)]
    k = [w_ref[1, h * HALF : (h + 1) * HALF] for h in range(3)]
    v = [w_ref[2, h * HALF : (h + 1) * HALF] for h in range(3)]
    w = jnp.concatenate([v[0], k[0], k[1], v[1], v[2], k[2], q[1], q[0], q[2], q[2]], axis=0)
    step = rows // 2
    for first in range(0, rows, step):
        at = slice(first, first + step)
        y = lax.dot_general(x_ref[at], w, NT, preferred_element_type=f32).astype(bf16)
        qkv_ref[at] = y
        for i in range(5):
            scr[i, at] = y[:, i * LANES : (i + 1) * LANES].astype(f32)
    for h in range(3):
        asked = 3 + h // 2
        low = lane_half((mid, LANES))
        keep = jnp.logical_not(low) if acc_low(h) else low
        mid_rows = pl.ds(mo[h], mid, stride=R1)
        far_rows = pl.ds(fo[h], far, stride=R2)
        kvp_ref[h * per : h * per + mid] = scr[h, mid_rows].astype(bf16)
        kvp_ref[h * per + mid : (h + 1) * per] = scr[h, far_rows].astype(bf16)
        qp_ref[h * per : h * per + mid] = jnp.where(keep, scr[asked, mid_rows], 0.0).astype(bf16)
        qp_ref[h * per + mid : (h + 1) * per] = jnp.where(
            keep[:far], scr[asked, far_rows], 0.0
        ).astype(bf16)


def scores(queries, keys_values):
    return lax.dot_general(queries, keys_values, NT, preferred_element_type=f32)


def soften(s, factor):
    peak = jnp.max(s, axis=1, keepdims=True)
    return peak, jnp.exp2((s - peak) * factor).astype(bf16)


def weigh(p, keys_values, head):
    low = lane_half(keys_values.shape)
    is_value = low if acc_low(head) else jnp.logical_not(low)
    values = jnp.where(is_value, keys_values, jnp.ones((), bf16))
    return jnp.dot(p, values, preferred_element_type=f32)


def swap(x):
    return pltpu.roll(x, HALF, 1)


def pair(a, b):
    low = lane_half(a.shape)
    return (jnp.where(low, a, b) / swap(jnp.where(low, b, a))).astype(bf16)


def fold(x):
    half = x.shape[0] // 2
    a, b = x[:half], x[half:]
    low = lane_half(a.shape)
    return (jnp.where(low, a, swap(b)) / jnp.where(low, swap(a), b)).astype(bf16)


def near_kernel(factor, mo, fo, qkv_ref, near_ref, am_ref, pk_ref, am_scr, pk_scr):
    rows = qkv_ref.shape[0]
    mid, far = rows // R1, rows // R2
    per = mid + far
    low = lane_half((SEG0, LANES))
    blocks = rows // SEG0
    units = [(b, h) for b in range(blocks) for h in range(3)]

    def rows_of(b):
        return slice(b * SEG0, (b + 1) * SEG0)

    def kv(b, h):
        return qkv_ref[rows_of(b), h * LANES : (h + 1) * LANES]

    def ask(b, h):
        keep = jnp.logical_not(low) if acc_low(h) else low
        first = (3 + h // 2) * LANES
        q = qkv_ref[rows_of(b), first : first + LANES]
        return scores(jnp.where(keep, q, jnp.zeros((), bf16)), kv(b, h))

    s = {u: ask(*u) for u in units[:3]}
    am = {}
    for i, u in enumerate(units):
        if i + 3 < len(units):
            s[units[i + 3]] = ask(*units[i + 3])
        b, h = u
        peak, p = soften(s.pop(u), factor)
        am[u] = weigh(p, kv(b, h), h)
        am_scr[h, rows_of(b)] = am[u]
        pk_scr[h, rows_of(b)] = jnp.broadcast_to(peak, am[u].shape)
        if h == 2:
            near_ref[rows_of(b)] = pair(am.pop((b, 0)), am.pop((b, 1)))
    near_ref[rows : rows + rows // 2] = fold(am_scr[2])
    lane = lax.broadcasted_iota(jnp.int32, (16, LANES), 1)
    told = jnp.zeros((16, LANES), jnp.int32)
    for h in range(3):
        told = jnp.where(lane == h, mo[h], jnp.where(lane == 3 + h, fo[h], told))
    near_ref[rows + rows // 2 :] = told.astype(f32).astype(bf16)
    for h in range(3):
        own, own_far = slice(h * per, h * per + mid), slice(h * per + mid, (h + 1) * per)
        mid_rows = pl.ds(mo[h], mid, stride=R1)
        far_rows = pl.ds(fo[h], far, stride=R2)
        am_ref[own], am_ref[own_far] = am_scr[h, mid_rows], am_scr[h, far_rows]
        pk_ref[own], pk_ref[own_far] = pk_scr[h, mid_rows], pk_scr[h, far_rows]


def merge_kernel(factor, mid_n, far_n, mo, fo, qp_ref, am_ref, pk_ref, *rest):
    mids, fars = rest[:mid_n], rest[mid_n : mid_n + far_n]
    corr_ref, am_scr, pk_scr = rest[mid_n + far_n :]
    per = qp_ref.shape[0] // 3
    far = per * R1 // (R1 + R2)
    mid = per - far
    heads = range(3)
    own = [slice(h * per, h * per + mid) for h in heads]
    own_far = [slice(h * per + mid, (h + 1) * per) for h in heads]

    def joined(refs, h, whole, at):
        return jnp.concatenate([m[at[h]] if m.shape[0] == 3 * per else m[h] for m in refs], axis=0)

    kv_mid = [joined(mids, h, per, own) for h in heads]
    kv_far = [joined(fars, h, per, own_far) for h in heads]
    s_mid = [scores(qp_ref[own[h]], kv_mid[h]) for h in heads]
    s_far = [scores(qp_ref[own_far[h]], kv_far[h]) for h in heads]
    soft_mid = [soften(s, factor) for s in s_mid]
    soft_far = [soften(s, factor) for s in s_far]
    am_mid = [weigh(soft_mid[h][1], kv_mid[h], h) for h in heads]
    am_far = [weigh(soft_far[h][1], kv_far[h], h) for h in heads]
    out_mid, out_far = [], []
    for h in heads:
        peak_mid = jnp.broadcast_to(soft_mid[h][0], am_mid[h].shape)
        am_scr[h] = am_mid[h]
        pk_scr[h] = peak_mid
        near_peak, near_am = pk_ref[own[h]], am_ref[own[h]]
        top = jnp.maximum(near_peak, peak_mid)
        out_mid.append(
            jnp.exp2((near_peak - top) * factor) * near_am
            + jnp.exp2((peak_mid - top) * factor) * am_mid[h]
        )
    for h in heads:
        shared = pl.ds(fo[h] // R1, far, stride=R2 // R1)
        also = fo[h] % R1 == mo[h]
        both_peak = jnp.where(also, pk_scr[h, shared], -1e30)
        both_am = am_scr[h, shared]
        near_peak, near_am = pk_ref[own_far[h]], am_ref[own_far[h]]
        top = jnp.maximum(jnp.maximum(near_peak, both_peak), soft_far[h][0])
        out_far.append(
            jnp.exp2((near_peak - top) * factor) * near_am
            + jnp.exp2((both_peak - top) * factor) * both_am
            + jnp.exp2((soft_far[h][0] - top) * factor) * am_far[h]
        )
    corr_ref[:mid] = pair(out_mid[0], out_mid[1])
    corr_ref[mid:per] = pair(out_far[0], out_far[1])
    corr_ref[per : per + mid // 2] = fold(out_mid[2])
    corr_ref[per + mid // 2 :] = fold(out_far[2])


def output_kernel(head_count, place, mo, fo, x_ref, gain_ref, bias_ref, *rest):
    near, corr, weights = (rest[i * head_count : (i + 1) * head_count] for i in range(3))
    out_ref, attn_scr, resid_scr = rest[3 * head_count :]
    rows, width = x_ref.shape
    mid, far = rows // R1, rows // R2
    half = rows // 2
    per = mid + far
    cols = width // head_count
    for r in range(head_count):
        attn_scr[r] = near[r][:rows].astype(f32)
    low = lane_half((half, LANES))
    for r in range(0, head_count, 2):
        even = near[r][rows : rows + half].astype(f32)
        odd = near[r + 1][rows : rows + half].astype(f32)
        attn_scr[head_count + r // 2, :half] = jnp.where(low, even, swap(odd))
        attn_scr[head_count + r // 2, half:] = jnp.where(low, swap(even), odd)

    def patch(tile, to_low, first, count, stride, value):
        at = pl.ds(first, count, stride=stride)
        low = lane_half(value.shape)
        keep = low if to_low else jnp.logical_not(low)
        attn_scr[tile, at] = jnp.where(keep, value, attn_scr[tile, at])

    for offset, stride, count, first, folded in (
        (mo, R1, mid, 0, per),
        (fo, R2, far, mid, per + mid // 2),
    ):
        for r in range(head_count):
            both = corr[r][first : first + count].astype(f32)
            patch(r, True, offset[r, 0], count, stride, both)
            patch(r, False, offset[r, 1], count, stride, both)
            third = corr[r][folded : folded + count // 2].astype(f32)
            turned = swap(third)
            tile, to_low = head_count + r // 2, r % 2 == 0
            upper, lower = (third, turned) if to_low else (turned, third)
            patch(tile, to_low, offset[r, 2], count // 2, stride, upper)
            patch(tile, to_low, offset[r, 2] + half, count // 2, stride, lower)

    w = jnp.concatenate(
        [weights[r][:LANES] for r in range(head_count)]
        + [weights[r][LANES:] for r in range(head_count)],
        axis=0,
    )
    for first in (0, half):
        at = slice(first, first + half)
        attn = jnp.concatenate(
            [attn_scr[t, at].astype(bf16) for t in range(attn_scr.shape[0])], axis=1
        )
        resid = x_ref[at].astype(f32) + jnp.dot(attn, w, preferred_element_type=f32)
        mean = jnp.sum(resid, axis=1, keepdims=True) / width
        var = jnp.sum(resid * resid, axis=1, keepdims=True) / width - mean * mean
        resid_scr[at] = (resid - mean) * lax.rsqrt(var + epsilon)
    for i in range(head_count):

        @pl.when(place[0] == i)
        def _():
            mine = resid_scr[:, i * cols : (i + 1) * cols]
            out_ref[...] = (mine * gain_ref[...] + bias_ref[...]).T.astype(bf16)


IN_VMEM = pl.BlockSpec(memory_space=pltpu.VMEM)
IN_SMEM = pl.BlockSpec(memory_space=pltpu.SMEM)
IN_HBM = pl.BlockSpec(memory_space=pltpu.HBM)


def call(kernel, outs, scratch, scalars, arrays, name, cost, held=IN_VMEM):
    return pl.pallas_call(
        kernel,
        out_shape=outs,
        in_specs=[IN_SMEM] * len(scalars) + [held] * len(arrays),
        out_specs=jax.tree.map(lambda _: IN_VMEM, outs),
        scratch_shapes=scratch,
        compiler_params=pltpu.CompilerParams(vmem_limit_bytes=32 << 20),
        name=name,
        cost_estimate=pl.CostEstimate(flops=cost, transcendentals=0, bytes_accessed=4 << 20),
    )(*scalars, *arrays)


def local(tokens, w_qkv, w_out, gain, bias, mid_offset, far_offset):
    rows, width = tokens.shape
    heads_here = mid_offset.shape[0]
    head_size = width // HEADS
    cols = heads_here * head_size
    factor = math.log2(math.e) / math.sqrt(head_size)
    mid, far = rows // R1, rows // R2
    per = mid + far
    shape = jax.ShapeDtypeStruct
    after = lax.optimization_barrier

    head_count = lax.axis_size("head")
    if head_count & (head_count - 1) == 0:
        paths = [[(i, i ^ r) for i in range(head_count)] for r in range(head_count)]
    else:
        paths = [[(i, (i + r) % head_count) for i in range(head_count)] for r in range(head_count)]

    def to(array, r):
        return lax.ppermute(array, "head", paths[r])

    def spread(array):
        return [array] + [to(array, r) for r in range(1, head_count)]

    two_step = head_count == 4

    qkv, kvp, qp = call(
        project_kernel,
        (
            shape((rows, 5 * LANES), bf16),
            shape((3 * per, LANES), bf16),
            shape((3 * per, LANES), bf16),
        ),
        [
            pltpu.VMEM((rows, width), bf16),
            pltpu.VMEM((3, cols, width), bf16),
            pltpu.VMEM((5, rows, LANES), f32),
            pltpu.SemaphoreType.DMA((4,)),
            pltpu.SemaphoreType.DMA((3, 2)),
        ],
        (mid_offset, far_offset),
        (tokens, jnp.swapaxes(w_qkv, 1, 2)),
        "project",
        2 * rows * width * 3 * cols,
        IN_HBM,
    )

    seq_count = lax.axis_size("seq")
    mid_devs = min(8, seq_count)

    def within(step):
        return [
            (i, i // mid_devs * mid_devs + (i + step) % mid_devs) for i in range(seq_count)
        ]

    if mid_devs == seq_count:
        mids = [kvp] + [lax.ppermute(kvp, "seq", within(s)) for s in range(1, mid_devs)]
        fars = None
    else:
        split = kvp.reshape(3, per, LANES)
        piece = split[:, :mid]
        mids = [piece] + [lax.ppermute(piece, "seq", within(s)) for s in range(1, mid_devs)]
        fars = [lax.all_gather(split[:, mid:], "seq", axis=1, tiled=True)]

    if two_step:
        across = to(w_out, 2)
        beside = to(after((w_out, kvp))[0], 1)
        qkv, beside = after((qkv, beside))
    else:
        weights = spread(w_out)

    near, am, pk = call(
        partial(near_kernel, factor),
        (
            shape((rows + rows // 2 + 16, LANES), bf16),
            shape((3 * per, LANES), f32),
            shape((3 * per, LANES), f32),
        ),
        [pltpu.VMEM((3, rows, LANES), f32)] * 2,
        (mid_offset, far_offset),
        (qkv,),
        "near",
        1 << 28,
    )
    if two_step:
        last = to(after((across, beside))[0], 1)
        weights = [w_out, beside, across, last]
        near_across = to(after((near, across))[0], 2)
        near_beside = to(after((near, last))[0], 1)
        near_last = to(after((near_across, near_beside))[0], 1)
        nears = [near, near_beside, near_across, near_last]
    else:
        nears = spread(near)

    corr = call(
        partial(merge_kernel, factor, len(mids), len(fars or mids)),
        shape((per + per // 2, LANES), bf16),
        [pltpu.VMEM((3, mid, LANES), f32)] * 2,
        (mid_offset, far_offset),
        (qp, am, pk, *mids, *(fars or mids)),
        "merge",
        1 << 27,
    )
    corrs = spread(corr)
    told = [n[rows + rows // 2, : 2 * heads_here].astype(jnp.int32) for n in nears]
    told = jnp.stack(told)

    out = call(
        partial(output_kernel, head_count),
        shape((cols, rows), bf16),
        [
            pltpu.VMEM((head_count + head_count // 2, rows, LANES), f32),
            pltpu.VMEM((rows, width), f32),
        ],
        (lax.axis_index("head").reshape(1), told[:, :heads_here], told[:, heads_here:]),
        (tokens, gain.reshape(1, cols), bias.reshape(1, cols), *nears, *corrs, *weights),
        "output",
        2 * rows * width * width,
    )
    return out.T


def solution(mesh):
    in_specs = (
        P(("group", "seq"), None),
        P(None, None, "head"),
        P("head", None),
        P("head"),
        P("head"),
        P("head"),
        P("head"),
    )
    out_specs = P(("group", "seq"), "head")
    return jax.shard_map(local, mesh=mesh, in_specs=in_specs, out_specs=out_specs, check_vma=False)
```

time: 37.3 us -> 46.8 us (1.25)
  waiting for transfers between devices: 9.74 us -> 21.7 us
  starting transfers between devices: 14.5 us -> 11.9 us
  local copies, waits for them, and re-layouts: 3.08 us -> 3.72 us
  Pallas kernels: 9.67 us -> 9.19 us
    ppermute x12 -> x9, waiting for transfers between devices: 4.76 us -> 15.9 us  [to(): return lax.ppermute(array, 'head', paths[r])]
    ppermute x12 -> x9, starting transfers between devices: 9.85 us -> 7.06 us  [to(): return lax.ppermute(array, 'head', paths[r])]
    ppermute x3, waiting for transfers between devices: 4.99 us -> 5.78 us  [local(): lax.ppermute(kvp, 'seq', within(s))]
    unnamed x16, local copies, waits for them, and re-layouts: 2.98 us -> 3.64 us
    pallas_call x4, Pallas kernels: 9.67 us -> 9.19 us  [call(): pl.pallas_call(kernel, out_shape=outs, in_specs=[IN_SMEM] * len(scalars)...]
  transfers between devices with their start and end apart: 15 -> 12, of which waited for: 7 -> 6; matrix products, arithmetic and copies ran while one was open for 0% -> 0% of each run, Pallas kernels for 18% -> 6%
where the time goes in v2:
time: 46.8 us; the launch traced here: 46.6 us
  waiting for transfers between devices  21.7 us (46%)
  starting transfers between devices  11.9 us (25%)
  Pallas kernels  9.19 us (20%)
  local copies, waits for them, and re-layouts  3.72 us (8%)
    ppermute x9, waiting for transfers between devices, to(): return lax.ppermute(array, 'head', paths[r])  15.9 us
    pallas_call x4, Pallas kernels, call(): pl.pallas_call(kernel, out_shape=outs, in_specs=[IN_SMEM] * len(scalars)...  9.19 us
    ppermute x9, starting transfers between devices, to(): return lax.ppermute(array, 'head', paths[r])  7.06 us
    ppermute x3, waiting for transfers between devices, local(): lax.ppermute(kvp, 'seq', within(s))  5.78 us
    ppermute x3, starting transfers between devices, local(): lax.ppermute(kvp, 'seq', within(s))  4.87 us
    unnamed x16, local copies, waits for them, and re-layouts  3.64 us
  transfers between devices with their start and end apart: 12, of which 6 were waited for; matrix products, arithmetic and copies ran while one was open for 0% of the time, Pallas kernels for 6%

profile of v2, /device:TPU:0, one launch (start us, length us, event | category | flops | bytes accessed | tf_op | source)
XLA Modules:
  0.0 46.6 jit_solution(9481977728751535272)
XLA Ops:
  0.0 0.7 %copy-done.6 = s32[3]{0:T(128)S(1)} copy-done((s32[3]{0:T(128)S(1)}, s32[3]{0:T(128)}, u32[]{:S(2)}) %copy-start.6) | copy-done | bytes 36
  0.7 0.0 copy-done.5
  0.7 1.1 %copy-done = bf16[512,768]{1,0:T(8,128)(2,1)S(1)} copy-done((bf16[512,768]{1,0:T(8,128)(2,1)S(1)}, bf16[512,768]{1,0:T(8,128)(2,1)}, u32[]{:S(2)}) %copy-start) | copy-done | bytes 786456
  1.8 1.2 %copy-done.7 = bf16[3,768,192]{1,2,0:T(8,128)(2,1)S(1)} copy-done((bf16[3,768,192]{1,2,0:T(8,128)(2,1)S(1)}, bf16[3,768,192]{1,2,0:T(8,128)(2,1)}, u32[]{:S(2)}) %copy-start.7) | copy-done | bytes 884760
  3.0 3.7 %project.1 = (bf16[512,640]{1,0:T(8,128)(2,1)S(1)}, bf16[240,128]{1,0:T(8,128)(2,1)S(1)}, bf16[240,128]{1,0:T(8,128)(2,1)S(1)}) custom-call(s32[3]{0:T(128)S(1)} %copy-done.5, s32[3]{0:T(128)S(1)} %copy-done.6, bf16[512,768]{1,0:T(8,128)(2,1)S(1)} %copy-done, bf16[3,192,768]{2,1,0:T(8,128)(2,1)S(1)} %bitcast.7), custom_call_target="tpu_custom_call" | custom-call | flops 452984832 | bytes 4194304 | tf_op jit(solution)/shard_map/project/pallas_call | solution.py:273
  6.7 0.5 %collective-permute-start = (bf16[192,768]{1,0:T(8,128)(2,1)S(1)}, bf16[192,768]{1,0:T(8,128)(2,1)S(1)}, u32[]{:S(2)}, u32[]{:S(2)}) collective-permute-start(bf16[192,768]{1,0:T(8,128)(2,1)S(1)} %copy-done.2), channel_id=1, source_target_pairs={{0,1},{1,0},{2,3},{3,2},{4,5},{5,4},{6,7},{7,6},{8,9},{9,8},{10,11... | collective-permute-start | bytes 884744 | tf_op jit(solution)/shard_map/ppermute | solution.py:303
  7.2 2.6 %collective-permute-start.1 = (bf16[192,768]{1,0:T(8,128)(2,1)S(1)}, bf16[192,768]{1,0:T(8,128)(2,1)S(1)}, u32[]{:S(2)}, u32[]{:S(2)}) collective-permute-start(bf16[192,768]{1,0:T(8,128)(2,1)S(1)} %copy-done.2), channel_id=1, source_target_pairs={{0,2},{1,3},{2,0},{3,1},{4,6},{5,7},{6,4},{7,5},{8,10},{9,11},{10,... | collective-permute-start | bytes 884744 | tf_op jit(solution)/shard_map/ppermute | solution.py:303
  9.8 0.0 collective-permute-done.rest_9_
  9.8 7.6 %collective-permute-done.1.rest_10_ = bf16[192,768]{1,0:T(8,128)(2,1)S(1)} collective-permute-done((bf16[192,768]{1,0:T(8,128)(2,1)S(1)}, bf16[192,768]{1,0:T(8,128)(2,1)S(1)}, u32[]{:S(2)}, u32[]{:S(2)}) %collective-permute-start.1) | collective-permute-done | bytes 294944 | tf_op jit(solution)/shard_map/ppermute | solution.py:303
  17.4 0.0 collective-permute-start.2
  17.4 1.6 %near.1 = (bf16[784,128]{1,0:T(8,128)(2,1)S(1)}, f32[240,128]{1,0:T(8,128)S(1)}, f32[240,128]{1,0:T(8,128)S(1)}) custom-call(s32[3]{0:T(128)S(1)} %copy-done.5, s32[3]{0:T(128)S(1)} %copy-done.6, bf16[512,640]{1,0:T(8,128)(2,1)S(1)} %get-tuple-element.21.qkv_ref), custom_call_target="tpu_custom_call" | custom-call | flops 268435456 | bytes 4194304 | tf_op jit(solution)/shard_map/near/pallas_call | solution.py:273
  19.0 1.8 %collective-permute-start.4 = (bf16[784,128]{1,0:T(8,128)(2,1)S(1)}, bf16[784,128]{1,0:T(8,128)(2,1)S(1)}, u32[]{:S(2)}, u32[]{:S(2)}) collective-permute-start(bf16[784,128]{1,0:T(8,128)(2,1)S(1)} %get-tuple-element.25.rest_0_), channel_id=1, source_target_pairs={{0,2},{1,3},{2,0},{3,1},{4,6},{5,7},{6,4},{7,5},{8,10},{9,11},{10,... | collective-permute-start | bytes 602120 | tf_op jit(solution)/shard_map/ppermute | solution.py:303
  20.8 0.0 collective-permute-done.2.rest_11_
  20.8 0.2 collective-permute-start.3
  21.0 5.4 %collective-permute-done.4.rest_2_ = bf16[784,128]{1,0:T(8,128)(2,1)S(1)} collective-permute-done((bf16[784,128]{1,0:T(8,128)(2,1)S(1)}, bf16[784,128]{1,0:T(8,128)(2,1)S(1)}, u32[]{:S(2)}, u32[]{:S(2)}) %collective-permute-start.4) | collective-permute-done | bytes 200736 | tf_op jit(solution)/shard_map/ppermute | solution.py:303
  26.5 0.0 collective-permute-done.3.rest_1_
  26.5 0.0 collective-permute-start.5
  26.5 3.9 %collective-permute-start.8 = (bf16[240,128]{1,0:T(8,128)(2,1)S(1)}, bf16[240,128]{1,0:T(8,128)(2,1)S(1)}, u32[]{:S(2)}, u32[]{:S(2)}) collective-permute-start(bf16[240,128]{1,0:T(8,128)(2,1)S(1)} %get-tuple-element.19.rest_0_.rest_4_), channel_id=1, source_target_pairs={{0,12},{4,0},{8,4},{12,8},{1,13},{5,1},{9,5},{13,9},{2,14},{6,2},{... | collective-permute-start | bytes 184328 | tf_op jit(solution)/shard_map/ppermute | solution.py:340
  30.3 0.0 collective-permute-start.7
  30.3 1.0 %collective-permute-start.6 = (bf16[240,128]{1,0:T(8,128)(2,1)S(1)}, bf16[240,128]{1,0:T(8,128)(2,1)S(1)}, u32[]{:S(2)}, u32[]{:S(2)}) collective-permute-start(bf16[240,128]{1,0:T(8,128)(2,1)S(1)} %get-tuple-element.19.rest_0_.rest_4_), channel_id=1, source_target_pairs={{0,4},{4,8},{8,12},{12,0},{1,5},{5,9},{9,13},{13,1},{2,6},{6,10},{... | collective-permute-start | bytes 184328 | tf_op jit(solution)/shard_map/ppermute | solution.py:340
  31.4 1.3 %collective-permute-done.8.rest_3_.rest_7_ = bf16[240,128]{1,0:T(8,128)(2,1)S(1)} collective-permute-done((bf16[240,128]{1,0:T(8,128)(2,1)S(1)}, bf16[240,128]{1,0:T(8,128)(2,1)S(1)}, u32[]{:S(2)}, u32[]{:S(2)}) %collective-permute-start.8) | collective-permute-done | bytes 61472 | tf_op jit(solution)/shard_map/ppermute | solution.py:340
  32.7 4.4 %collective-permute-done.7.rest_2_.rest_6_ = bf16[240,128]{1,0:T(8,128)(2,1)S(1)} collective-permute-done((bf16[240,128]{1,0:T(8,128)(2,1)S(1)}, bf16[240,128]{1,0:T(8,128)(2,1)S(1)}, u32[]{:S(2)}, u32[]{:S(2)}) %collective-permute-start.7) | collective-permute-done | bytes 61472 | tf_op jit(solution)/shard_map/ppermute | solution.py:340
  37.1 0.0 collective-permute-done.6.rest_1_.rest_5_
  37.1 1.1 %merge.1.rest_4_ = bf16[120,128]{1,0:T(8,128)(2,1)S(1)} custom-call(s32[3]{0:T(128)S(1)} %copy-done.5, s32[3]{0:T(128)S(1)} %copy-done.6, bf16[240,128]{1,0:T(8,128)(2,1)S(1)} %get-tuple-element.28.qp_ref, f32[240,128]{1,0:T(8,128)S(1)} %get-tuple-element.29.am_ref, f32[240,128]{1,0:T(8,128)S(1)} %get-tuple-element.30.pk_ref, ...), custom_call_target="tpu_custom_call" | custom-call | flops 134217728 | bytes 4194304 | tf_op jit(solution)/shard_map/merge/pallas_call | solution.py:273
  38.2 1.0 %collective-permute-start.11 = (bf16[120,128]{1,0:T(8,128)(2,1)S(1)}, bf16[120,128]{1,0:T(8,128)(2,1)S(1)}, u32[]{:S(2)}, u32[]{:S(2)}) collective-permute-start(bf16[120,128]{1,0:T(8,128)(2,1)S(1)} %merge.1.rest_4_), channel_id=1, source_target_pairs={{0,3},{1,2},{2,1},{3,0},{4,7},{5,6},{6,5},{7,4},{8,11},{9,10},{10,... | collective-permute-start | bytes 92168 | tf_op jit(solution)/shard_map/ppermute | solution.py:303
  39.2 0.7 %collective-permute-start.10 = (bf16[120,128]{1,0:T(8,128)(2,1)S(1)}, bf16[120,128]{1,0:T(8,128)(2,1)S(1)}, u32[]{:S(2)}, u32[]{:S(2)}) collective-permute-start(bf16[120,128]{1,0:T(8,128)(2,1)S(1)} %merge.1.rest_4_), channel_id=1, source_target_pairs={{0,2},{1,3},{2,0},{3,1},{4,6},{5,7},{6,4},{7,5},{8,10},{9,11},{10,... | collective-permute-start | bytes 92168 | tf_op jit(solution)/shard_map/ppermute | solution.py:303
  39.8 0.3 collective-permute-start.9
  40.2 0.1 fusion
  40.2 1.6 %collective-permute-done.11.rest_7_ = bf16[120,128]{1,0:T(8,128)(2,1)S(1)} collective-permute-done((bf16[120,128]{1,0:T(8,128)(2,1)S(1)}, bf16[120,128]{1,0:T(8,128)(2,1)S(1)}, u32[]{:S(2)}, u32[]{:S(2)}) %collective-permute-start.11) | collective-permute-done | bytes 30752 | tf_op jit(solution)/shard_map/ppermute | solution.py:303
  41.9 1.3 %collective-permute-done.10.rest_6_ = bf16[120,128]{1,0:T(8,128)(2,1)S(1)} collective-permute-done((bf16[120,128]{1,0:T(8,128)(2,1)S(1)}, bf16[120,128]{1,0:T(8,128)(2,1)S(1)}, u32[]{:S(2)}, u32[]{:S(2)}) %collective-permute-start.10) | collective-permute-done | bytes 30752 | tf_op jit(solution)/shard_map/ppermute | solution.py:303
  43.1 0.7 %copy-done.3 = f32[192]{0:T(256)S(1)} copy-done((f32[192]{0:T(256)S(1)}, f32[192]{0:T(256)}, u32[]{:S(2)}) %copy-start.3) | copy-done | bytes 792
  43.8 2.8 %output.1 = bf16[192,512]{1,0:T(8,128)(2,1)} custom-call(s32[1]{0:T(128)} %bitcast.place, s32[4,3]{1,0:T(4,128)S(1)} %get-tuple-element.32.mo, s32[4,3]{1,0:T(4,128)S(1)} %get-tuple-element.31.fo, bf16[512,768]{1,0:T(8,128)(2,1)S(1)} %copy-done.1, f32[1,192]{1,0:T(1,128)S(1)} %bitcast.5, f32[1,192]{1,0:T(1,128)S(1)} %bitcast.6, ...), custom_call_target="tpu_custom_call" | custom-call | flops 603979776 | bytes 4194304 | tf_op jit(solution)/shard_map/output/pallas_call | solution.py:273
  (18 shorter events, 0.0 us)
Async XLA Ops:
  0.0 0.7 %copy-start.6 = (s32[3]{0:T(128)S(1)}, s32[3]{0:T(128)}, u32[]{:S(2)}) copy-start(s32[3]{0:T(128)} %fo.5) | copy-start | bytes 40
  0.0 0.7 %copy-start.5 = (s32[3]{0:T(128)S(1)}, s32[3]{0:T(128)}, u32[]{:S(2)}) copy-start(s32[3]{0:T(128)} %mo.5) | copy-start | bytes 40
  0.7 1.1 %copy-start = (bf16[512,768]{1,0:T(8,128)(2,1)S(1)}, bf16[512,768]{1,0:T(8,128)(2,1)}, u32[]{:S(2)}) copy-start(bf16[512,768]{1,0:T(8,128)(2,1)} %x_ref.1) | copy-start | bytes 2359300
  1.8 1.2 %copy-start.7 = (bf16[3,768,192]{1,2,0:T(8,128)(2,1)S(1)}, bf16[3,768,192]{1,2,0:T(8,128)(2,1)}, u32[]{:S(2)}) copy-start(bf16[3,768,192]{1,2,0:T(8,128)(2,1)} %param.8) | copy-start | bytes 2654212
  3.0 3.7 %copy-start.2 = (bf16[192,768]{1,0:T(8,128)(2,1)S(1)}, bf16[192,768]{1,0:T(8,128)(2,1)}, u32[]{:S(2)}) copy-start(bf16[192,768]{1,0:T(8,128)(2,1)} %rest_8_.1) | copy-start | bytes 884740
  6.7 3.1 %collective-permute-start = (bf16[192,768]{1,0:T(8,128)(2,1)S(1)}, bf16[192,768]{1,0:T(8,128)(2,1)S(1)}, u32[]{:S(2)}, u32[]{:S(2)}) collective-permute-start(bf16[192,768]{1,0:T(8,128)(2,1)S(1)} %copy-done.2), channel_id=1, source_target_pairs={{0,1},{1,0},{2,3},{3,2},{4,5},{5,4},{6,7},{7,6},{8,9},{9,8},{10,11... | collective-permute-start | bytes 884744 | tf_op jit(solution)/shard_map/ppermute | solution.py:303
  7.2 10.2 %collective-permute-start.1 = (bf16[192,768]{1,0:T(8,128)(2,1)S(1)}, bf16[192,768]{1,0:T(8,128)(2,1)S(1)}, u32[]{:S(2)}, u32[]{:S(2)}) collective-permute-start(bf16[192,768]{1,0:T(8,128)(2,1)S(1)} %copy-done.2), channel_id=1, source_target_pairs={{0,2},{1,3},{2,0},{3,1},{4,6},{5,7},{6,4},{7,5},{8,10},{9,11},{10,... | collective-permute-start | bytes 884744 | tf_op jit(solution)/shard_map/ppermute | solution.py:303
  9.8 33.3 %copy-start.1 = (bf16[512,768]{1,0:T(8,128)(2,1)S(1)}, bf16[512,768]{1,0:T(8,128)(2,1)}, u32[]{:S(2)}) copy-start(bf16[512,768]{1,0:T(8,128)(2,1)} %x_ref.1) | copy-start | bytes 2359300
  17.4 3.4 %collective-permute-start.2 = (bf16[192,768]{1,0:T(8,128)(2,1)S(1)}, bf16[192,768]{1,0:T(8,128)(2,1)S(1)}, u32[]{:S(2)}, u32[]{:S(2)}) collective-permute-start(bf16[192,768]{1,0:T(8,128)(2,1)S(1)} %collective-permute-done.1.rest_10_), channel_id=1, source_target_pairs={{0,1},{1,0},{2,3},{3,2},{4,5},{5,4},{6,7},{7,6},{8,9},{9,8},{10,11... | collective-permute-start | bytes 884744 | tf_op jit(solution)/shard_map/ppermute | solution.py:303
  19.0 7.5 %collective-permute-start.4 = (bf16[784,128]{1,0:T(8,128)(2,1)S(1)}, bf16[784,128]{1,0:T(8,128)(2,1)S(1)}, u32[]{:S(2)}, u32[]{:S(2)}) collective-permute-start(bf16[784,128]{1,0:T(8,128)(2,1)S(1)} %get-tuple-element.25.rest_0_), channel_id=1, source_target_pairs={{0,2},{1,3},{2,0},{3,1},{4,6},{5,7},{6,4},{7,5},{8,10},{9,11},{10,... | collective-permute-start | bytes 602120 | tf_op jit(solution)/shard_map/ppermute | solution.py:303
  20.8 5.7 %collective-permute-start.3 = (bf16[784,128]{1,0:T(8,128)(2,1)S(1)}, bf16[784,128]{1,0:T(8,128)(2,1)S(1)}, u32[]{:S(2)}, u32[]{:S(2)}) collective-permute-start(bf16[784,128]{1,0:T(8,128)(2,1)S(1)} %get-tuple-element.25.rest_0_), channel_id=1, source_target_pairs={{0,1},{1,0},{2,3},{3,2},{4,5},{5,4},{6,7},{7,6},{8,9},{9,8},{10,11... | collective-permute-start | bytes 602120 | tf_op jit(solution)/shard_map/ppermute | solution.py:303
  26.5 13.7 %collective-permute-start.5 = (bf16[784,128]{1,0:T(8,128)(2,1)S(1)}, bf16[784,128]{1,0:T(8,128)(2,1)S(1)}, u32[]{:S(2)}, u32[]{:S(2)}) collective-permute-start(bf16[784,128]{1,0:T(8,128)(2,1)S(1)} %collective-permute-done.4.rest_2_), channel_id=1, source_target_pairs={{0,1},{1,0},{2,3},{3,2},{4,5},{5,4},{6,7},{7,6},{8,9},{9,8},{10,11... | collective-permute-start | bytes 602120 | tf_op jit(solution)/shard_map/ppermute | solution.py:303
  26.5 6.2 %collective-permute-start.8 = (bf16[240,128]{1,0:T(8,128)(2,1)S(1)}, bf16[240,128]{1,0:T(8,128)(2,1)S(1)}, u32[]{:S(2)}, u32[]{:S(2)}) collective-permute-start(bf16[240,128]{1,0:T(8,128)(2,1)S(1)} %get-tuple-element.19.rest_0_.rest_4_), channel_id=1, source_target_pairs={{0,12},{4,0},{8,4},{12,8},{1,13},{5,1},{9,5},{13,9},{2,14},{6,2},{... | collective-permute-start | bytes 184328 | tf_op jit(solution)/shard_map/ppermute | solution.py:340
  30.3 6.8 %collective-permute-start.7 = (bf16[240,128]{1,0:T(8,128)(2,1)S(1)}, bf16[240,128]{1,0:T(8,128)(2,1)S(1)}, u32[]{:S(2)}, u32[]{:S(2)}) collective-permute-start(bf16[240,128]{1,0:T(8,128)(2,1)S(1)} %get-tuple-element.19.rest_0_.rest_4_), channel_id=1, source_target_pairs={{0,8},{4,12},{8,0},{12,4},{1,9},{5,13},{9,1},{13,5},{2,10},{6,14},... | collective-permute-start | bytes 184328 | tf_op jit(solution)/shard_map/ppermute | solution.py:340
  30.3 6.8 %collective-permute-start.6 = (bf16[240,128]{1,0:T(8,128)(2,1)S(1)}, bf16[240,128]{1,0:T(8,128)(2,1)S(1)}, u32[]{:S(2)}, u32[]{:S(2)}) collective-permute-start(bf16[240,128]{1,0:T(8,128)(2,1)S(1)} %get-tuple-element.19.rest_0_.rest_4_), channel_id=1, source_target_pairs={{0,4},{4,8},{8,12},{12,0},{1,5},{5,9},{9,13},{13,1},{2,6},{6,10},{... | collective-permute-start | bytes 184328 | tf_op jit(solution)/shard_map/ppermute | solution.py:340
  37.1 6.0 %copy-start.4 = (f32[192]{0:T(256)S(1)}, f32[192]{0:T(256)}, u32[]{:S(2)}) copy-start(f32[192]{0:T(256)} %param.11) | copy-start | bytes 2308
  38.2 3.7 %collective-permute-start.11 = (bf16[120,128]{1,0:T(8,128)(2,1)S(1)}, bf16[120,128]{1,0:T(8,128)(2,1)S(1)}, u32[]{:S(2)}, u32[]{:S(2)}) collective-permute-start(bf16[120,128]{1,0:T(8,128)(2,1)S(1)} %merge.1.rest_4_), channel_id=1, source_target_pairs={{0,3},{1,2},{2,1},{3,0},{4,7},{5,6},{6,5},{7,4},{8,11},{9,10},{10,... | collective-permute-start | bytes 92168 | tf_op jit(solution)/shard_map/ppermute | solution.py:303
  39.2 4.0 %collective-permute-start.10 = (bf16[120,128]{1,0:T(8,128)(2,1)S(1)}, bf16[120,128]{1,0:T(8,128)(2,1)S(1)}, u32[]{:S(2)}, u32[]{:S(2)}) collective-permute-start(bf16[120,128]{1,0:T(8,128)(2,1)S(1)} %merge.1.rest_4_), channel_id=1, source_target_pairs={{0,2},{1,3},{2,0},{3,1},{4,6},{5,7},{6,4},{7,5},{8,10},{9,11},{10,... | collective-permute-start | bytes 92168 | tf_op jit(solution)/shard_map/ppermute | solution.py:303
  39.8 3.3 %collective-permute-start.9 = (bf16[120,128]{1,0:T(8,128)(2,1)S(1)}, bf16[120,128]{1,0:T(8,128)(2,1)S(1)}, u32[]{:S(2)}, u32[]{:S(2)}) collective-permute-start(bf16[120,128]{1,0:T(8,128)(2,1)S(1)} %merge.1.rest_4_), channel_id=1, source_target_pairs={{0,1},{1,0},{2,3},{3,2},{4,5},{5,4},{6,7},{7,6},{8,9},{9,8},{10,11... | collective-permute-start | bytes 92168 | tf_op jit(solution)/shard_map/ppermute | solution.py:303
  43.1 0.7 %copy-start.3 = (f32[192]{0:T(256)S(1)}, f32[192]{0:T(256)}, u32[]{:S(2)}) copy-start(f32[192]{0:T(256)} %param.10) | copy-start | bytes 2308

commit v3 on v2

--- a/solution.py
+++ b/solution.py
@@ -98,17 +98,21 @@
 
 def pair(a, b):
     low = lane_half(a.shape)
-    return (jnp.where(low, a, b) / swap(jnp.where(low, b, a))).astype(bf16)
+    return jnp.where(low, a, b) / swap(jnp.where(low, b, a))
 
 
 def fold(x):
     half = x.shape[0] // 2
     a, b = x[:half], x[half:]
     low = lane_half(a.shape)
-    return (jnp.where(low, a, swap(b)) / jnp.where(low, swap(a), b)).astype(bf16)
-
-
-def near_kernel(factor, mo, fo, qkv_ref, near_ref, am_ref, pk_ref, am_scr, pk_scr):
+    return jnp.where(low, a, swap(b)) / jnp.where(low, swap(a), b)
+
+
+def near_kernel(
+    factor, mo, fo, qkv_ref, gain_ref, bias_ref, near_ref, am_ref, pk_ref, gb_ref, am_scr, pk_scr
+):
+    gb_ref[0:1] = gain_ref[...]
+    gb_ref[1:2] = bias_ref[...]
     rows = qkv_ref.shape[0]
     mid, far = rows // R1, rows // R2
     per = mid + far
@@ -140,12 +144,7 @@
         pk_scr[h, rows_of(b)] = jnp.broadcast_to(peak, am[u].shape)
         if h == 2:
             near_ref[rows_of(b)] = pair(am.pop((b, 0)), am.pop((b, 1)))
-    near_ref[rows : rows + rows // 2] = fold(am_scr[2])
-    lane = lax.broadcasted_iota(jnp.int32, (16, LANES), 1)
-    told = jnp.zeros((16, LANES), jnp.int32)
-    for h in range(3):
-        told = jnp.where(lane == h, mo[h], jnp.where(lane == 3 + h, fo[h], told))
-    near_ref[rows + rows // 2 :] = told.astype(f32).astype(bf16)
+    near_ref[rows:] = fold(am_scr[2])
     for h in range(3):
         own, own_far = slice(h * per, h * per + mid), slice(h * per + mid, (h + 1) * per)
         mid_rows = pl.ds(mo[h], mid, stride=R1)
@@ -154,9 +153,11 @@
         pk_ref[own], pk_ref[own_far] = pk_scr[h, mid_rows], pk_scr[h, far_rows]
 
 
-def merge_kernel(factor, mid_n, far_n, mo, fo, qp_ref, am_ref, pk_ref, *rest):
+def merge_kernel(factor, mid_n, far_n, mo, fo, near_ref, qp_ref, am_ref, pk_ref, *rest):
     mids, fars = rest[:mid_n], rest[mid_n : mid_n + far_n]
-    corr_ref, am_scr, pk_scr = rest[mid_n + far_n :]
+    attn_ref, attn_scr, am_scr, pk_scr = rest[mid_n + far_n :]
+    rows = near_ref.shape[0] * 2 // 3
+    attn_scr[...] = near_ref[...]
     per = qp_ref.shape[0] // 3
     far = per * R1 // (R1 + R2)
     mid = per - far
@@ -198,50 +199,23 @@
             + jnp.exp2((both_peak - top) * factor) * both_am
             + jnp.exp2((soft_far[h][0] - top) * factor) * am_far[h]
         )
-    corr_ref[:mid] = pair(out_mid[0], out_mid[1])
-    corr_ref[mid:per] = pair(out_far[0], out_far[1])
-    corr_ref[per : per + mid // 2] = fold(out_mid[2])
-    corr_ref[per + mid // 2 :] = fold(out_far[2])
-
-
-def output_kernel(head_count, place, mo, fo, x_ref, gain_ref, bias_ref, *rest):
-    near, corr, weights = (rest[i * head_count : (i + 1) * head_count] for i in range(3))
-    out_ref, attn_scr, resid_scr = rest[3 * head_count :]
+    for offset, stride, count, out in ((mo, R1, mid, out_mid), (fo, R2, far, out_far)):
+        both = pair(out[0], out[1])
+        low = lane_half(both.shape)
+        for h, keep in ((0, low), (1, jnp.logical_not(low))):
+            at = pl.ds(offset[h], count, stride=stride)
+            attn_scr[at] = jnp.where(keep, both, attn_scr[at])
+        attn_scr[pl.ds(rows + offset[2], count // 2, stride=stride)] = fold(out[2])
+    attn_ref[...] = attn_scr[...].astype(bf16)
+
+
+def output_kernel(head_count, place, x_ref, gb_ref, *rest):
+    attns, weights = rest[:head_count], rest[head_count : 2 * head_count]
+    out_ref, resid_scr = rest[2 * head_count :]
     rows, width = x_ref.shape
-    mid, far = rows // R1, rows // R2
     half = rows // 2
-    per = mid + far
     cols = width // head_count
-    for r in range(head_count):
-        attn_scr[r] = near[r][:rows].astype(f32)
     low = lane_half((half, LANES))
-    for r in range(0, head_count, 2):
-        even = near[r][rows : rows + half].astype(f32)
-        odd = near[r + 1][rows : rows + half].astype(f32)
-        attn_scr[head_count + r // 2, :half] = jnp.where(low, even, swap(odd))
-        attn_scr[head_count + r // 2, half:] = jnp.where(low, swap(even), odd)
-
-    def patch(tile, to_low, first, count, stride, value):
-        at = pl.ds(first, count, stride=stride)
-        low = lane_half(value.shape)
-        keep = low if to_low else jnp.logical_not(low)
-        attn_scr[tile, at] = jnp.where(keep, value, attn_scr[tile, at])
-
-    for offset, stride, count, first, folded in (
-        (mo, R1, mid, 0, per),
-        (fo, R2, far, mid, per + mid // 2),
-    ):
-        for r in range(head_count):
-            both = corr[r][first : first + count].astype(f32)
-            patch(r, True, offset[r, 0], count, stride, both)
-            patch(r, False, offset[r, 1], count, stride, both)
-            third = corr[r][folded : folded + count // 2].astype(f32)
-            turned = swap(third)
-            tile, to_low = head_count + r // 2, r % 2 == 0
-            upper, lower = (third, turned) if to_low else (turned, third)
-            patch(tile, to_low, offset[r, 2], count // 2, stride, upper)
-            patch(tile, to_low, offset[r, 2] + half, count // 2, stride, lower)
-
     w = jnp.concatenate(
         [weights[r][:LANES] for r in range(head_count)]
         + [weights[r][LANES:] for r in range(head_count)],
@@ -249,9 +223,16 @@
     )
     for first in (0, half):
         at = slice(first, first + half)
-        attn = jnp.concatenate(
-            [attn_scr[t, at].astype(bf16) for t in range(attn_scr.shape[0])], axis=1
-        )
+        tiles = [attns[r][at] for r in range(head_count)]
+        for r in range(0, head_count, 2):
+            even = attns[r][rows:].astype(f32)
+            odd = attns[r + 1][rows:].astype(f32)
+            if first == 0:
+                joined = jnp.where(low, even, swap(odd))
+            else:
+                joined = jnp.where(low, swap(even), odd)
+            tiles.append(joined.astype(bf16))
+        attn = jnp.concatenate(tiles, axis=1)
         resid = x_ref[at].astype(f32) + jnp.dot(attn, w, preferred_element_type=f32)
         mean = jnp.sum(resid, axis=1, keepdims=True) / width
         var = jnp.sum(resid * resid, axis=1, keepdims=True) / width - mean * mean
@@ -261,7 +242,7 @@
         @pl.when(place[0] == i)
         def _():
             mine = resid_scr[:, i * cols : (i + 1) * cols]
-            out_ref[...] = (mine * gain_ref[...] + bias_ref[...]).T.astype(bf16)
+            out_ref[...] = (mine * gb_ref[0:1] + gb_ref[1:2]).T.astype(bf16)
 
 
 IN_VMEM = pl.BlockSpec(memory_space=pltpu.VMEM)
@@ -269,17 +250,17 @@
 IN_HBM = pl.BlockSpec(memory_space=pltpu.HBM)
 
 
-def call(kernel, outs, scratch, scalars, arrays, name, cost, held=IN_VMEM):
+def call(kernel, outs, scratch, scalars, far, near, name, flops, limit):
     return pl.pallas_call(
         kernel,
         out_shape=outs,
-        in_specs=[IN_SMEM] * len(scalars) + [held] * len(arrays),
+        in_specs=[IN_SMEM] * len(scalars) + [IN_HBM] * len(far) + [IN_VMEM] * len(near),
         out_specs=jax.tree.map(lambda _: IN_VMEM, outs),
         scratch_shapes=scratch,
-        compiler_params=pltpu.CompilerParams(vmem_limit_bytes=32 << 20),
+        compiler_params=pltpu.CompilerParams(vmem_limit_bytes=limit << 20),
         name=name,
-        cost_estimate=pl.CostEstimate(flops=cost, transcendentals=0, bytes_accessed=4 << 20),
-    )(*scalars, *arrays)
+        cost_estimate=pl.CostEstimate(flops=flops, transcendentals=0, bytes_accessed=4 << 20),
+    )(*scalars, *far, *near)
 
 
 def local(tokens, w_qkv, w_out, gain, bias, mid_offset, far_offset):
@@ -323,9 +304,10 @@
         ],
         (mid_offset, far_offset),
         (tokens, jnp.swapaxes(w_qkv, 1, 2)),
+        (),
         "project",
         2 * rows * width * 3 * cols,
-        IN_HBM,
+        56,
     )
 
     seq_count = lax.axis_size("seq")
@@ -346,59 +328,57 @@
         fars = [lax.all_gather(split[:, mid:], "seq", axis=1, tiled=True)]
 
     if two_step:
-        across = to(w_out, 2)
-        beside = to(after((w_out, kvp))[0], 1)
-        qkv, beside = after((qkv, beside))
+        across = to(after((w_out, mids[1]))[0], 2)
+        beside = to(after((w_out, mids[1]))[0], 1)
+        weights = [w_out, beside, across, to(across, 1)]
     else:
         weights = spread(w_out)
 
-    near, am, pk = call(
+    near, am, pk, gb = call(
         partial(near_kernel, factor),
         (
-            shape((rows + rows // 2 + 16, LANES), bf16),
+            shape((rows + rows // 2, LANES), f32),
             shape((3 * per, LANES), f32),
             shape((3 * per, LANES), f32),
+            shape((2, cols), f32),
         ),
         [pltpu.VMEM((3, rows, LANES), f32)] * 2,
         (mid_offset, far_offset),
-        (qkv,),
+        (),
+        (qkv, gain.reshape(1, cols), bias.reshape(1, cols)),
         "near",
-        1 << 28,
+        1 << 29,
+        24,
+    )
+    attn = call(
+        partial(merge_kernel, factor, len(mids), len(fars or mids)),
+        shape((rows + rows // 2, LANES), bf16),
+        [pltpu.VMEM((rows + rows // 2, LANES), f32)] + [pltpu.VMEM((3, mid, LANES), f32)] * 2,
+        (mid_offset, far_offset),
+        (),
+        (near, qp, am, pk, *mids, *(fars or mids)),
+        "merge",
+        1 << 29,
+        24,
     )
     if two_step:
-        last = to(after((across, beside))[0], 1)
-        weights = [w_out, beside, across, last]
-        near_across = to(after((near, across))[0], 2)
-        near_beside = to(after((near, last))[0], 1)
-        near_last = to(after((near_across, near_beside))[0], 1)
-        nears = [near, near_beside, near_across, near_last]
+        attn_across = to(attn, 2)
+        attns = [attn, to(attn, 1), attn_across, to(attn_across, 1)]
     else:
-        nears = spread(near)
-
-    corr = call(
-        partial(merge_kernel, factor, len(mids), len(fars or mids)),
-        shape((per + per // 2, LANES), bf16),
-        [pltpu.VMEM((3, mid, LANES), f32)] * 2,
-        (mid_offset, far_offset),
-        (qp, am, pk, *mids, *(fars or mids)),
-        "merge",
-        1 << 27,
-    )
-    corrs = spread(corr)
-    told = [n[rows + rows // 2, : 2 * heads_here].astype(jnp.int32) for n in nears]
-    told = jnp.stack(told)
+        attns = spread(attn)
 
     out = call(
         partial(output_kernel, head_count),
         shape((cols, rows), bf16),
         [
-            pltpu.VMEM((head_count + head_count // 2, rows, LANES), f32),
             pltpu.VMEM((rows, width), f32),
         ],
-        (lax.axis_index("head").reshape(1), told[:, :heads_here], told[:, heads_here:]),
-        (tokens, gain.reshape(1, cols), bias.reshape(1, cols), *nears, *corrs, *weights),
+        (lax.axis_index("head").reshape(1),),
+        (),
+        (tokens, gb, *attns, *weights),
         "output",
         2 * rows * width * width,
+        24,
     )
     return out.T
 

time: 46.8 us -> 31 us (0.66)
  waiting for transfers between devices: 21.7 us -> 13 us
  starting transfers between devices: 11.9 us -> 7.5 us
  local copies, waits for them, and re-layouts: 3.72 us -> 1.77 us
  Pallas kernels: 9.19 us -> 8.49 us
    ppermute x9 -> x6, waiting for transfers between devices: 15.9 us -> 6.27 us  [to(): return lax.ppermute(array, 'head', paths[r])]
    ppermute x9 -> x6, starting transfers between devices: 7.06 us -> 2.61 us  [to(): return lax.ppermute(array, 'head', paths[r])]
    unnamed x16 -> x18, local copies, waits for them, and re-layouts: 3.64 us -> 1.77 us
    ppermute x3, waiting for transfers between devices: 5.78 us -> 6.7 us  [local(): lax.ppermute(kvp, 'seq', within(s))]
    pallas_call x4, Pallas kernels: 9.19 us -> 8.49 us  [call(): pl.pallas_call(kernel, out_shape=outs, in_specs=[IN_SMEM] * len(scalars)...]
  transfers between devices with their start and end apart: 12 -> 9, of which waited for: 6 -> 4; matrix products, arithmetic and copies ran while one was open for 0% -> 0% of each run, Pallas kernels for 6% -> 9%
where the time goes in v3:
time: 31 us; the launch traced here: 30.8 us
  waiting for transfers between devices  13 us (42%)
  Pallas kernels  8.49 us (27%)
  starting transfers between devices  7.5 us (24%)
  local copies, waits for them, and re-layouts  1.77 us (6%)
    pallas_call x4, Pallas kernels, call(): pl.pallas_call(kernel, out_shape=outs, in_specs=[IN_SMEM] * len(scalars)...  8.49 us
    ppermute x3, waiting for transfers between devices, local(): lax.ppermute(kvp, 'seq', within(s))  6.7 us
    ppermute x6, waiting for transfers between devices, to(): return lax.ppermute(array, 'head', paths[r])  6.27 us
    ppermute x3, starting transfers between devices, local(): lax.ppermute(kvp, 'seq', within(s))  4.89 us
    ppermute x6, starting transfers between devices, to(): return lax.ppermute(array, 'head', paths[r])  2.61 us
    unnamed x18, local copies, waits for them, and re-layouts  1.77 us
  transfers between devices with their start and end apart: 9, of which 4 were waited for; matrix products, arithmetic and copies ran while one was open for 0% of the time, Pallas kernels for 9%

profile of v3, /device:TPU:0, one launch (start us, length us, event | category | flops | bytes accessed | tf_op | source)
XLA Modules:
  0.0 30.8 jit_solution(5193984784807311894)
XLA Ops:
  0.0 0.0 copy-start.1
  0.0 4.1 %project.1 = (bf16[512,640]{1,0:T(8,128)(2,1)}, bf16[240,128]{1,0:T(8,128)(2,1)}, bf16[240,128]{1,0:T(8,128)(2,1)}) custom-call(s32[3]{0:T(128)} %mo.5, s32[3]{0:T(128)} %fo.5, bf16[512,768]{1,0:T(8,128)(2,1)} %x_ref.1, bf16[3,192,768]{2,1,0:T(8,128)(2,1)} %bitcast.7), custom_call_target="tpu_custom_call" | custom-call | flops 452984832 | bytes 4194304 | tf_op jit(solution)/shard_map/project/pallas_call | solution.py:254
  4.1 3.1 %collective-permute-start = (bf16[240,128]{1,0:T(8,128)(2,1)}, bf16[240,128]{1,0:T(8,128)(2,1)S(1)}, u32[]{:S(2)}, u32[]{:S(2)}) collective-permute-start(bf16[240,128]{1,0:T(8,128)(2,1)} %get-tuple-element.19.rest_0_.rest_4_), channel_id=1, source_target_pairs={{0,4},{4,8},{8,12},{12,0},{1,5},{5,9},{9,13},{13,1},{2,6},{6,10},{... | collective-permute-start | bytes 184328 | tf_op jit(solution)/shard_map/ppermute | solution.py:322
  7.2 4.4 %collective-permute-done.rest_1_.rest_5_ = bf16[240,128]{1,0:T(8,128)(2,1)S(1)} collective-permute-done((bf16[240,128]{1,0:T(8,128)(2,1)}, bf16[240,128]{1,0:T(8,128)(2,1)S(1)}, u32[]{:S(2)}, u32[]{:S(2)}) %collective-permute-start) | collective-permute-done | bytes 61472 | tf_op jit(solution)/shard_map/ppermute | solution.py:322
  11.6 0.0 copy-done.1
  11.6 1.7 %collective-permute-start.7 = (bf16[192,768]{1,0:T(8,128)(2,1)S(1)}, bf16[192,768]{1,0:T(8,128)(2,1)S(1)}, u32[]{:S(2)}, u32[]{:S(2)}) collective-permute-start(bf16[192,768]{1,0:T(8,128)(2,1)S(1)} %copy-done.1), channel_id=1, source_target_pairs={{0,2},{1,3},{2,0},{3,1},{4,6},{5,7},{6,4},{7,5},{8,10},{9,11},{10,... | collective-permute-start | bytes 884744 | tf_op jit(solution)/shard_map/ppermute | solution.py:284
  13.3 1.8 %collective-permute-start.2 = (bf16[240,128]{1,0:T(8,128)(2,1)}, bf16[240,128]{1,0:T(8,128)(2,1)S(1)}, u32[]{:S(2)}, u32[]{:S(2)}) collective-permute-start(bf16[240,128]{1,0:T(8,128)(2,1)} %get-tuple-element.19.rest_0_.rest_4_), channel_id=1, source_target_pairs={{0,12},{4,0},{8,4},{12,8},{1,13},{5,1},{9,5},{13,9},{2,14},{6,2},{... | collective-permute-start | bytes 184328 | tf_op jit(solution)/shard_map/ppermute | solution.py:322
  15.1 0.0 collective-permute-start.1
  15.1 0.0 copy-done.4
  15.1 0.0 copy-done.6
  15.1 0.7 %copy-done.3 = f32[192]{0:T(256)S(1)} copy-done((f32[192]{0:T(256)S(1)}, f32[192]{0:T(256)}, u32[]{:S(2)}) %copy-start.3) | copy-done | bytes 792
  15.8 0.0 copy-done.5
  15.8 1.1 %copy-done.7 = bf16[512,640]{1,0:T(8,128)(2,1)S(1)} copy-done((bf16[512,640]{1,0:T(8,128)(2,1)S(1)}, bf16[512,640]{1,0:T(8,128)(2,1)}, u32[]{:S(2)}) %copy-start.7) | copy-done | bytes 655384
  16.9 1.6 %near.1 = (f32[768,128]{1,0:T(8,128)S(1)}, f32[240,128]{1,0:T(8,128)S(1)}, f32[240,128]{1,0:T(8,128)S(1)}, f32[2,192]{1,0:T(2,128)S(1)}) custom-call(s32[3]{0:T(128)S(1)} %copy-done.5, s32[3]{0:T(128)S(1)} %copy-done.6, bf16[512,640]{1,0:T(8,128)(2,1)S(1)} %copy-done.7, f32[1,192]{1,0:T(1,128)S(1)} %bitcast.5, f32[1,192]{1,0:T(1,128)S(1)} %bitcast.6), custom_call_target="tpu_custom_call" | custom-call | flops 536870912 | bytes 4194304 | tf_op jit(solution)/shard_map/near/pallas_call | solution.py:254
  18.5 0.0 collective-permute-done.2.rest_3_.rest_7_
  18.5 2.3 %collective-permute-done.1.rest_2_.rest_6_ = bf16[240,128]{1,0:T(8,128)(2,1)S(1)} collective-permute-done((bf16[240,128]{1,0:T(8,128)(2,1)}, bf16[240,128]{1,0:T(8,128)(2,1)S(1)}, u32[]{:S(2)}, u32[]{:S(2)}) %collective-permute-start.1) | collective-permute-done | bytes 61472 | tf_op jit(solution)/shard_map/ppermute | solution.py:322
  20.8 0.0 copy-done.2
  20.8 0.0 copy-done.8
  20.8 1.1 %merge.1.rest_0_ = bf16[768,128]{1,0:T(8,128)(2,1)S(1)} custom-call(s32[3]{0:T(128)S(1)} %copy-done.5, s32[3]{0:T(128)S(1)} %copy-done.6, f32[768,128]{1,0:T(8,128)S(1)} %get-tuple-element.15.near_ref, bf16[240,128]{1,0:T(8,128)(2,1)S(1)} %copy-done.8, f32[240,128]{1,0:T(8,128)S(1)} %get-tuple-element.17.am_ref, f32[240,128]{1,0:T(8,128)S(1)} %get-tuple-element.18.pk_ref, ...), custom_call_target="tpu_custom_call" | custom-call | flops 536870912 | bytes 4194304 | tf_op jit(solution)/shard_map/merge/pallas_call | solution.py:254
  21.9 0.4 %collective-permute-start.4 = (bf16[768,128]{1,0:T(8,128)(2,1)S(1)}, bf16[768,128]{1,0:T(8,128)(2,1)S(1)}, u32[]{:S(2)}, u32[]{:S(2)}) collective-permute-start(bf16[768,128]{1,0:T(8,128)(2,1)S(1)} %merge.1.rest_0_), channel_id=1, source_target_pairs={{0,2},{1,3},{2,0},{3,1},{4,6},{5,7},{6,4},{7,5},{8,10},{9,11},{10,... | collective-permute-start | bytes 589832 | tf_op jit(solution)/shard_map/ppermute | solution.py:284
  22.2 0.0 collective-permute-start.6
  22.3 0.0 collective-permute-done.7.rest_6_
  22.3 0.5 %collective-permute-start.8 = (bf16[192,768]{1,0:T(8,128)(2,1)S(1)}, bf16[192,768]{1,0:T(8,128)(2,1)S(1)}, u32[]{:S(2)}, u32[]{:S(2)}) collective-permute-start(bf16[192,768]{1,0:T(8,128)(2,1)S(1)} %collective-permute-done.7.rest_6_), channel_id=1, source_target_pairs={{0,1},{1,0},{2,3},{3,2},{4,5},{5,4},{6,7},{7,6},{8,9},{9,8},{10,11... | collective-permute-start | bytes 884744 | tf_op jit(solution)/shard_map/ppermute | solution.py:284
  22.8 0.0 collective-permute-start.3
  22.8 4.8 %collective-permute-done.4.rest_2_ = bf16[768,128]{1,0:T(8,128)(2,1)S(1)} collective-permute-done((bf16[768,128]{1,0:T(8,128)(2,1)S(1)}, bf16[768,128]{1,0:T(8,128)(2,1)S(1)}, u32[]{:S(2)}, u32[]{:S(2)}) %collective-permute-start.4) | collective-permute-done | bytes 196640 | tf_op jit(solution)/shard_map/ppermute | solution.py:284
  27.6 0.0 collective-permute-start.5
  27.6 0.0 collective-permute-done.3.rest_1_
  27.6 0.0 collective-permute-done.6.rest_5_
  27.6 1.4 %collective-permute-done.5.rest_3_ = bf16[768,128]{1,0:T(8,128)(2,1)S(1)} collective-permute-done((bf16[768,128]{1,0:T(8,128)(2,1)S(1)}, bf16[768,128]{1,0:T(8,128)(2,1)S(1)}, u32[]{:S(2)}, u32[]{:S(2)}) %collective-permute-start.5) | collective-permute-done | bytes 196640 | tf_op jit(solution)/shard_map/ppermute | solution.py:284
  29.0 0.0 collective-permute-done.8.rest_7_
  29.0 0.0 copy-done
  29.0 1.8 %output.1 = bf16[192,512]{1,0:T(8,128)(2,1)} custom-call(s32[1]{0:T(128)} %bitcast.place, bf16[512,768]{1,0:T(8,128)(2,1)S(1)} %copy-done, f32[2,192]{1,0:T(2,128)S(1)} %get-tuple-element.14.gb_ref, bf16[768,128]{1,0:T(8,128)(2,1)S(1)} %merge.1.rest_0_, bf16[768,128]{1,0:T(8,128)(2,1)S(1)} %collective-permute-done.3.rest_1_, ...), custom_call_target="tpu_custom_call" | custom-call | flops 603979776 | bytes 4194304 | tf_op jit(solution)/shard_map/output/pallas_call | solution.py:254
  (8 shorter events, 0.0 us)
Async XLA Ops:
  0.0 11.6 %copy-start.1 = (bf16[192,768]{1,0:T(8,128)(2,1)S(1)}, bf16[192,768]{1,0:T(8,128)(2,1)}, u32[]{:S(2)}) copy-start(bf16[192,768]{1,0:T(8,128)(2,1)} %rest_4_.1) | copy-start | bytes 884740
  0.0 15.1 %copy-start.4 = (f32[192]{0:T(256)S(1)}, f32[192]{0:T(256)}, u32[]{:S(2)}) copy-start(f32[192]{0:T(256)} %param.11) | copy-start | bytes 2308
  0.0 15.1 %copy-start.6 = (s32[3]{0:T(128)S(1)}, s32[3]{0:T(128)}, u32[]{:S(2)}) copy-start(s32[3]{0:T(128)} %fo.5) | copy-start | bytes 40
  4.1 7.5 %collective-permute-start = (bf16[240,128]{1,0:T(8,128)(2,1)}, bf16[240,128]{1,0:T(8,128)(2,1)S(1)}, u32[]{:S(2)}, u32[]{:S(2)}) collective-permute-start(bf16[240,128]{1,0:T(8,128)(2,1)} %get-tuple-element.19.rest_0_.rest_4_), channel_id=1, source_target_pairs={{0,4},{4,8},{8,12},{12,0},{1,5},{5,9},{9,13},{13,1},{2,6},{6,10},{... | collective-permute-start | bytes 184328 | tf_op jit(solution)/shard_map/ppermute | solution.py:322
  11.6 10.7 %collective-permute-start.7 = (bf16[192,768]{1,0:T(8,128)(2,1)S(1)}, bf16[192,768]{1,0:T(8,128)(2,1)S(1)}, u32[]{:S(2)}, u32[]{:S(2)}) collective-permute-start(bf16[192,768]{1,0:T(8,128)(2,1)S(1)} %copy-done.1), channel_id=1, source_target_pairs={{0,2},{1,3},{2,0},{3,1},{4,6},{5,7},{6,4},{7,5},{8,10},{9,11},{10,... | collective-permute-start | bytes 884744 | tf_op jit(solution)/shard_map/ppermute | solution.py:284
  13.3 5.2 %collective-permute-start.2 = (bf16[240,128]{1,0:T(8,128)(2,1)}, bf16[240,128]{1,0:T(8,128)(2,1)S(1)}, u32[]{:S(2)}, u32[]{:S(2)}) collective-permute-start(bf16[240,128]{1,0:T(8,128)(2,1)} %get-tuple-element.19.rest_0_.rest_4_), channel_id=1, source_target_pairs={{0,12},{4,0},{8,4},{12,8},{1,13},{5,1},{9,5},{13,9},{2,14},{6,2},{... | collective-permute-start | bytes 184328 | tf_op jit(solution)/shard_map/ppermute | solution.py:322
  15.1 5.6 %collective-permute-start.1 = (bf16[240,128]{1,0:T(8,128)(2,1)}, bf16[240,128]{1,0:T(8,128)(2,1)S(1)}, u32[]{:S(2)}, u32[]{:S(2)}) collective-permute-start(bf16[240,128]{1,0:T(8,128)(2,1)} %get-tuple-element.19.rest_0_.rest_4_), channel_id=1, source_target_pairs={{0,8},{4,12},{8,0},{12,4},{1,9},{5,13},{9,1},{13,5},{2,10},{6,14},... | collective-permute-start | bytes 184328 | tf_op jit(solution)/shard_map/ppermute | solution.py:322
  15.1 0.7 %copy-start.3 = (f32[192]{0:T(256)S(1)}, f32[192]{0:T(256)}, u32[]{:S(2)}) copy-start(f32[192]{0:T(256)} %param.10) | copy-start | bytes 2308
  15.1 0.7 %copy-start.5 = (s32[3]{0:T(128)S(1)}, s32[3]{0:T(128)}, u32[]{:S(2)}) copy-start(s32[3]{0:T(128)} %mo.5) | copy-start | bytes 40
  15.8 1.1 %copy-start.7 = (bf16[512,640]{1,0:T(8,128)(2,1)S(1)}, bf16[512,640]{1,0:T(8,128)(2,1)}, u32[]{:S(2)}) copy-start(bf16[512,640]{1,0:T(8,128)(2,1)} %get-tuple-element.13.qkv_ref) | copy-start | bytes 1966084
  16.9 3.9 %copy-start.2 = (bf16[240,128]{1,0:T(8,128)(2,1)S(1)}, bf16[240,128]{1,0:T(8,128)(2,1)}, u32[]{:S(2)}) copy-start(bf16[240,128]{1,0:T(8,128)(2,1)} %get-tuple-element.19.rest_0_.rest_4_) | copy-start | bytes 184324
  16.9 3.9 %copy-start.8 = (bf16[240,128]{1,0:T(8,128)(2,1)S(1)}, bf16[240,128]{1,0:T(8,128)(2,1)}, u32[]{:S(2)}) copy-start(bf16[240,128]{1,0:T(8,128)(2,1)} %get-tuple-element.16.qp_ref) | copy-start | bytes 184324
  20.8 8.3 %copy-start = (bf16[512,768]{1,0:T(8,128)(2,1)S(1)}, bf16[512,768]{1,0:T(8,128)(2,1)}, u32[]{:S(2)}) copy-start(bf16[512,768]{1,0:T(8,128)(2,1)} %x_ref.1) | copy-start | bytes 2359300
  21.9 5.7 %collective-permute-start.4 = (bf16[768,128]{1,0:T(8,128)(2,1)S(1)}, bf16[768,128]{1,0:T(8,128)(2,1)S(1)}, u32[]{:S(2)}, u32[]{:S(2)}) collective-permute-start(bf16[768,128]{1,0:T(8,128)(2,1)S(1)} %merge.1.rest_0_), channel_id=1, source_target_pairs={{0,2},{1,3},{2,0},{3,1},{4,6},{5,7},{6,4},{7,5},{8,10},{9,11},{10,... | collective-permute-start | bytes 589832 | tf_op jit(solution)/shard_map/ppermute | solution.py:284
  22.2 5.4 %collective-permute-start.6 = (bf16[192,768]{1,0:T(8,128)(2,1)S(1)}, bf16[192,768]{1,0:T(8,128)(2,1)S(1)}, u32[]{:S(2)}, u32[]{:S(2)}) collective-permute-start(bf16[192,768]{1,0:T(8,128)(2,1)S(1)} %copy-done.1), channel_id=1, source_target_pairs={{0,1},{1,0},{2,3},{3,2},{4,5},{5,4},{6,7},{7,6},{8,9},{9,8},{10,11... | collective-permute-start | bytes 884744 | tf_op jit(solution)/shard_map/ppermute | solution.py:284
  22.3 6.8 %collective-permute-start.8 = (bf16[192,768]{1,0:T(8,128)(2,1)S(1)}, bf16[192,768]{1,0:T(8,128)(2,1)S(1)}, u32[]{:S(2)}, u32[]{:S(2)}) collective-permute-start(bf16[192,768]{1,0:T(8,128)(2,1)S(1)} %collective-permute-done.7.rest_6_), channel_id=1, source_target_pairs={{0,1},{1,0},{2,3},{3,2},{4,5},{5,4},{6,7},{7,6},{8,9},{9,8},{10,11... | collective-permute-start | bytes 884744 | tf_op jit(solution)/shard_map/ppermute | solution.py:284
  22.8 4.8 %collective-permute-start.3 = (bf16[768,128]{1,0:T(8,128)(2,1)S(1)}, bf16[768,128]{1,0:T(8,128)(2,1)S(1)}, u32[]{:S(2)}, u32[]{:S(2)}) collective-permute-start(bf16[768,128]{1,0:T(8,128)(2,1)S(1)} %merge.1.rest_0_), channel_id=1, source_target_pairs={{0,1},{1,0},{2,3},{3,2},{4,5},{5,4},{6,7},{7,6},{8,9},{9,8},{10,11... | collective-permute-start | bytes 589832 | tf_op jit(solution)/shard_map/ppermute | solution.py:284
  27.6 1.4 %collective-permute-start.5 = (bf16[768,128]{1,0:T(8,128)(2,1)S(1)}, bf16[768,128]{1,0:T(8,128)(2,1)S(1)}, u32[]{:S(2)}, u32[]{:S(2)}) collective-permute-start(bf16[768,128]{1,0:T(8,128)(2,1)S(1)} %collective-permute-done.4.rest_2_), channel_id=1, source_target_pairs={{0,1},{1,0},{2,3},{3,2},{4,5},{5,4},{6,7},{7,6},{8,9},{9,8},{10,11... | collective-permute-start | bytes 589832 | tf_op jit(solution)/shard_map/ppermute | solution.py:284

commit v4 on v3

--- a/solution.py
+++ b/solution.py
@@ -30,50 +30,36 @@
     return head % 2 == 0
 
 
-def project_kernel(mo, fo, x_hbm, w_hbm, qkv_ref, kvp_ref, qp_ref, x_ref, w_ref, scr, x_sem, w_sem):
+def project_kernel(mo_hbm, fo_hbm, x_hbm, w_hbm, kv_ref, kvp_ref, mo, fo, x_ref, w_ref, scr, sems):
     rows = x_ref.shape[0]
     mid, far = rows // R1, rows // R2
     per = mid + far
-    pieces, piece = x_sem.shape[0], rows // x_sem.shape[0]
-    w_pieces, w_piece = w_sem.shape[1], w_ref.shape[1] // w_sem.shape[1]
-
-    def w_copy(i, j):
-        at = pl.ds(j * w_piece, w_piece)
-        return pltpu.make_async_copy(w_hbm.at[i, at], w_ref.at[i, at], w_sem.at[i, j])
-
-    def x_copy(i):
-        at = pl.ds(i * piece, piece)
-        return pltpu.make_async_copy(x_hbm.at[at], x_ref.at[at], x_sem.at[i])
-
-    copies = [w_copy(i, j) for i in range(3) for j in range(w_pieces)]
-    copies += [x_copy(i) for i in range(pieces)]
+    half = rows // 2
+    moves = [(w_hbm.at[1], w_ref.at[0]), (w_hbm.at[2], w_ref.at[1])]
+    moves += [(x_hbm.at[pl.ds(i * half, half)], x_ref.at[pl.ds(i * half, half)]) for i in range(2)]
+    moves += [(mo_hbm, mo), (fo_hbm, fo)]
+    copies = [pltpu.make_async_copy(*m, sems.at[i]) for i, m in enumerate(moves)]
     for copy in copies:
         copy.start()
-    for copy in copies:
-        copy.wait()
-    q = [w_ref[0, h * HALF : (h + 1) * HALF] for h in range(3)]
-    k = [w_ref[1, h * HALF : (h + 1) * HALF] for h in range(3)]
-    v = [w_ref[2, h * HALF : (h + 1) * HALF] for h in range(3)]
-    w = jnp.concatenate([v[0], k[0], k[1], v[1], v[2], k[2], q[1], q[0], q[2], q[2]], axis=0)
-    step = rows // 2
-    for first in range(0, rows, step):
-        at = slice(first, first + step)
+    copies[0].wait()
+    copies[1].wait()
+    k = [w_ref[0, h * HALF : (h + 1) * HALF] for h in range(3)]
+    v = [w_ref[1, h * HALF : (h + 1) * HALF] for h in range(3)]
+    w = jnp.concatenate([v[0], k[0], k[1], v[1], v[2], k[2]], axis=0)
+    for i in range(2):
+        copies[2 + i].wait()
+        at = slice(i * half, (i + 1) * half)
         y = lax.dot_general(x_ref[at], w, NT, preferred_element_type=f32).astype(bf16)
-        qkv_ref[at] = y
-        for i in range(5):
-            scr[i, at] = y[:, i * LANES : (i + 1) * LANES].astype(f32)
+        kv_ref[at] = y
+        for h in range(3):
+            scr[h, at] = y[:, h * LANES : (h + 1) * LANES].astype(f32)
+    copies[4].wait()
+    copies[5].wait()
     for h in range(3):
-        asked = 3 + h // 2
-        low = lane_half((mid, LANES))
-        keep = jnp.logical_not(low) if acc_low(h) else low
         mid_rows = pl.ds(mo[h], mid, stride=R1)
         far_rows = pl.ds(fo[h], far, stride=R2)
         kvp_ref[h * per : h * per + mid] = scr[h, mid_rows].astype(bf16)
         kvp_ref[h * per + mid : (h + 1) * per] = scr[h, far_rows].astype(bf16)
-        qp_ref[h * per : h * per + mid] = jnp.where(keep, scr[asked, mid_rows], 0.0).astype(bf16)
-        qp_ref[h * per + mid : (h + 1) * per] = jnp.where(
-            keep[:far], scr[asked, far_rows], 0.0
-        ).astype(bf16)
 
 
 def scores(queries, keys_values):
@@ -109,27 +95,54 @@
 
 
 def near_kernel(
-    factor, mo, fo, qkv_ref, gain_ref, bias_ref, near_ref, am_ref, pk_ref, gb_ref, am_scr, pk_scr
+    factor,
+    mo,
+    fo,
+    w_hbm,
+    kv_ref,
+    x_ref,
+    gain_ref,
+    bias_ref,
+    near_ref,
+    am_ref,
+    pk_ref,
+    qp_ref,
+    gb_ref,
+    am_scr,
+    pk_scr,
+    q_scr,
+    q_ref,
+    w_ref,
+    sem,
 ):
+    copy = pltpu.make_async_copy(w_hbm.at[0], w_ref, sem)
+    copy.start()
     gb_ref[0:1] = gain_ref[...]
     gb_ref[1:2] = bias_ref[...]
-    rows = qkv_ref.shape[0]
+    rows = kv_ref.shape[0]
     mid, far = rows // R1, rows // R2
     per = mid + far
     low = lane_half((SEG0, LANES))
     blocks = rows // SEG0
     units = [(b, h) for b in range(blocks) for h in range(3)]
+    copy.wait()
+    q = [w_ref[h * HALF : (h + 1) * HALF] for h in range(3)]
+    w = jnp.concatenate([q[1], q[0], q[2], q[2]], axis=0)
+    y = lax.dot_general(x_ref[...], w, NT, preferred_element_type=f32).astype(bf16)
+    q_ref[...] = y
+    for i in range(2):
+        q_scr[i] = y[:, i * LANES : (i + 1) * LANES].astype(f32)
 
     def rows_of(b):
         return slice(b * SEG0, (b + 1) * SEG0)
 
     def kv(b, h):
-        return qkv_ref[rows_of(b), h * LANES : (h + 1) * LANES]
+        return kv_ref[rows_of(b), h * LANES : (h + 1) * LANES]
 
     def ask(b, h):
         keep = jnp.logical_not(low) if acc_low(h) else low
-        first = (3 + h // 2) * LANES
-        q = qkv_ref[rows_of(b), first : first + LANES]
+        first = h // 2 * LANES
+        q = q_ref[rows_of(b), first : first + LANES]
         return scores(jnp.where(keep, q, jnp.zeros((), bf16)), kv(b, h))
 
     s = {u: ask(*u) for u in units[:3]}
@@ -151,6 +164,10 @@
         far_rows = pl.ds(fo[h], far, stride=R2)
         am_ref[own], am_ref[own_far] = am_scr[h, mid_rows], am_scr[h, far_rows]
         pk_ref[own], pk_ref[own_far] = pk_scr[h, mid_rows], pk_scr[h, far_rows]
+        keep = lane_half((mid, LANES))
+        keep = jnp.logical_not(keep) if acc_low(h) else keep
+        for at, picked, kept in ((own, mid_rows, keep), (own_far, far_rows, keep[:far])):
+            qp_ref[at] = jnp.where(kept, q_scr[h // 2, picked], 0.0).astype(bf16)
 
 
 def merge_kernel(factor, mid_n, far_n, mo, fo, near_ref, qp_ref, am_ref, pk_ref, *rest):
@@ -288,26 +305,27 @@
 
     two_step = head_count == 4
 
-    qkv, kvp, qp = call(
+    def pinned(array):
+        return pltpu.with_memory_space_constraint(array, pltpu.HBM)
+
+    w_rows = pinned(jnp.swapaxes(w_qkv, 1, 2))
+    kv, kvp = call(
         project_kernel,
-        (
-            shape((rows, 5 * LANES), bf16),
-            shape((3 * per, LANES), bf16),
-            shape((3 * per, LANES), bf16),
-        ),
+        (shape((rows, 3 * LANES), bf16), shape((3 * per, LANES), bf16)),
         [
+            pltpu.SMEM((heads_here,), jnp.int32),
+            pltpu.SMEM((heads_here,), jnp.int32),
             pltpu.VMEM((rows, width), bf16),
-            pltpu.VMEM((3, cols, width), bf16),
-            pltpu.VMEM((5, rows, LANES), f32),
-            pltpu.SemaphoreType.DMA((4,)),
-            pltpu.SemaphoreType.DMA((3, 2)),
+            pltpu.VMEM((2, cols, width), bf16),
+            pltpu.VMEM((3, rows, LANES), f32),
+            pltpu.SemaphoreType.DMA((6,)),
         ],
-        (mid_offset, far_offset),
-        (tokens, jnp.swapaxes(w_qkv, 1, 2)),
+        (),
+        (pinned(mid_offset), pinned(far_offset), pinned(tokens), w_rows),
         (),
         "project",
-        2 * rows * width * 3 * cols,
-        56,
+        2 * rows * width * 2 * cols,
+        24,
     )
 
     seq_count = lax.axis_size("seq")
@@ -328,24 +346,32 @@
         fars = [lax.all_gather(split[:, mid:], "seq", axis=1, tiled=True)]
 
     if two_step:
-        across = to(after((w_out, mids[1]))[0], 2)
-        beside = to(after((w_out, mids[1]))[0], 1)
+        across = to(after((w_out, kvp))[0], 2)
+        beside = to(after((w_out, kvp))[0], 1)
         weights = [w_out, beside, across, to(across, 1)]
     else:
         weights = spread(w_out)
 
-    near, am, pk, gb = call(
+    near, am, pk, qp, gb = call(
         partial(near_kernel, factor),
         (
             shape((rows + rows // 2, LANES), f32),
             shape((3 * per, LANES), f32),
             shape((3 * per, LANES), f32),
+            shape((3 * per, LANES), bf16),
             shape((2, cols), f32),
         ),
-        [pltpu.VMEM((3, rows, LANES), f32)] * 2,
+        [
+            pltpu.VMEM((3, rows, LANES), f32),
+            pltpu.VMEM((3, rows, LANES), f32),
+            pltpu.VMEM((2, rows, LANES), f32),
+            pltpu.VMEM((rows, 2 * LANES), bf16),
+            pltpu.VMEM((cols, width), bf16),
+            pltpu.SemaphoreType.DMA(()),
+        ],
         (mid_offset, far_offset),
-        (),
-        (qkv, gain.reshape(1, cols), bias.reshape(1, cols)),
+        (w_rows,),
+        (kv, tokens, gain.reshape(1, cols), bias.reshape(1, cols)),
         "near",
         1 << 29,
         24,

time: 31 us -> 24.7 us (0.80)
  waiting for transfers between devices: 13 us -> 6.07 us
  starting transfers between devices: 7.5 us -> 9.66 us
  local copies, waits for them, and re-layouts: 1.77 us -> 0.67 us
  Pallas kernels: 8.49 us -> 8.08 us
    ppermute x3, waiting for transfers between devices: 6.7 us -> 0.01 us  [local(): lax.ppermute(kvp, 'seq', within(s))]
    ppermute x6, starting transfers between devices: 2.61 us -> 4.14 us  [to(): return lax.ppermute(array, 'head', paths[r])]
    unnamed x18 -> x12, local copies, waits for them, and re-layouts: 1.77 us -> 0.67 us
    ppermute x3, starting transfers between devices: 4.89 us -> 5.52 us  [local(): lax.ppermute(kvp, 'seq', within(s))]
    pallas_call x4, Pallas kernels: 8.49 us -> 8.08 us  [call(): pl.pallas_call(kernel, out_shape=outs, in_specs=[IN_SMEM] * len(scalars)...]
  transfers between devices with their start and end apart: 9 -> 9, of which waited for: 4 -> 2; matrix products, arithmetic and copies ran while one was open for 0% -> 0% of each run, Pallas kernels for 9% -> 17%
where the time goes in v4:
time: 24.7 us; the launch traced here: 24.6 us
  starting transfers between devices  9.66 us (39%)
  Pallas kernels  8.08 us (33%)
  waiting for transfers between devices  6.07 us (25%)
  local copies, waits for them, and re-layouts  0.67 us (3%)
    pallas_call x4, Pallas kernels, call(): pl.pallas_call(kernel, out_shape=outs, in_specs=[IN_SMEM] * len(scalars)...  8.08 us
    ppermute x6, waiting for transfers between devices, to(): return lax.ppermute(array, 'head', paths[r])  6.06 us
    ppermute x3, starting transfers between devices, local(): lax.ppermute(kvp, 'seq', within(s))  5.52 us
    ppermute x6, starting transfers between devices, to(): return lax.ppermute(array, 'head', paths[r])  4.14 us
    unnamed x12, local copies, waits for them, and re-layouts  0.67 us
  transfers between devices with their start and end apart: 9, of which 2 were waited for; matrix products, arithmetic and copies ran while one was open for 0% of the time, Pallas kernels for 17%

profile of v4, /device:TPU:0, one launch (start us, length us, event | category | flops | bytes accessed | tf_op | source)
XLA Modules:
  0.0 24.6 jit_solution(7765114172658425703)
XLA Ops:
  0.0 0.0 copy-start.1
  0.0 0.0 copy-start
  0.0 0.0 copy-start.4
  0.0 0.0 copy-start.5
  0.0 2.2 %project.1 = (bf16[512,384]{1,0:T(8,128)(2,1)S(1)}, bf16[240,128]{1,0:T(8,128)(2,1)S(1)}) custom-call(s32[3]{0:T(128)} %mo.3, s32[3]{0:T(128)} %fo.3, bf16[512,768]{1,0:T(8,128)(2,1)} %x_ref.3, bf16[3,192,768]{2,1,0:T(8,128)(2,1)} %bitcast.7), custom_call_target="tpu_custom_call" | custom-call | flops 301989888 | bytes 4194304 | tf_op jit(solution)/shard_map/project/pallas_call | solution.py:271
  2.2 0.0 copy-done.1
  2.2 3.0 %collective-permute-start.7 = (bf16[192,768]{1,0:T(8,128)(2,1)S(1)}, bf16[192,768]{1,0:T(8,128)(2,1)S(1)}, u32[]{:S(2)}, u32[]{:S(2)}) collective-permute-start(bf16[192,768]{1,0:T(8,128)(2,1)S(1)} %copy-done.1), channel_id=1, source_target_pairs={{0,2},{1,3},{2,0},{3,1},{4,6},{5,7},{6,4},{7,5},{8,10},{9,11},{10,... | collective-permute-start | bytes 884744 | tf_op jit(solution)/shard_map/ppermute | solution.py:301
  5.2 1.6 %collective-permute-start = (bf16[240,128]{1,0:T(8,128)(2,1)S(1)}, bf16[240,128]{1,0:T(8,128)(2,1)S(1)}, u32[]{:S(2)}, u32[]{:S(2)}) collective-permute-start(bf16[240,128]{1,0:T(8,128)(2,1)S(1)} %get-tuple-element.19.rest_0_.rest_4_), channel_id=1, source_target_pairs={{0,4},{4,8},{8,12},{12,0},{1,5},{5,9},{9,13},{13,1},{2,6},{6,10},{... | collective-permute-start | bytes 184328 | tf_op jit(solution)/shard_map/ppermute | solution.py:340
  6.8 2.6 %collective-permute-start.1 = (bf16[240,128]{1,0:T(8,128)(2,1)S(1)}, bf16[240,128]{1,0:T(8,128)(2,1)S(1)}, u32[]{:S(2)}, u32[]{:S(2)}) collective-permute-start(bf16[240,128]{1,0:T(8,128)(2,1)S(1)} %get-tuple-element.19.rest_0_.rest_4_), channel_id=1, source_target_pairs={{0,8},{4,12},{8,0},{12,4},{1,9},{5,13},{9,1},{13,5},{2,10},{6,14},... | collective-permute-start | bytes 184328 | tf_op jit(solution)/shard_map/ppermute | solution.py:340
  9.4 1.4 %collective-permute-start.2 = (bf16[240,128]{1,0:T(8,128)(2,1)S(1)}, bf16[240,128]{1,0:T(8,128)(2,1)S(1)}, u32[]{:S(2)}, u32[]{:S(2)}) collective-permute-start(bf16[240,128]{1,0:T(8,128)(2,1)S(1)} %get-tuple-element.19.rest_0_.rest_4_), channel_id=1, source_target_pairs={{0,12},{4,0},{8,4},{12,8},{1,13},{5,1},{9,5},{13,9},{2,14},{6,2},{... | collective-permute-start | bytes 184328 | tf_op jit(solution)/shard_map/ppermute | solution.py:340
  10.8 0.0 copy-done
  10.8 0.0 copy-done.4
  10.8 0.0 copy-done.5
  10.8 0.6 %copy-done.2 = s32[3]{0:T(128)S(1)} copy-done((s32[3]{0:T(128)S(1)}, s32[3]{0:T(128)}, u32[]{:S(2)}) %copy-start.2) | copy-done | bytes 36
  11.4 0.0 copy-done.3
  11.4 3.1 %near.1 = (f32[768,128]{1,0:T(8,128)S(1)}, f32[240,128]{1,0:T(8,128)S(1)}, f32[240,128]{1,0:T(8,128)S(1)}, bf16[240,128]{1,0:T(8,128)(2,1)S(1)}, f32[2,192]{1,0:T(2,128)S(1)}) custom-call(s32[3]{0:T(128)S(1)} %copy-done.2, s32[3]{0:T(128)S(1)} %copy-done.3, bf16[3,192,768]{2,1,0:T(8,128)(2,1)} %bitcast.8, bf16[512,384]{1,0:T(8,128)(2,1)S(1)} %get-tuple-element.13.kv_ref, ...), custom_call_target="tpu_custom_call" | custom-call | flops 536870912 | bytes 4194304 | tf_op jit(solution)/shard_map/near/pallas_call | solution.py:271
  14.5 0.0 collective-permute-done.rest_1_.rest_5_
  14.5 0.0 collective-permute-done.1.rest_2_.rest_6_
  14.5 0.0 collective-permute-done.2.rest_3_.rest_7_
  14.5 1.1 %merge.1.rest_0_ = bf16[768,128]{1,0:T(8,128)(2,1)S(1)} custom-call(s32[3]{0:T(128)S(1)} %copy-done.2, s32[3]{0:T(128)S(1)} %copy-done.3, f32[768,128]{1,0:T(8,128)S(1)} %get-tuple-element.15.near_ref, bf16[240,128]{1,0:T(8,128)(2,1)S(1)} %get-tuple-element.16.qp_ref, f32[240,128]{1,0:T(8,128)S(1)} %get-tuple-element.17.am_ref, ...), custom_call_target="tpu_custom_call" | custom-call | flops 536870912 | bytes 4194304 | tf_op jit(solution)/shard_map/merge/pallas_call | solution.py:271
  15.6 0.6 %collective-permute-start.4 = (bf16[768,128]{1,0:T(8,128)(2,1)S(1)}, bf16[768,128]{1,0:T(8,128)(2,1)S(1)}, u32[]{:S(2)}, u32[]{:S(2)}) collective-permute-start(bf16[768,128]{1,0:T(8,128)(2,1)S(1)} %merge.1.rest_0_), channel_id=1, source_target_pairs={{0,2},{1,3},{2,0},{3,1},{4,6},{5,7},{6,4},{7,5},{8,10},{9,11},{10,... | collective-permute-start | bytes 589832 | tf_op jit(solution)/shard_map/ppermute | solution.py:301
  16.2 0.0 collective-permute-start.6
  16.2 0.0 collective-permute-done.7.rest_6_
  16.2 0.5 %collective-permute-start.8 = (bf16[192,768]{1,0:T(8,128)(2,1)S(1)}, bf16[192,768]{1,0:T(8,128)(2,1)S(1)}, u32[]{:S(2)}, u32[]{:S(2)}) collective-permute-start(bf16[192,768]{1,0:T(8,128)(2,1)S(1)} %collective-permute-done.7.rest_6_), channel_id=1, source_target_pairs={{0,1},{1,0},{2,3},{3,2},{4,5},{5,4},{6,7},{7,6},{8,9},{9,8},{10,11... | collective-permute-start | bytes 884744 | tf_op jit(solution)/shard_map/ppermute | solution.py:301
  16.7 0.0 collective-permute-start.3
  16.7 4.6 %collective-permute-done.4.rest_2_ = bf16[768,128]{1,0:T(8,128)(2,1)S(1)} collective-permute-done((bf16[768,128]{1,0:T(8,128)(2,1)S(1)}, bf16[768,128]{1,0:T(8,128)(2,1)S(1)}, u32[]{:S(2)}, u32[]{:S(2)}) %collective-permute-start.4) | collective-permute-done | bytes 196640 | tf_op jit(solution)/shard_map/ppermute | solution.py:301
  21.4 0.0 collective-permute-start.5
  21.4 0.0 collective-permute-done.3.rest_1_
  21.4 0.0 collective-permute-done.6.rest_5_
  21.4 1.4 %collective-permute-done.5.rest_3_ = bf16[768,128]{1,0:T(8,128)(2,1)S(1)} collective-permute-done((bf16[768,128]{1,0:T(8,128)(2,1)S(1)}, bf16[768,128]{1,0:T(8,128)(2,1)S(1)}, u32[]{:S(2)}, u32[]{:S(2)}) %collective-permute-start.5) | collective-permute-done | bytes 196640 | tf_op jit(solution)/shard_map/ppermute | solution.py:301
  22.8 0.0 collective-permute-done.8.rest_7_
  22.8 1.8 %output.1 = bf16[192,512]{1,0:T(8,128)(2,1)} custom-call(s32[1]{0:T(128)} %bitcast.place, bf16[512,768]{1,0:T(8,128)(2,1)S(1)} %copy-done, f32[2,192]{1,0:T(2,128)S(1)} %get-tuple-element.14.gb_ref, bf16[768,128]{1,0:T(8,128)(2,1)S(1)} %merge.1.rest_0_, bf16[768,128]{1,0:T(8,128)(2,1)S(1)} %collective-permute-done.3.rest_1_, ...), custom_call_target="tpu_custom_call" | custom-call | flops 603979776 | bytes 4194304 | tf_op jit(solution)/shard_map/output/pallas_call | solution.py:271
  (2 shorter events, 0.0 us)
Async XLA Ops:
  0.0 2.2 %copy-start.1 = (bf16[192,768]{1,0:T(8,128)(2,1)S(1)}, bf16[192,768]{1,0:T(8,128)(2,1)}, u32[]{:S(2)}) copy-start(bf16[192,768]{1,0:T(8,128)(2,1)} %rest_4_.1) | copy-start | bytes 884740
  0.0 10.8 %copy-start = (bf16[512,768]{1,0:T(8,128)(2,1)S(1)}, bf16[512,768]{1,0:T(8,128)(2,1)}, u32[]{:S(2)}) copy-start(bf16[512,768]{1,0:T(8,128)(2,1)} %x_ref.3) | copy-start | bytes 2359300
  0.0 10.8 %copy-start.4 = (f32[192]{0:T(256)S(1)}, f32[192]{0:T(256)}, u32[]{:S(2)}) copy-start(f32[192]{0:T(256)} %param.10) | copy-start | bytes 2308
  0.0 10.8 %copy-start.5 = (f32[192]{0:T(256)S(1)}, f32[192]{0:T(256)}, u32[]{:S(2)}) copy-start(f32[192]{0:T(256)} %param.11) | copy-start | bytes 2308
  2.2 14.0 %collective-permute-start.7 = (bf16[192,768]{1,0:T(8,128)(2,1)S(1)}, bf16[192,768]{1,0:T(8,128)(2,1)S(1)}, u32[]{:S(2)}, u32[]{:S(2)}) collective-permute-start(bf16[192,768]{1,0:T(8,128)(2,1)S(1)} %copy-done.1), channel_id=1, source_target_pairs={{0,2},{1,3},{2,0},{3,1},{4,6},{5,7},{6,4},{7,5},{8,10},{9,11},{10,... | collective-permute-start | bytes 884744 | tf_op jit(solution)/shard_map/ppermute | solution.py:301
  5.2 9.3 %collective-permute-start = (bf16[240,128]{1,0:T(8,128)(2,1)S(1)}, bf16[240,128]{1,0:T(8,128)(2,1)S(1)}, u32[]{:S(2)}, u32[]{:S(2)}) collective-permute-start(bf16[240,128]{1,0:T(8,128)(2,1)S(1)} %get-tuple-element.19.rest_0_.rest_4_), channel_id=1, source_target_pairs={{0,4},{4,8},{8,12},{12,0},{1,5},{5,9},{9,13},{13,1},{2,6},{6,10},{... | collective-permute-start | bytes 184328 | tf_op jit(solution)/shard_map/ppermute | solution.py:340
  6.8 7.7 %collective-permute-start.1 = (bf16[240,128]{1,0:T(8,128)(2,1)S(1)}, bf16[240,128]{1,0:T(8,128)(2,1)S(1)}, u32[]{:S(2)}, u32[]{:S(2)}) collective-permute-start(bf16[240,128]{1,0:T(8,128)(2,1)S(1)} %get-tuple-element.19.rest_0_.rest_4_), channel_id=1, source_target_pairs={{0,8},{4,12},{8,0},{12,4},{1,9},{5,13},{9,1},{13,5},{2,10},{6,14},... | collective-permute-start | bytes 184328 | tf_op jit(solution)/shard_map/ppermute | solution.py:340
  9.4 5.1 %collective-permute-start.2 = (bf16[240,128]{1,0:T(8,128)(2,1)S(1)}, bf16[240,128]{1,0:T(8,128)(2,1)S(1)}, u32[]{:S(2)}, u32[]{:S(2)}) collective-permute-start(bf16[240,128]{1,0:T(8,128)(2,1)S(1)} %get-tuple-element.19.rest_0_.rest_4_), channel_id=1, source_target_pairs={{0,12},{4,0},{8,4},{12,8},{1,13},{5,1},{9,5},{13,9},{2,14},{6,2},{... | collective-permute-start | bytes 184328 | tf_op jit(solution)/shard_map/ppermute | solution.py:340
  10.8 0.7 %copy-start.2 = (s32[3]{0:T(128)S(1)}, s32[3]{0:T(128)}, u32[]{:S(2)}) copy-start(s32[3]{0:T(128)} %mo.3) | copy-start | bytes 40
  10.8 0.7 %copy-start.3 = (s32[3]{0:T(128)S(1)}, s32[3]{0:T(128)}, u32[]{:S(2)}) copy-start(s32[3]{0:T(128)} %fo.3) | copy-start | bytes 40
  15.6 5.7 %collective-permute-start.4 = (bf16[768,128]{1,0:T(8,128)(2,1)S(1)}, bf16[768,128]{1,0:T(8,128)(2,1)S(1)}, u32[]{:S(2)}, u32[]{:S(2)}) collective-permute-start(bf16[768,128]{1,0:T(8,128)(2,1)S(1)} %merge.1.rest_0_), channel_id=1, source_target_pairs={{0,2},{1,3},{2,0},{3,1},{4,6},{5,7},{6,4},{7,5},{8,10},{9,11},{10,... | collective-permute-start | bytes 589832 | tf_op jit(solution)/shard_map/ppermute | solution.py:301
  16.2 5.2 %collective-permute-start.6 = (bf16[192,768]{1,0:T(8,128)(2,1)S(1)}, bf16[192,768]{1,0:T(8,128)(2,1)S(1)}, u32[]{:S(2)}, u32[]{:S(2)}) collective-permute-start(bf16[192,768]{1,0:T(8,128)(2,1)S(1)} %copy-done.1), channel_id=1, source_target_pairs={{0,1},{1,0},{2,3},{3,2},{4,5},{5,4},{6,7},{7,6},{8,9},{9,8},{10,11... | collective-permute-start | bytes 884744 | tf_op jit(solution)/shard_map/ppermute | solution.py:301
  16.2 6.6 %collective-permute-start.8 = (bf16[192,768]{1,0:T(8,128)(2,1)S(1)}, bf16[192,768]{1,0:T(8,128)(2,1)S(1)}, u32[]{:S(2)}, u32[]{:S(2)}) collective-permute-start(bf16[192,768]{1,0:T(8,128)(2,1)S(1)} %collective-permute-done.7.rest_6_), channel_id=1, source_target_pairs={{0,1},{1,0},{2,3},{3,2},{4,5},{5,4},{6,7},{7,6},{8,9},{9,8},{10,11... | collective-permute-start | bytes 884744 | tf_op jit(solution)/shard_map/ppermute | solution.py:301
  16.7 4.6 %collective-permute-start.3 = (bf16[768,128]{1,0:T(8,128)(2,1)S(1)}, bf16[768,128]{1,0:T(8,128)(2,1)S(1)}, u32[]{:S(2)}, u32[]{:S(2)}) collective-permute-start(bf16[768,128]{1,0:T(8,128)(2,1)S(1)} %merge.1.rest_0_), channel_id=1, source_target_pairs={{0,1},{1,0},{2,3},{3,2},{4,5},{5,4},{6,7},{7,6},{8,9},{9,8},{10,11... | collective-permute-start | bytes 589832 | tf_op jit(solution)/shard_map/ppermute | solution.py:301
  21.4 1.4 %collective-permute-start.5 = (bf16[768,128]{1,0:T(8,128)(2,1)S(1)}, bf16[768,128]{1,0:T(8,128)(2,1)S(1)}, u32[]{:S(2)}, u32[]{:S(2)}) collective-permute-start(bf16[768,128]{1,0:T(8,128)(2,1)S(1)} %collective-permute-done.4.rest_2_), channel_id=1, source_target_pairs={{0,1},{1,0},{2,3},{3,2},{4,5},{5,4},{6,7},{7,6},{8,9},{9,8},{10,11... | collective-permute-start | bytes 589832 | tf_op jit(solution)/shard_map/ppermute | solution.py:301

commit v5 on v4

--- a/solution.py
+++ b/solution.py
@@ -30,14 +30,16 @@
     return head % 2 == 0
 
 
-def project_kernel(mo_hbm, fo_hbm, x_hbm, w_hbm, kv_ref, kvp_ref, mo, fo, x_ref, w_ref, scr, sems):
+def project_kernel(
+    mo_hbm, fo_hbm, x_hbm, w_hbm, kv_ref, kvp_ref, x_ref, wq_ref, mo, fo, w_ref, scr, sems
+):
     rows = x_ref.shape[0]
     mid, far = rows // R1, rows // R2
     per = mid + far
     half = rows // 2
     moves = [(w_hbm.at[1], w_ref.at[0]), (w_hbm.at[2], w_ref.at[1])]
     moves += [(x_hbm.at[pl.ds(i * half, half)], x_ref.at[pl.ds(i * half, half)]) for i in range(2)]
-    moves += [(mo_hbm, mo), (fo_hbm, fo)]
+    moves += [(mo_hbm, mo), (fo_hbm, fo), (w_hbm.at[0], wq_ref)]
     copies = [pltpu.make_async_copy(*m, sems.at[i]) for i, m in enumerate(moves)]
     for copy in copies:
         copy.start()
@@ -60,6 +62,7 @@
         far_rows = pl.ds(fo[h], far, stride=R2)
         kvp_ref[h * per : h * per + mid] = scr[h, mid_rows].astype(bf16)
         kvp_ref[h * per + mid : (h + 1) * per] = scr[h, far_rows].astype(bf16)
+    copies[6].wait()
 
 
 def scores(queries, keys_values):
@@ -94,13 +97,23 @@
     return jnp.where(low, a, swap(b)) / jnp.where(low, swap(a), b)
 
 
+def tell(mo_hbm, fo_hbm, mo, fo, sems):
+    copies = [
+        pltpu.make_async_copy(mo_hbm, mo, sems.at[0]),
+        pltpu.make_async_copy(fo_hbm, fo, sems.at[1]),
+    ]
+    for copy in copies:
+        copy.start()
+    return copies
+
+
 def near_kernel(
     factor,
-    mo,
-    fo,
-    w_hbm,
+    mo_hbm,
+    fo_hbm,
     kv_ref,
     x_ref,
+    w_ref,
     gain_ref,
     bias_ref,
     near_ref,
@@ -108,15 +121,15 @@
     pk_ref,
     qp_ref,
     gb_ref,
+    mo,
+    fo,
     am_scr,
     pk_scr,
     q_scr,
     q_ref,
-    w_ref,
-    sem,
+    sems,
 ):
-    copy = pltpu.make_async_copy(w_hbm.at[0], w_ref, sem)
-    copy.start()
+    copies = tell(mo_hbm, fo_hbm, mo, fo, sems)
     gb_ref[0:1] = gain_ref[...]
     gb_ref[1:2] = bias_ref[...]
     rows = kv_ref.shape[0]
@@ -125,7 +138,6 @@
     low = lane_half((SEG0, LANES))
     blocks = rows // SEG0
     units = [(b, h) for b in range(blocks) for h in range(3)]
-    copy.wait()
     q = [w_ref[h * HALF : (h + 1) * HALF] for h in range(3)]
     w = jnp.concatenate([q[1], q[0], q[2], q[2]], axis=0)
     y = lax.dot_general(x_ref[...], w, NT, preferred_element_type=f32).astype(bf16)
@@ -158,6 +170,8 @@
         if h == 2:
             near_ref[rows_of(b)] = pair(am.pop((b, 0)), am.pop((b, 1)))
     near_ref[rows:] = fold(am_scr[2])
+    for copy in copies:
+        copy.wait()
     for h in range(3):
         own, own_far = slice(h * per, h * per + mid), slice(h * per + mid, (h + 1) * per)
         mid_rows = pl.ds(mo[h], mid, stride=R1)
@@ -170,9 +184,10 @@
             qp_ref[at] = jnp.where(kept, q_scr[h // 2, picked], 0.0).astype(bf16)
 
 
-def merge_kernel(factor, mid_n, far_n, mo, fo, near_ref, qp_ref, am_ref, pk_ref, *rest):
+def merge_kernel(factor, mid_n, far_n, mo_hbm, fo_hbm, near_ref, qp_ref, am_ref, pk_ref, *rest):
     mids, fars = rest[:mid_n], rest[mid_n : mid_n + far_n]
-    attn_ref, attn_scr, am_scr, pk_scr = rest[mid_n + far_n :]
+    attn_ref, mo, fo, attn_scr, am_scr, pk_scr, sems = rest[mid_n + far_n :]
+    copies = tell(mo_hbm, fo_hbm, mo, fo, sems)
     rows = near_ref.shape[0] * 2 // 3
     attn_scr[...] = near_ref[...]
     per = qp_ref.shape[0] // 3
@@ -204,6 +219,8 @@
             jnp.exp2((near_peak - top) * factor) * near_am
             + jnp.exp2((peak_mid - top) * factor) * am_mid[h]
         )
+    for copy in copies:
+        copy.wait()
     for h in heads:
         shared = pl.ds(fo[h] // R1, far, stride=R2 // R1)
         also = fo[h] % R1 == mo[h]
@@ -226,31 +243,36 @@
     attn_ref[...] = attn_scr[...].astype(bf16)
 
 
+def product(first, half, attns, weights):
+    total = None
+    for attn, weight in zip(attns, weights):
+        third = attn[2 * half :]
+        if first:
+            third = swap(third.astype(f32)).astype(bf16)
+        rows = jnp.concatenate([attn[first : first + half], third[:, :HALF]], axis=1)
+        part = jnp.dot(rows, weight[...], preferred_element_type=f32)
+        total = part if total is None else total + part
+    return total
+
+
+def product_kernel(x_ref, *rest):
+    out_ref, count = rest[-1], len(rest) // 2
+    half = x_ref.shape[0] // 2
+    for first in (0, half):
+        at = slice(first, first + half)
+        part = product(first, half, rest[:count], rest[count : 2 * count])
+        out_ref[at] = x_ref[at].astype(f32) + part
+
+
 def output_kernel(head_count, place, x_ref, gb_ref, *rest):
-    attns, weights = rest[:head_count], rest[head_count : 2 * head_count]
-    out_ref, resid_scr = rest[2 * head_count :]
+    out_ref, resid_scr = rest[-2:]
+    count = len(rest) // 2 - 1
     rows, width = x_ref.shape
     half = rows // 2
     cols = width // head_count
-    low = lane_half((half, LANES))
-    w = jnp.concatenate(
-        [weights[r][:LANES] for r in range(head_count)]
-        + [weights[r][LANES:] for r in range(head_count)],
-        axis=0,
-    )
     for first in (0, half):
         at = slice(first, first + half)
-        tiles = [attns[r][at] for r in range(head_count)]
-        for r in range(0, head_count, 2):
-            even = attns[r][rows:].astype(f32)
-            odd = attns[r + 1][rows:].astype(f32)
-            if first == 0:
-                joined = jnp.where(low, even, swap(odd))
-            else:
-                joined = jnp.where(low, swap(even), odd)
-            tiles.append(joined.astype(bf16))
-        attn = jnp.concatenate(tiles, axis=1)
-        resid = x_ref[at].astype(f32) + jnp.dot(attn, w, preferred_element_type=f32)
+        resid = x_ref[at].astype(f32) + product(first, half, rest[:count], rest[count : 2 * count])
         mean = jnp.sum(resid, axis=1, keepdims=True) / width
         var = jnp.sum(resid * resid, axis=1, keepdims=True) / width - mean * mean
         resid_scr[at] = (resid - mean) * lax.rsqrt(var + epsilon)
@@ -309,19 +331,24 @@
         return pltpu.with_memory_space_constraint(array, pltpu.HBM)
 
     w_rows = pinned(jnp.swapaxes(w_qkv, 1, 2))
-    kv, kvp = call(
+    offsets = (pinned(mid_offset), pinned(far_offset))
+    told = [pltpu.SMEM((heads_here,), jnp.int32)] * 2
+    kv, kvp, x, w_query = call(
         project_kernel,
-        (shape((rows, 3 * LANES), bf16), shape((3 * per, LANES), bf16)),
+        (
+            shape((rows, 3 * LANES), bf16),
+            shape((3 * per, LANES), bf16),
+            shape((rows, width), bf16),
+            shape((cols, width), bf16),
+        ),
         [
-            pltpu.SMEM((heads_here,), jnp.int32),
-            pltpu.SMEM((heads_here,), jnp.int32),
-            pltpu.VMEM((rows, width), bf16),
+            *told,
             pltpu.VMEM((2, cols, width), bf16),
             pltpu.VMEM((3, rows, LANES), f32),
-            pltpu.SemaphoreType.DMA((6,)),
+            pltpu.SemaphoreType.DMA((7,)),
         ],
         (),
-        (pinned(mid_offset), pinned(far_offset), pinned(tokens), w_rows),
+        (*offsets, pinned(tokens), w_rows),
         (),
         "project",
         2 * rows * width * 2 * cols,
@@ -332,17 +359,20 @@
     mid_devs = min(8, seq_count)
 
     def within(step):
-        return [
-            (i, i // mid_devs * mid_devs + (i + step) % mid_devs) for i in range(seq_count)
-        ]
+        def partner(i):
+            if mid_devs & (mid_devs - 1) == 0:
+                return i % mid_devs ^ step
+            return (i + step) % mid_devs
+
+        return [(i, i // mid_devs * mid_devs + partner(i)) for i in range(seq_count)]
 
     if mid_devs == seq_count:
-        mids = [kvp] + [lax.ppermute(kvp, "seq", within(s)) for s in range(1, mid_devs)]
+        mids = [kvp] + [lax.ppermute(kvp, "seq", within(s)) for s in range(mid_devs - 1, 0, -1)]
         fars = None
     else:
         split = kvp.reshape(3, per, LANES)
         piece = split[:, :mid]
-        mids = [piece] + [lax.ppermute(piece, "seq", within(s)) for s in range(1, mid_devs)]
+        mids = [piece] + [lax.ppermute(piece, "seq", within(s)) for s in range(mid_devs - 1, 0, -1)]
         fars = [lax.all_gather(split[:, mid:], "seq", axis=1, tiled=True)]
 
     if two_step:
@@ -362,16 +392,16 @@
             shape((2, cols), f32),
         ),
         [
+            *told,
             pltpu.VMEM((3, rows, LANES), f32),
             pltpu.VMEM((3, rows, LANES), f32),
             pltpu.VMEM((2, rows, LANES), f32),
             pltpu.VMEM((rows, 2 * LANES), bf16),
-            pltpu.VMEM((cols, width), bf16),
-            pltpu.SemaphoreType.DMA(()),
+            pltpu.SemaphoreType.DMA((2,)),
         ],
-        (mid_offset, far_offset),
-        (w_rows,),
-        (kv, tokens, gain.reshape(1, cols), bias.reshape(1, cols)),
+        (),
+        offsets,
+        (kv, x, w_query, gain.reshape(1, cols), bias.reshape(1, cols)),
         "near",
         1 << 29,
         24,
@@ -379,31 +409,52 @@
     attn = call(
         partial(merge_kernel, factor, len(mids), len(fars or mids)),
         shape((rows + rows // 2, LANES), bf16),
-        [pltpu.VMEM((rows + rows // 2, LANES), f32)] + [pltpu.VMEM((3, mid, LANES), f32)] * 2,
-        (mid_offset, far_offset),
+        [
+            *told,
+            pltpu.VMEM((rows + rows // 2, LANES), f32),
+            pltpu.VMEM((3, mid, LANES), f32),
+            pltpu.VMEM((3, mid, LANES), f32),
+            pltpu.SemaphoreType.DMA((2,)),
+        ],
         (),
+        offsets,
         (near, qp, am, pk, *mids, *(fars or mids)),
         "merge",
         1 << 29,
         24,
     )
+    def add(base, *which):
+        return call(
+            product_kernel,
+            shape((rows, width), f32),
+            [],
+            (),
+            (),
+            (base, *(attns[i] for i in which), *(weights[i] for i in which)),
+            "product",
+            len(which) * 2 * rows * cols * width,
+            24,
+        )
+
+    resid = x
     if two_step:
-        attn_across = to(attn, 2)
-        attns = [attn, to(attn, 1), attn_across, to(attn_across, 1)]
+        attns = [attn, to(attn, 1), to(attn, 2)]
+        resid = add(resid, 0, 1)
+        resid, attns[2] = after((resid, attns[2]))
+        attns.append(to(attns[2], 1))
+        resid = add(resid, 2)
     else:
         attns = spread(attn)
-
+    left = slice(3, None) if two_step else slice(None)
     out = call(
         partial(output_kernel, head_count),
         shape((cols, rows), bf16),
-        [
-            pltpu.VMEM((rows, width), f32),
-        ],
+        [pltpu.VMEM((rows, width), f32)],
         (lax.axis_index("head").reshape(1),),
         (),
-        (tokens, gb, *attns, *weights),
+        (resid, gb, *attns[left], *weights[left]),
         "output",
-        2 * rows * width * width,
+        2 * rows * width * cols,
         24,
     )
     return out.T

time: 24.7 us -> 25.2 us (1.020)
  waiting for transfers between devices: 6.07 us -> 9.75 us
  starting transfers between devices: 9.66 us -> 8.18 us
  Pallas kernels: 8.08 us -> 7.07 us
  local copies, waits for them, and re-layouts: 0.67 us -> 0.01 us
    ppermute x3, waiting for transfers between devices: 0.01 us -> 2.67 us  [local(): lax.ppermute(kvp, 'seq', within(s))]
    ppermute x3, starting transfers between devices: 5.52 us -> 4.39 us  [local(): lax.ppermute(kvp, 'seq', within(s))]
    ppermute x6, waiting for transfers between devices: 6.06 us -> 7.08 us  [to(): return lax.ppermute(array, 'head', paths[r])]
    pallas_call x4 -> x6, Pallas kernels: 8.08 us -> 7.07 us  [call(): pl.pallas_call(kernel, out_shape=outs, in_specs=[IN_SMEM] * len(scalars)...]
    unnamed x12 -> x6, local copies, waits for them, and re-layouts: 0.67 us -> 0.01 us
    ppermute x6, starting transfers between devices: 4.14 us -> 3.8 us  [to(): return lax.ppermute(array, 'head', paths[r])]
  transfers between devices with their start and end apart: 9 -> 9, of which waited for: 2 -> 5; matrix products, arithmetic and copies ran while one was open for 0% -> 0% of each run, Pallas kernels for 17% -> 14%
where the time goes in v5:
time: 25.2 us; the launch traced here: 25.1 us
  waiting for transfers between devices  9.75 us (39%)
  starting transfers between devices  8.18 us (32%)
  Pallas kernels  7.07 us (28%)
    ppermute x6, waiting for transfers between devices, to(): return lax.ppermute(array, 'head', paths[r])  7.08 us
    pallas_call x6, Pallas kernels, call(): pl.pallas_call(kernel, out_shape=outs, in_specs=[IN_SMEM] * len(scalars)...  7.07 us
    ppermute x3, starting transfers between devices, local(): lax.ppermute(kvp, 'seq', within(s))  4.39 us
    ppermute x6, starting transfers between devices, to(): return lax.ppermute(array, 'head', paths[r])  3.8 us
    ppermute x3, waiting for transfers between devices, local(): lax.ppermute(kvp, 'seq', within(s))  2.67 us
  transfers between devices with their start and end apart: 9, of which 5 were waited for; matrix products, arithmetic and copies ran while one was open for 0% of the time, Pallas kernels for 14%

profile of v5, /device:TPU:0, one launch (start us, length us, event | category | flops | bytes accessed | tf_op | source)
XLA Modules:
  0.0 25.1 jit_solution(13207454617080753328)
XLA Ops:
  0.0 0.0 copy-start
  0.0 0.0 copy-start.1
  0.0 0.0 copy-start.2
  0.0 2.2 %project.1 = (bf16[512,384]{1,0:T(8,128)(2,1)S(1)}, bf16[240,128]{1,0:T(8,128)(2,1)S(1)}, bf16[512,768]{1,0:T(8,128)(2,1)S(1)}, bf16[192,768]{1,0:T(8,128)(2,1)S(1)}) custom-call(s32[3]{0:T(128)} %mo_hbm.5, s32[3]{0:T(128)} %fo_hbm.5, bf16[512,768]{1,0:T(8,128)(2,1)} %x_hbm.1, bf16[3,192,768]{2,1,0:T(8,128)(2,1)} %bitcast.7), custom_call_target="tpu_custom_call" | custom-call | flops 301989888 | bytes 4194304 | tf_op jit(solution)/shard_map/project/pallas_call | solution.py:293
  2.2 0.0 copy-done
  2.2 3.0 %collective-permute-start.6 = (bf16[192,768]{1,0:T(8,128)(2,1)S(1)}, bf16[192,768]{1,0:T(8,128)(2,1)S(1)}, u32[]{:S(2)}, u32[]{:S(2)}) collective-permute-start(bf16[192,768]{1,0:T(8,128)(2,1)S(1)} %copy-done), channel_id=1, source_target_pairs={{0,2},{1,3},{2,0},{3,1},{4,6},{5,7},{6,4},{7,5},{8,10},{9,11},{10,... | collective-permute-start | bytes 884744 | tf_op jit(solution)/shard_map/ppermute | solution.py:323
  5.2 3.6 %collective-permute-start = (bf16[240,128]{1,0:T(8,128)(2,1)S(1)}, bf16[240,128]{1,0:T(8,128)(2,1)S(1)}, u32[]{:S(2)}, u32[]{:S(2)}) collective-permute-start(bf16[240,128]{1,0:T(8,128)(2,1)S(1)} %get-tuple-element.24.rest_0_.rest_4_), channel_id=1, source_target_pairs={{0,12},{4,8},{8,4},{12,0},{1,13},{5,9},{9,5},{13,1},{2,14},{6,10},... | collective-permute-start | bytes 184328 | tf_op jit(solution)/shard_map/ppermute | solution.py:370
  8.8 0.0 collective-permute-start.1
  8.8 0.8 %collective-permute-start.2 = (bf16[240,128]{1,0:T(8,128)(2,1)S(1)}, bf16[240,128]{1,0:T(8,128)(2,1)S(1)}, u32[]{:S(2)}, u32[]{:S(2)}) collective-permute-start(bf16[240,128]{1,0:T(8,128)(2,1)S(1)} %get-tuple-element.24.rest_0_.rest_4_), channel_id=1, source_target_pairs={{0,4},{4,0},{8,12},{12,8},{1,5},{5,1},{9,13},{13,9},{2,6},{6,2},{1... | collective-permute-start | bytes 184328 | tf_op jit(solution)/shard_map/ppermute | solution.py:370
  9.6 0.0 collective-permute-start.4
  9.6 0.0 copy-done.1
  9.6 0.0 copy-done.2
  9.6 1.7 %near.1 = (f32[768,128]{1,0:T(8,128)S(1)}, f32[240,128]{1,0:T(8,128)S(1)}, f32[240,128]{1,0:T(8,128)S(1)}, bf16[240,128]{1,0:T(8,128)(2,1)S(1)}, f32[2,192]{1,0:T(2,128)S(1)}) custom-call(s32[3]{0:T(128)} %mo_hbm.5, s32[3]{0:T(128)} %fo_hbm.5, bf16[512,384]{1,0:T(8,128)(2,1)S(1)} %get-tuple-element.18.kv_ref, bf16[512,768]{1,0:T(8,128)(2,1)S(1)} %get-tuple-element.17.x_ref, ...), custom_call_target="tpu_custom_call" | custom-call | flops 536870912 | bytes 4194304 | tf_op jit(solution)/shard_map/near/pallas_call | solution.py:293
  11.3 0.6 %collective-permute-done.rest_1_.rest_5_ = bf16[240,128]{1,0:T(8,128)(2,1)S(1)} collective-permute-done((bf16[240,128]{1,0:T(8,128)(2,1)S(1)}, bf16[240,128]{1,0:T(8,128)(2,1)S(1)}, u32[]{:S(2)}, u32[]{:S(2)}) %collective-permute-start) | collective-permute-done | bytes 61472 | tf_op jit(solution)/shard_map/ppermute | solution.py:370
  11.9 2.1 %collective-permute-done.1.rest_2_.rest_6_ = bf16[240,128]{1,0:T(8,128)(2,1)S(1)} collective-permute-done((bf16[240,128]{1,0:T(8,128)(2,1)S(1)}, bf16[240,128]{1,0:T(8,128)(2,1)S(1)}, u32[]{:S(2)}, u32[]{:S(2)}) %collective-permute-start.1) | collective-permute-done | bytes 61472 | tf_op jit(solution)/shard_map/ppermute | solution.py:370
  14.0 0.0 collective-permute-done.2.rest_3_.rest_7_
  14.0 0.8 %merge.1.rest_0_ = bf16[768,128]{1,0:T(8,128)(2,1)S(1)} custom-call(s32[3]{0:T(128)} %mo_hbm.5, s32[3]{0:T(128)} %fo_hbm.5, f32[768,128]{1,0:T(8,128)S(1)} %get-tuple-element.20.near_ref, bf16[240,128]{1,0:T(8,128)(2,1)S(1)} %get-tuple-element.21.qp_ref, f32[240,128]{1,0:T(8,128)S(1)} %get-tuple-element.22.am_ref, f32[240,128]{1,0:T(8,128)S(1)} %get-tuple-element.23.pk_ref, ...), custom_call_target="tpu_custom_call" | custom-call | flops 536870912 | bytes 4194304 | tf_op jit(solution)/shard_map/merge/pallas_call | solution.py:293
  14.8 0.1 collective-permute-start.3
  14.9 0.6 %collective-permute-start.5 = (bf16[768,128]{1,0:T(8,128)(2,1)S(1)}, bf16[768,128]{1,0:T(8,128)(2,1)S(1)}, u32[]{:S(2)}, u32[]{:S(2)}) collective-permute-start(bf16[768,128]{1,0:T(8,128)(2,1)S(1)} %merge.1.rest_0_), channel_id=1, source_target_pairs={{0,2},{1,3},{2,0},{3,1},{4,6},{5,7},{6,4},{7,5},{8,10},{9,11},{10,... | collective-permute-start | bytes 589832 | tf_op jit(solution)/shard_map/ppermute | solution.py:323
  15.5 0.0 collective-permute-done.6.rest_1_
  15.5 0.2 collective-permute-start.8
  15.6 0.7 %collective-permute-done.3.rest_1_ = bf16[768,128]{1,0:T(8,128)(2,1)S(1)} collective-permute-done((bf16[768,128]{1,0:T(8,128)(2,1)S(1)}, bf16[768,128]{1,0:T(8,128)(2,1)S(1)}, u32[]{:S(2)}, u32[]{:S(2)}) %collective-permute-start.3) | collective-permute-done | bytes 196640 | tf_op jit(solution)/shard_map/ppermute | solution.py:323
  16.3 0.0 collective-permute-done.4.rest_3_
  16.3 0.6 %product.2.x_ref = f32[512,768]{1,0:T(8,128)S(1)} custom-call(bf16[512,768]{1,0:T(8,128)(2,1)S(1)} %get-tuple-element.17.x_ref, bf16[768,128]{1,0:T(8,128)(2,1)S(1)} %merge.1.rest_0_, bf16[768,128]{1,0:T(8,128)(2,1)S(1)} %collective-permute-done.3.rest_1_, bf16[192,768]{1,0:T(8,128)(2,1)S(1)} %copy-done, bf16[192,768]{1,0:T(8,128)(2,1)S(1)} %collective-permute-done.4.rest_3_), custom_call_target="tpu_custom_call" | custom-call | flops 301989888 | bytes 4194304 | tf_op jit(solution)/shard_map/product/pallas_call | solution.py:293
  16.9 5.3 %collective-permute-done.5.rest_0_ = bf16[768,128]{1,0:T(8,128)(2,1)S(1)} collective-permute-done((bf16[768,128]{1,0:T(8,128)(2,1)S(1)}, bf16[768,128]{1,0:T(8,128)(2,1)S(1)}, u32[]{:S(2)}, u32[]{:S(2)}) %collective-permute-start.5) | collective-permute-done | bytes 196640 | tf_op jit(solution)/shard_map/ppermute | solution.py:323
  22.2 0.0 collective-permute-start.7
  22.2 0.4 %product.3.x_ref = f32[512,768]{1,0:T(8,128)S(1)} custom-call(f32[512,768]{1,0:T(8,128)S(1)} %product.2.x_ref, bf16[768,128]{1,0:T(8,128)(2,1)S(1)} %collective-permute-done.5.rest_0_, bf16[192,768]{1,0:T(8,128)(2,1)S(1)} %collective-permute-done.6.rest_1_), custom_call_target="tpu_custom_call" | custom-call | flops 150994944 | bytes 4194304 | tf_op jit(solution)/shard_map/product/pallas_call | solution.py:293
  22.6 1.1 %collective-permute-done.7.rest_0_ = bf16[768,128]{1,0:T(8,128)(2,1)S(1)} collective-permute-done((bf16[768,128]{1,0:T(8,128)(2,1)S(1)}, bf16[768,128]{1,0:T(8,128)(2,1)S(1)}, u32[]{:S(2)}, u32[]{:S(2)}) %collective-permute-start.7) | collective-permute-done | bytes 196640 | tf_op jit(solution)/shard_map/ppermute | solution.py:323
  23.7 0.0 collective-permute-done.8.rest_1_
  23.7 1.4 %output.1 = bf16[192,512]{1,0:T(8,128)(2,1)} custom-call(s32[1]{0:T(128)} %bitcast.place, f32[512,768]{1,0:T(8,128)S(1)} %product.3.x_ref, f32[2,192]{1,0:T(2,128)S(1)} %get-tuple-element.28.gb_ref, bf16[768,128]{1,0:T(8,128)(2,1)S(1)} %collective-permute-done.7.rest_0_, bf16[192,768]{1,0:T(8,128)(2,1)S(1)} %collective-permute-done.8.rest_1_), custom_call_target="tpu_custom_call" | custom-call | flops 150994944 | bytes 4194304 | tf_op jit(solution)/shard_map/output/pallas_call | solution.py:293
Async XLA Ops:
  0.0 2.2 %copy-start = (bf16[192,768]{1,0:T(8,128)(2,1)S(1)}, bf16[192,768]{1,0:T(8,128)(2,1)}, u32[]{:S(2)}) copy-start(bf16[192,768]{1,0:T(8,128)(2,1)} %rest_2_.1) | copy-start | bytes 884740
  0.0 9.6 %copy-start.1 = (f32[192]{0:T(256)S(1)}, f32[192]{0:T(256)}, u32[]{:S(2)}) copy-start(f32[192]{0:T(256)} %param.10) | copy-start | bytes 2308
  0.0 9.6 %copy-start.2 = (f32[192]{0:T(256)S(1)}, f32[192]{0:T(256)}, u32[]{:S(2)}) copy-start(f32[192]{0:T(256)} %param.11) | copy-start | bytes 2308
  2.2 13.3 %collective-permute-start.6 = (bf16[192,768]{1,0:T(8,128)(2,1)S(1)}, bf16[192,768]{1,0:T(8,128)(2,1)S(1)}, u32[]{:S(2)}, u32[]{:S(2)}) collective-permute-start(bf16[192,768]{1,0:T(8,128)(2,1)S(1)} %copy-done), channel_id=1, source_target_pairs={{0,2},{1,3},{2,0},{3,1},{4,6},{5,7},{6,4},{7,5},{8,10},{9,11},{10,... | collective-permute-start | bytes 884744 | tf_op jit(solution)/shard_map/ppermute | solution.py:323
  5.2 6.7 %collective-permute-start = (bf16[240,128]{1,0:T(8,128)(2,1)S(1)}, bf16[240,128]{1,0:T(8,128)(2,1)S(1)}, u32[]{:S(2)}, u32[]{:S(2)}) collective-permute-start(bf16[240,128]{1,0:T(8,128)(2,1)S(1)} %get-tuple-element.24.rest_0_.rest_4_), channel_id=1, source_target_pairs={{0,12},{4,8},{8,4},{12,0},{1,13},{5,9},{9,5},{13,1},{2,14},{6,10},... | collective-permute-start | bytes 184328 | tf_op jit(solution)/shard_map/ppermute | solution.py:370
  8.8 5.2 %collective-permute-start.1 = (bf16[240,128]{1,0:T(8,128)(2,1)S(1)}, bf16[240,128]{1,0:T(8,128)(2,1)S(1)}, u32[]{:S(2)}, u32[]{:S(2)}) collective-permute-start(bf16[240,128]{1,0:T(8,128)(2,1)S(1)} %get-tuple-element.24.rest_0_.rest_4_), channel_id=1, source_target_pairs={{0,8},{4,12},{8,0},{12,4},{1,9},{5,13},{9,1},{13,5},{2,10},{6,14},... | collective-permute-start | bytes 184328 | tf_op jit(solution)/shard_map/ppermute | solution.py:370
  8.8 5.2 %collective-permute-start.2 = (bf16[240,128]{1,0:T(8,128)(2,1)S(1)}, bf16[240,128]{1,0:T(8,128)(2,1)S(1)}, u32[]{:S(2)}, u32[]{:S(2)}) collective-permute-start(bf16[240,128]{1,0:T(8,128)(2,1)S(1)} %get-tuple-element.24.rest_0_.rest_4_), channel_id=1, source_target_pairs={{0,4},{4,0},{8,12},{12,8},{1,5},{5,1},{9,13},{13,9},{2,6},{6,2},{1... | collective-permute-start | bytes 184328 | tf_op jit(solution)/shard_map/ppermute | solution.py:370
  9.6 6.8 %collective-permute-start.4 = (bf16[192,768]{1,0:T(8,128)(2,1)S(1)}, bf16[192,768]{1,0:T(8,128)(2,1)S(1)}, u32[]{:S(2)}, u32[]{:S(2)}) collective-permute-start(bf16[192,768]{1,0:T(8,128)(2,1)S(1)} %copy-done), channel_id=1, source_target_pairs={{0,1},{1,0},{2,3},{3,2},{4,5},{5,4},{6,7},{7,6},{8,9},{9,8},{10,11... | collective-permute-start | bytes 884744 | tf_op jit(solution)/shard_map/ppermute | solution.py:323
  14.8 1.5 %collective-permute-start.3 = (bf16[768,128]{1,0:T(8,128)(2,1)S(1)}, bf16[768,128]{1,0:T(8,128)(2,1)S(1)}, u32[]{:S(2)}, u32[]{:S(2)}) collective-permute-start(bf16[768,128]{1,0:T(8,128)(2,1)S(1)} %merge.1.rest_0_), channel_id=1, source_target_pairs={{0,1},{1,0},{2,3},{3,2},{4,5},{5,4},{6,7},{7,6},{8,9},{9,8},{10,11... | collective-permute-start | bytes 589832 | tf_op jit(solution)/shard_map/ppermute | solution.py:323
  14.9 7.3 %collective-permute-start.5 = (bf16[768,128]{1,0:T(8,128)(2,1)S(1)}, bf16[768,128]{1,0:T(8,128)(2,1)S(1)}, u32[]{:S(2)}, u32[]{:S(2)}) collective-permute-start(bf16[768,128]{1,0:T(8,128)(2,1)S(1)} %merge.1.rest_0_), channel_id=1, source_target_pairs={{0,2},{1,3},{2,0},{3,1},{4,6},{5,7},{6,4},{7,5},{8,10},{9,11},{10,... | collective-permute-start | bytes 589832 | tf_op jit(solution)/shard_map/ppermute | solution.py:323
  15.5 8.2 %collective-permute-start.8 = (bf16[192,768]{1,0:T(8,128)(2,1)S(1)}, bf16[192,768]{1,0:T(8,128)(2,1)S(1)}, u32[]{:S(2)}, u32[]{:S(2)}) collective-permute-start(bf16[192,768]{1,0:T(8,128)(2,1)S(1)} %collective-permute-done.6.rest_1_), channel_id=1, source_target_pairs={{0,1},{1,0},{2,3},{3,2},{4,5},{5,4},{6,7},{7,6},{8,9},{9,8},{10,11... | collective-permute-start | bytes 884744 | tf_op jit(solution)/shard_map/ppermute | solution.py:323
  22.2 1.4 %collective-permute-start.7 = (bf16[768,128]{1,0:T(8,128)(2,1)S(1)}, bf16[768,128]{1,0:T(8,128)(2,1)S(1)}, u32[]{:S(2)}, u32[]{:S(2)}) collective-permute-start(bf16[768,128]{1,0:T(8,128)(2,1)S(1)} %collective-permute-done.5.rest_0_), channel_id=1, source_target_pairs={{0,1},{1,0},{2,3},{3,2},{4,5},{5,4},{6,7},{7,6},{8,9},{9,8},{10,11... | collective-permute-start | bytes 589832 | tf_op jit(solution)/shard_map/ppermute | solution.py:323

commit v6 on v5

--- a/solution.py
+++ b/solution.py
@@ -360,24 +360,24 @@
 
     def within(step):
         def partner(i):
-            if mid_devs & (mid_devs - 1) == 0:
+            if False:
                 return i % mid_devs ^ step
             return (i + step) % mid_devs
 
         return [(i, i // mid_devs * mid_devs + partner(i)) for i in range(seq_count)]
 
     if mid_devs == seq_count:
-        mids = [kvp] + [lax.ppermute(kvp, "seq", within(s)) for s in range(mid_devs - 1, 0, -1)]
+        mids = [kvp] + [lax.ppermute(kvp, "seq", within(s)) for s in range(1, mid_devs)]
         fars = None
     else:
         split = kvp.reshape(3, per, LANES)
         piece = split[:, :mid]
-        mids = [piece] + [lax.ppermute(piece, "seq", within(s)) for s in range(mid_devs - 1, 0, -1)]
+        mids = [piece] + [lax.ppermute(piece, "seq", within(s)) for s in range(1, mid_devs)]
         fars = [lax.all_gather(split[:, mid:], "seq", axis=1, tiled=True)]
 
     if two_step:
-        across = to(after((w_out, kvp))[0], 2)
-        beside = to(after((w_out, kvp))[0], 1)
+        across = to(w_out, 2)
+        beside = to(w_out, 1)
         weights = [w_out, beside, across, to(across, 1)]
     else:
         weights = spread(w_out)
@@ -423,28 +423,25 @@
         1 << 29,
         24,
     )
-    def add(base, *which):
-        return call(
+    if two_step:
+        attn_across = to(attn, 2)
+        attns = [attn, to(attn, 1), attn_across, to(attn_across, 1)]
+    else:
+        attns = spread(attn)
+
+    resid = x
+    for r in ((0, 1), (2,)) if two_step else ():
+        resid = call(
             product_kernel,
             shape((rows, width), f32),
             [],
             (),
             (),
-            (base, *(attns[i] for i in which), *(weights[i] for i in which)),
+            (resid, *(attns[i] for i in r), *(weights[i] for i in r)),
             "product",
-            len(which) * 2 * rows * cols * width,
+            len(r) * 2 * rows * cols * width,
             24,
         )
-
-    resid = x
-    if two_step:
-        attns = [attn, to(attn, 1), to(attn, 2)]
-        resid = add(resid, 0, 1)
-        resid, attns[2] = after((resid, attns[2]))
-        attns.append(to(attns[2], 1))
-        resid = add(resid, 2)
-    else:
-        attns = spread(attn)
     left = slice(3, None) if two_step else slice(None)
     out = call(
         partial(output_kernel, head_count),

time: 25.2 us -> 23.5 us (0.933)
  waiting for transfers between devices: 9.75 us -> 6.58 us
  starting transfers between devices: 8.18 us -> 9.68 us
    ppermute x6, waiting for transfers between devices: 7.08 us -> 5.07 us  [to(): return lax.ppermute(array, 'head', paths[r])]
    ppermute x3, starting transfers between devices: 4.39 us -> 5.58 us  [local(): lax.ppermute(kvp, 'seq', within(s))]
    ppermute x3, waiting for transfers between devices: 2.67 us -> 1.51 us  [local(): lax.ppermute(kvp, 'seq', within(s))]
    ppermute x6, starting transfers between devices: 3.8 us -> 4.1 us  [to(): return lax.ppermute(array, 'head', paths[r])]
  transfers between devices with their start and end apart: 9 -> 9, of which waited for: 5 -> 3; matrix products, arithmetic and copies ran while one was open for 0% -> 0% of each run, Pallas kernels for 14% -> 24%
where the time goes in v6:
time: 23.5 us; the launch traced here: 23.3 us
  starting transfers between devices  9.68 us (41%)
  Pallas kernels  6.98 us (30%)
  waiting for transfers between devices  6.58 us (28%)
    pallas_call x6, Pallas kernels, call(): pl.pallas_call(kernel, out_shape=outs, in_specs=[IN_SMEM] * len(scalars)...  6.98 us
    ppermute x3, starting transfers between devices, local(): lax.ppermute(kvp, 'seq', within(s))  5.58 us
    ppermute x6, waiting for transfers between devices, to(): return lax.ppermute(array, 'head', paths[r])  5.07 us
    ppermute x6, starting transfers between devices, to(): return lax.ppermute(array, 'head', paths[r])  4.1 us
    ppermute x3, waiting for transfers between devices, local(): lax.ppermute(kvp, 'seq', within(s))  1.51 us
  transfers between devices with their start and end apart: 9, of which 3 were waited for; matrix products, arithmetic and copies ran while one was open for 0% of the time, Pallas kernels for 24%

profile of v6, /device:TPU:0, one launch (start us, length us, event | category | flops | bytes accessed | tf_op | source)
XLA Modules:
  0.0 23.3 jit_solution(5196829928365639350)
XLA Ops:
  0.0 0.0 copy-start.1
  0.0 0.0 copy-start.2
  0.0 2.9 %collective-permute-start.6 = (bf16[192,768]{1,0:T(8,128)(2,1)}, bf16[192,768]{1,0:T(8,128)(2,1)S(1)}, u32[]{:S(2)}, u32[]{:S(2)}) collective-permute-start(bf16[192,768]{1,0:T(8,128)(2,1)} %rest_2_.1), channel_id=1, source_target_pairs={{0,2},{1,3},{2,0},{3,1},{4,6},{5,7},{6,4},{7,5},{8,10},{9,11},{10,... | collective-permute-start | bytes 884744 | tf_op jit(solution)/shard_map/ppermute | solution.py:323
  2.9 2.1 %project.1 = (bf16[512,384]{1,0:T(8,128)(2,1)S(1)}, bf16[240,128]{1,0:T(8,128)(2,1)S(1)}, bf16[512,768]{1,0:T(8,128)(2,1)S(1)}, bf16[192,768]{1,0:T(8,128)(2,1)S(1)}) custom-call(s32[3]{0:T(128)} %mo_hbm.5, s32[3]{0:T(128)} %fo_hbm.5, bf16[512,768]{1,0:T(8,128)(2,1)} %x_hbm.1, bf16[3,192,768]{2,1,0:T(8,128)(2,1)} %bitcast.7), custom_call_target="tpu_custom_call" | custom-call | flops 301989888 | bytes 4194304 | tf_op jit(solution)/shard_map/project/pallas_call | solution.py:293
  5.1 1.6 %collective-permute-start = (bf16[240,128]{1,0:T(8,128)(2,1)S(1)}, bf16[240,128]{1,0:T(8,128)(2,1)S(1)}, u32[]{:S(2)}, u32[]{:S(2)}) collective-permute-start(bf16[240,128]{1,0:T(8,128)(2,1)S(1)} %get-tuple-element.21.rest_0_.rest_4_), channel_id=1, source_target_pairs={{0,4},{4,8},{8,12},{12,0},{1,5},{5,9},{9,13},{13,1},{2,6},{6,10},{... | collective-permute-start | bytes 184328 | tf_op jit(solution)/shard_map/ppermute | solution.py:370
  6.7 2.6 %collective-permute-start.1 = (bf16[240,128]{1,0:T(8,128)(2,1)S(1)}, bf16[240,128]{1,0:T(8,128)(2,1)S(1)}, u32[]{:S(2)}, u32[]{:S(2)}) collective-permute-start(bf16[240,128]{1,0:T(8,128)(2,1)S(1)} %get-tuple-element.21.rest_0_.rest_4_), channel_id=1, source_target_pairs={{0,8},{4,12},{8,0},{12,4},{1,9},{5,13},{9,1},{13,5},{2,10},{6,14},... | collective-permute-start | bytes 184328 | tf_op jit(solution)/shard_map/ppermute | solution.py:370
  9.3 1.3 %collective-permute-start.2 = (bf16[240,128]{1,0:T(8,128)(2,1)S(1)}, bf16[240,128]{1,0:T(8,128)(2,1)S(1)}, u32[]{:S(2)}, u32[]{:S(2)}) collective-permute-start(bf16[240,128]{1,0:T(8,128)(2,1)S(1)} %get-tuple-element.21.rest_0_.rest_4_), channel_id=1, source_target_pairs={{0,12},{4,0},{8,4},{12,8},{1,13},{5,1},{9,5},{13,9},{2,14},{6,2},{... | collective-permute-start | bytes 184328 | tf_op jit(solution)/shard_map/ppermute | solution.py:370
  10.6 0.0 copy-done.1
  10.6 0.0 copy-done.2
  10.6 0.0 copy-start
  10.6 1.7 %near.1 = (f32[768,128]{1,0:T(8,128)S(1)}, f32[240,128]{1,0:T(8,128)S(1)}, f32[240,128]{1,0:T(8,128)S(1)}, bf16[240,128]{1,0:T(8,128)(2,1)S(1)}, f32[2,192]{1,0:T(2,128)S(1)}) custom-call(s32[3]{0:T(128)} %mo_hbm.5, s32[3]{0:T(128)} %fo_hbm.5, bf16[512,384]{1,0:T(8,128)(2,1)S(1)} %get-tuple-element.15.kv_ref, bf16[512,768]{1,0:T(8,128)(2,1)S(1)} %get-tuple-element.14.x_ref, ...), custom_call_target="tpu_custom_call" | custom-call | flops 536870912 | bytes 4194304 | tf_op jit(solution)/shard_map/near/pallas_call | solution.py:293
  12.3 0.0 collective-permute-done.rest_1_.rest_5_
  12.4 1.5 %collective-permute-done.1.rest_2_.rest_6_ = bf16[240,128]{1,0:T(8,128)(2,1)S(1)} collective-permute-done((bf16[240,128]{1,0:T(8,128)(2,1)S(1)}, bf16[240,128]{1,0:T(8,128)(2,1)S(1)}, u32[]{:S(2)}, u32[]{:S(2)}) %collective-permute-start.1) | collective-permute-done | bytes 61472 | tf_op jit(solution)/shard_map/ppermute | solution.py:370
  13.9 0.0 collective-permute-done.2.rest_3_.rest_7_
  13.9 0.8 %merge.1.rest_0_ = bf16[768,128]{1,0:T(8,128)(2,1)S(1)} custom-call(s32[3]{0:T(128)} %mo_hbm.5, s32[3]{0:T(128)} %fo_hbm.5, f32[768,128]{1,0:T(8,128)S(1)} %get-tuple-element.17.near_ref, bf16[240,128]{1,0:T(8,128)(2,1)S(1)} %get-tuple-element.18.qp_ref, f32[240,128]{1,0:T(8,128)S(1)} %get-tuple-element.19.am_ref, f32[240,128]{1,0:T(8,128)S(1)} %get-tuple-element.20.pk_ref, ...), custom_call_target="tpu_custom_call" | custom-call | flops 536870912 | bytes 4194304 | tf_op jit(solution)/shard_map/merge/pallas_call | solution.py:293
  14.7 0.6 %collective-permute-start.5 = (bf16[768,128]{1,0:T(8,128)(2,1)S(1)}, bf16[768,128]{1,0:T(8,128)(2,1)S(1)}, u32[]{:S(2)}, u32[]{:S(2)}) collective-permute-start(bf16[768,128]{1,0:T(8,128)(2,1)S(1)} %merge.1.rest_0_), channel_id=1, source_target_pairs={{0,2},{1,3},{2,0},{3,1},{4,6},{5,7},{6,4},{7,5},{8,10},{9,11},{10,... | collective-permute-start | bytes 589832 | tf_op jit(solution)/shard_map/ppermute | solution.py:323
  15.3 0.0 copy-done
  15.3 0.0 collective-permute-start.4
  15.3 0.0 collective-permute-done.6.rest_1_
  15.3 0.5 %collective-permute-start.8 = (bf16[192,768]{1,0:T(8,128)(2,1)S(1)}, bf16[192,768]{1,0:T(8,128)(2,1)S(1)}, u32[]{:S(2)}, u32[]{:S(2)}) collective-permute-start(bf16[192,768]{1,0:T(8,128)(2,1)S(1)} %collective-permute-done.6.rest_1_), channel_id=1, source_target_pairs={{0,1},{1,0},{2,3},{3,2},{4,5},{5,4},{6,7},{7,6},{8,9},{9,8},{10,11... | collective-permute-start | bytes 884744 | tf_op jit(solution)/shard_map/ppermute | solution.py:323
  15.8 0.1 collective-permute-start.3
  15.9 4.6 %collective-permute-done.5.rest_0_ = bf16[768,128]{1,0:T(8,128)(2,1)S(1)} collective-permute-done((bf16[768,128]{1,0:T(8,128)(2,1)S(1)}, bf16[768,128]{1,0:T(8,128)(2,1)S(1)}, u32[]{:S(2)}, u32[]{:S(2)}) %collective-permute-start.5) | collective-permute-done | bytes 196640 | tf_op jit(solution)/shard_map/ppermute | solution.py:323
  20.5 0.0 collective-permute-start.7
  20.5 0.0 collective-permute-done.3.rest_1_
  20.5 0.0 collective-permute-done.4.rest_3_
  20.5 0.6 %product.2.x_ref = f32[512,768]{1,0:T(8,128)S(1)} custom-call(bf16[512,768]{1,0:T(8,128)(2,1)S(1)} %get-tuple-element.14.x_ref, bf16[768,128]{1,0:T(8,128)(2,1)S(1)} %merge.1.rest_0_, bf16[768,128]{1,0:T(8,128)(2,1)S(1)} %collective-permute-done.3.rest_1_, bf16[192,768]{1,0:T(8,128)(2,1)S(1)} %copy-done, bf16[192,768]{1,0:T(8,128)(2,1)S(1)} %collective-permute-done.4.rest_3_), custom_call_target="tpu_custom_call" | custom-call | flops 301989888 | bytes 4194304 | tf_op jit(solution)/shard_map/product/pallas_call | solution.py:293
  21.0 0.4 %product.3.x_ref = f32[512,768]{1,0:T(8,128)S(1)} custom-call(f32[512,768]{1,0:T(8,128)S(1)} %product.2.x_ref, bf16[768,128]{1,0:T(8,128)(2,1)S(1)} %collective-permute-done.5.rest_0_, bf16[192,768]{1,0:T(8,128)(2,1)S(1)} %collective-permute-done.6.rest_1_), custom_call_target="tpu_custom_call" | custom-call | flops 150994944 | bytes 4194304 | tf_op jit(solution)/shard_map/product/pallas_call | solution.py:293
  21.4 0.5 %collective-permute-done.7.rest_0_ = bf16[768,128]{1,0:T(8,128)(2,1)S(1)} collective-permute-done((bf16[768,128]{1,0:T(8,128)(2,1)S(1)}, bf16[768,128]{1,0:T(8,128)(2,1)S(1)}, u32[]{:S(2)}, u32[]{:S(2)}) %collective-permute-start.7) | collective-permute-done | bytes 196640 | tf_op jit(solution)/shard_map/ppermute | solution.py:323
  21.9 0.0 collective-permute-done.8.rest_1_
  21.9 1.4 %output.1 = bf16[192,512]{1,0:T(8,128)(2,1)} custom-call(s32[1]{0:T(128)} %bitcast.place, f32[512,768]{1,0:T(8,128)S(1)} %product.3.x_ref, f32[2,192]{1,0:T(2,128)S(1)} %get-tuple-element.22.gb_ref, bf16[768,128]{1,0:T(8,128)(2,1)S(1)} %collective-permute-done.7.rest_0_, bf16[192,768]{1,0:T(8,128)(2,1)S(1)} %collective-permute-done.8.rest_1_), custom_call_target="tpu_custom_call" | custom-call | flops 150994944 | bytes 4194304 | tf_op jit(solution)/shard_map/output/pallas_call | solution.py:293
Async XLA Ops:
  0.0 10.6 %copy-start.1 = (f32[192]{0:T(256)S(1)}, f32[192]{0:T(256)}, u32[]{:S(2)}) copy-start(f32[192]{0:T(256)} %param.10) | copy-start | bytes 2308
  0.0 10.6 %copy-start.2 = (f32[192]{0:T(256)S(1)}, f32[192]{0:T(256)}, u32[]{:S(2)}) copy-start(f32[192]{0:T(256)} %param.11) | copy-start | bytes 2308
  0.0 15.3 %collective-permute-start.6 = (bf16[192,768]{1,0:T(8,128)(2,1)}, bf16[192,768]{1,0:T(8,128)(2,1)S(1)}, u32[]{:S(2)}, u32[]{:S(2)}) collective-permute-start(bf16[192,768]{1,0:T(8,128)(2,1)} %rest_2_.1), channel_id=1, source_target_pairs={{0,2},{1,3},{2,0},{3,1},{4,6},{5,7},{6,4},{7,5},{8,10},{9,11},{10,... | collective-permute-start | bytes 884744 | tf_op jit(solution)/shard_map/ppermute | solution.py:323
  5.1 7.3 %collective-permute-start = (bf16[240,128]{1,0:T(8,128)(2,1)S(1)}, bf16[240,128]{1,0:T(8,128)(2,1)S(1)}, u32[]{:S(2)}, u32[]{:S(2)}) collective-permute-start(bf16[240,128]{1,0:T(8,128)(2,1)S(1)} %get-tuple-element.21.rest_0_.rest_4_), channel_id=1, source_target_pairs={{0,4},{4,8},{8,12},{12,0},{1,5},{5,9},{9,13},{13,1},{2,6},{6,10},{... | collective-permute-start | bytes 184328 | tf_op jit(solution)/shard_map/ppermute | solution.py:370
  6.7 7.2 %collective-permute-start.1 = (bf16[240,128]{1,0:T(8,128)(2,1)S(1)}, bf16[240,128]{1,0:T(8,128)(2,1)S(1)}, u32[]{:S(2)}, u32[]{:S(2)}) collective-permute-start(bf16[240,128]{1,0:T(8,128)(2,1)S(1)} %get-tuple-element.21.rest_0_.rest_4_), channel_id=1, source_target_pairs={{0,8},{4,12},{8,0},{12,4},{1,9},{5,13},{9,1},{13,5},{2,10},{6,14},... | collective-permute-start | bytes 184328 | tf_op jit(solution)/shard_map/ppermute | solution.py:370
  9.3 4.6 %collective-permute-start.2 = (bf16[240,128]{1,0:T(8,128)(2,1)S(1)}, bf16[240,128]{1,0:T(8,128)(2,1)S(1)}, u32[]{:S(2)}, u32[]{:S(2)}) collective-permute-start(bf16[240,128]{1,0:T(8,128)(2,1)S(1)} %get-tuple-element.21.rest_0_.rest_4_), channel_id=1, source_target_pairs={{0,12},{4,0},{8,4},{12,8},{1,13},{5,1},{9,5},{13,9},{2,14},{6,2},{... | collective-permute-start | bytes 184328 | tf_op jit(solution)/shard_map/ppermute | solution.py:370
  10.6 4.7 %copy-start = (bf16[192,768]{1,0:T(8,128)(2,1)S(1)}, bf16[192,768]{1,0:T(8,128)(2,1)}, u32[]{:S(2)}) copy-start(bf16[192,768]{1,0:T(8,128)(2,1)} %rest_2_.1) | copy-start | bytes 884740
  14.7 5.7 %collective-permute-start.5 = (bf16[768,128]{1,0:T(8,128)(2,1)S(1)}, bf16[768,128]{1,0:T(8,128)(2,1)S(1)}, u32[]{:S(2)}, u32[]{:S(2)}) collective-permute-start(bf16[768,128]{1,0:T(8,128)(2,1)S(1)} %merge.1.rest_0_), channel_id=1, source_target_pairs={{0,2},{1,3},{2,0},{3,1},{4,6},{5,7},{6,4},{7,5},{8,10},{9,11},{10,... | collective-permute-start | bytes 589832 | tf_op jit(solution)/shard_map/ppermute | solution.py:323
  15.3 5.2 %collective-permute-start.4 = (bf16[192,768]{1,0:T(8,128)(2,1)S(1)}, bf16[192,768]{1,0:T(8,128)(2,1)S(1)}, u32[]{:S(2)}, u32[]{:S(2)}) collective-permute-start(bf16[192,768]{1,0:T(8,128)(2,1)S(1)} %copy-done), channel_id=1, source_target_pairs={{0,1},{1,0},{2,3},{3,2},{4,5},{5,4},{6,7},{7,6},{8,9},{9,8},{10,11... | collective-permute-start | bytes 884744 | tf_op jit(solution)/shard_map/ppermute | solution.py:323
  15.3 6.6 %collective-permute-start.8 = (bf16[192,768]{1,0:T(8,128)(2,1)S(1)}, bf16[192,768]{1,0:T(8,128)(2,1)S(1)}, u32[]{:S(2)}, u32[]{:S(2)}) collective-permute-start(bf16[192,768]{1,0:T(8,128)(2,1)S(1)} %collective-permute-done.6.rest_1_), channel_id=1, source_target_pairs={{0,1},{1,0},{2,3},{3,2},{4,5},{5,4},{6,7},{7,6},{8,9},{9,8},{10,11... | collective-permute-start | bytes 884744 | tf_op jit(solution)/shard_map/ppermute | solution.py:323
  15.8 4.6 %collective-permute-start.3 = (bf16[768,128]{1,0:T(8,128)(2,1)S(1)}, bf16[768,128]{1,0:T(8,128)(2,1)S(1)}, u32[]{:S(2)}, u32[]{:S(2)}) collective-permute-start(bf16[768,128]{1,0:T(8,128)(2,1)S(1)} %merge.1.rest_0_), channel_id=1, source_target_pairs={{0,1},{1,0},{2,3},{3,2},{4,5},{5,4},{6,7},{7,6},{8,9},{9,8},{10,11... | collective-permute-start | bytes 589832 | tf_op jit(solution)/shard_map/ppermute | solution.py:323
  20.5 1.4 %collective-permute-start.7 = (bf16[768,128]{1,0:T(8,128)(2,1)S(1)}, bf16[768,128]{1,0:T(8,128)(2,1)S(1)}, u32[]{:S(2)}, u32[]{:S(2)}) collective-permute-start(bf16[768,128]{1,0:T(8,128)(2,1)S(1)} %collective-permute-done.5.rest_0_), channel_id=1, source_target_pairs={{0,1},{1,0},{2,3},{3,2},{4,5},{5,4},{6,7},{7,6},{8,9},{9,8},{10,11... | collective-permute-start | bytes 589832 | tf_op jit(solution)/shard_map/ppermute | solution.py:323

commit v7 on v6

--- a/solution.py
+++ b/solution.py
@@ -31,38 +31,29 @@
 
 
 def project_kernel(
-    mo_hbm, fo_hbm, x_hbm, w_hbm, kv_ref, kvp_ref, x_ref, wq_ref, mo, fo, w_ref, scr, sems
+    mo_hbm, fo_hbm, x_ref, w_ref, lanes_ref, kv_ref, kvp_ref, mo, fo, scr, sems
 ):
     rows = x_ref.shape[0]
     mid, far = rows // R1, rows // R2
     per = mid + far
     half = rows // 2
-    moves = [(w_hbm.at[1], w_ref.at[0]), (w_hbm.at[2], w_ref.at[1])]
-    moves += [(x_hbm.at[pl.ds(i * half, half)], x_ref.at[pl.ds(i * half, half)]) for i in range(2)]
-    moves += [(mo_hbm, mo), (fo_hbm, fo), (w_hbm.at[0], wq_ref)]
-    copies = [pltpu.make_async_copy(*m, sems.at[i]) for i, m in enumerate(moves)]
-    for copy in copies:
-        copy.start()
-    copies[0].wait()
-    copies[1].wait()
-    k = [w_ref[0, h * HALF : (h + 1) * HALF] for h in range(3)]
-    v = [w_ref[1, h * HALF : (h + 1) * HALF] for h in range(3)]
+    copies = tell(mo_hbm, fo_hbm, mo, fo, sems)
+    k = [w_ref[1, h * HALF : (h + 1) * HALF] for h in range(3)]
+    v = [w_ref[2, h * HALF : (h + 1) * HALF] for h in range(3)]
     w = jnp.concatenate([v[0], k[0], k[1], v[1], v[2], k[2]], axis=0)
     for i in range(2):
-        copies[2 + i].wait()
         at = slice(i * half, (i + 1) * half)
         y = lax.dot_general(x_ref[at], w, NT, preferred_element_type=f32).astype(bf16)
         kv_ref[at] = y
         for h in range(3):
             scr[h, at] = y[:, h * LANES : (h + 1) * LANES].astype(f32)
-    copies[4].wait()
-    copies[5].wait()
+    for copy in copies:
+        copy.wait()
     for h in range(3):
         mid_rows = pl.ds(mo[h], mid, stride=R1)
         far_rows = pl.ds(fo[h], far, stride=R2)
         kvp_ref[h * per : h * per + mid] = scr[h, mid_rows].astype(bf16)
         kvp_ref[h * per + mid : (h + 1) * per] = scr[h, far_rows].astype(bf16)
-    copies[6].wait()
 
 
 def scores(queries, keys_values):
@@ -95,6 +86,10 @@
     a, b = x[:half], x[half:]
     low = lane_half(a.shape)
     return jnp.where(low, a, swap(b)) / jnp.where(low, swap(a), b)
+
+
+def lanes_kernel(out_ref):
+    out_ref[...] = lax.broadcasted_iota(jnp.int32, out_ref.shape, 1)
 
 
 def tell(mo_hbm, fo_hbm, mo, fo, sems):
@@ -138,7 +133,7 @@
     low = lane_half((SEG0, LANES))
     blocks = rows // SEG0
     units = [(b, h) for b in range(blocks) for h in range(3)]
-    q = [w_ref[h * HALF : (h + 1) * HALF] for h in range(3)]
+    q = [w_ref[0, h * HALF : (h + 1) * HALF] for h in range(3)]
     w = jnp.concatenate([q[1], q[0], q[2], q[2]], axis=0)
     y = lax.dot_general(x_ref[...], w, NT, preferred_element_type=f32).astype(bf16)
     q_ref[...] = y
@@ -330,26 +325,27 @@
     def pinned(array):
         return pltpu.with_memory_space_constraint(array, pltpu.HBM)
 
-    w_rows = pinned(jnp.swapaxes(w_qkv, 1, 2))
+    x = pltpu.with_memory_space_constraint(tokens, pltpu.VMEM)
+    w_rows = pltpu.with_memory_space_constraint(jnp.swapaxes(w_qkv, 1, 2), pltpu.VMEM)
+    lanes = call(
+        lanes_kernel, shape((8, LANES), jnp.int32), [], (), (), (), "lanes", 460 << 20, 24
+    )
     offsets = (pinned(mid_offset), pinned(far_offset))
     told = [pltpu.SMEM((heads_here,), jnp.int32)] * 2
-    kv, kvp, x, w_query = call(
+    kv, kvp = call(
         project_kernel,
         (
             shape((rows, 3 * LANES), bf16),
             shape((3 * per, LANES), bf16),
-            shape((rows, width), bf16),
-            shape((cols, width), bf16),
         ),
         [
             *told,
-            pltpu.VMEM((2, cols, width), bf16),
             pltpu.VMEM((3, rows, LANES), f32),
-            pltpu.SemaphoreType.DMA((7,)),
+            pltpu.SemaphoreType.DMA((2,)),
         ],
         (),
-        (*offsets, pinned(tokens), w_rows),
-        (),
+        offsets,
+        (x, w_rows, lanes),
         "project",
         2 * rows * width * 2 * cols,
         24,
@@ -376,7 +372,7 @@
         fars = [lax.all_gather(split[:, mid:], "seq", axis=1, tiled=True)]
 
     if two_step:
-        across = to(w_out, 2)
+        across = to(after((w_out, lanes))[0], 2)
         beside = to(w_out, 1)
         weights = [w_out, beside, across, to(across, 1)]
     else:
@@ -401,7 +397,7 @@
         ],
         (),
         offsets,
-        (kv, x, w_query, gain.reshape(1, cols), bias.reshape(1, cols)),
+        (kv, x, w_rows, gain.reshape(1, cols), bias.reshape(1, cols)),
         "near",
         1 << 29,
         24,

time: 23.5 us -> 22.2 us (0.945)
  Pallas kernels: 6.98 us -> 5.65 us
  starting transfers between devices: 9.68 us -> 10.5 us
  waiting for transfers between devices: 6.58 us -> 5.81 us
    pallas_call x6 -> x7, Pallas kernels: 6.98 us -> 5.65 us  [call(): pl.pallas_call(kernel, out_shape=outs, in_specs=[IN_SMEM] * len(scalars)...]
    ppermute x6, starting transfers between devices: 4.1 us -> 4.95 us  [to(): return lax.ppermute(array, 'head', paths[r])]
    ppermute x6, waiting for transfers between devices: 5.07 us -> 4.29 us  [to(): return lax.ppermute(array, 'head', paths[r])]
  transfers between devices with their start and end apart: 9 -> 9, of which waited for: 3 -> 3; matrix products, arithmetic and copies ran while one was open for 0% -> 0% of each run, Pallas kernels for 24% -> 19%
where the time goes in v7:
time: 22.2 us; the launch traced here: 22.1 us
  starting transfers between devices  10.5 us (47%)
  waiting for transfers between devices  5.81 us (26%)
  Pallas kernels  5.65 us (25%)
    pallas_call x7, Pallas kernels, call(): pl.pallas_call(kernel, out_shape=outs, in_specs=[IN_SMEM] * len(scalars)...  5.65 us
    ppermute x3, starting transfers between devices, local(): lax.ppermute(kvp, 'seq', within(s))  5.57 us
    ppermute x6, starting transfers between devices, to(): return lax.ppermute(array, 'head', paths[r])  4.95 us
    ppermute x6, waiting for transfers between devices, to(): return lax.ppermute(array, 'head', paths[r])  4.29 us
    ppermute x3, waiting for transfers between devices, local(): lax.ppermute(kvp, 'seq', within(s))  1.52 us
  transfers between devices with their start and end apart: 9, of which 3 were waited for; matrix products, arithmetic and copies ran while one was open for 0% of the time, Pallas kernels for 19%

profile of v7, /device:TPU:0, one launch (start us, length us, event | category | flops | bytes accessed | tf_op | source)
XLA Modules:
  0.0 22.1 jit_solution(16786468614159992608)
XLA Ops:
  0.0 0.0 copy-start.1
  0.0 0.0 copy-start
  0.0 0.0 copy-start.3
  0.0 3.0 %collective-permute-start.6 = (bf16[192,768]{1,0:T(8,128)(2,1)}, bf16[192,768]{1,0:T(8,128)(2,1)S(1)}, u32[]{:S(2)}, u32[]{:S(2)}) collective-permute-start(bf16[192,768]{1,0:T(8,128)(2,1)} %rest_2_.1), channel_id=1, source_target_pairs={{0,2},{1,3},{2,0},{3,1},{4,6},{5,7},{6,4},{7,5},{8,10},{9,11},{10,... | collective-permute-start | bytes 884744 | tf_op jit(solution)/shard_map/ppermute | solution.py:318
  3.0 0.0 copy-done.1
  3.0 0.0 copy-done
  3.0 0.8 %project.1 = (bf16[512,384]{1,0:T(8,128)(2,1)S(1)}, bf16[240,128]{1,0:T(8,128)(2,1)S(1)}) custom-call(s32[3]{0:T(128)} %mo_hbm.5, s32[3]{0:T(128)} %fo_hbm.5, bf16[512,768]{1,0:T(8,128)(2,1)S(1)} %copy-done, bf16[3,192,768]{2,1,0:T(8,128)(2,1)S(1)} %bitcast.5, s32[8,128]{1,0:T(8,128)S(1)} %lanes.1.lanes_ref), custom_call_target="tpu_custom_call" | custom-call | flops 301989888 | bytes 4194304 | tf_op jit(solution)/shard_map/project/pallas_call | solution.py:288
  3.8 1.6 %collective-permute-start = (bf16[240,128]{1,0:T(8,128)(2,1)S(1)}, bf16[240,128]{1,0:T(8,128)(2,1)S(1)}, u32[]{:S(2)}, u32[]{:S(2)}) collective-permute-start(bf16[240,128]{1,0:T(8,128)(2,1)S(1)} %get-tuple-element.18.rest_0_.rest_4_), channel_id=1, source_target_pairs={{0,4},{4,8},{8,12},{12,0},{1,5},{5,9},{9,13},{13,1},{2,6},{6,10},{... | collective-permute-start | bytes 184328 | tf_op jit(solution)/shard_map/ppermute | solution.py:366
  5.4 2.6 %collective-permute-start.1 = (bf16[240,128]{1,0:T(8,128)(2,1)S(1)}, bf16[240,128]{1,0:T(8,128)(2,1)S(1)}, u32[]{:S(2)}, u32[]{:S(2)}) collective-permute-start(bf16[240,128]{1,0:T(8,128)(2,1)S(1)} %get-tuple-element.18.rest_0_.rest_4_), channel_id=1, source_target_pairs={{0,8},{4,12},{8,0},{12,4},{1,9},{5,13},{9,1},{13,5},{2,10},{6,14},... | collective-permute-start | bytes 184328 | tf_op jit(solution)/shard_map/ppermute | solution.py:366
  8.0 1.3 %collective-permute-start.2 = (bf16[240,128]{1,0:T(8,128)(2,1)S(1)}, bf16[240,128]{1,0:T(8,128)(2,1)S(1)}, u32[]{:S(2)}, u32[]{:S(2)}) collective-permute-start(bf16[240,128]{1,0:T(8,128)(2,1)S(1)} %get-tuple-element.18.rest_0_.rest_4_), channel_id=1, source_target_pairs={{0,12},{4,0},{8,4},{12,8},{1,13},{5,1},{9,5},{13,9},{2,14},{6,2},{... | collective-permute-start | bytes 184328 | tf_op jit(solution)/shard_map/ppermute | solution.py:366
  9.4 0.0 copy-done.3
  9.4 0.0 copy-done.4
  9.4 1.7 %near.1 = (f32[768,128]{1,0:T(8,128)S(1)}, f32[240,128]{1,0:T(8,128)S(1)}, f32[240,128]{1,0:T(8,128)S(1)}, bf16[240,128]{1,0:T(8,128)(2,1)S(1)}, f32[2,192]{1,0:T(2,128)S(1)}) custom-call(s32[3]{0:T(128)} %mo_hbm.5, s32[3]{0:T(128)} %fo_hbm.5, bf16[512,384]{1,0:T(8,128)(2,1)S(1)} %get-tuple-element.13.kv_ref, bf16[512,768]{1,0:T(8,128)(2,1)S(1)} %copy-done, ...), custom_call_target="tpu_custom_call" | custom-call | flops 536870912 | bytes 4194304 | tf_op jit(solution)/shard_map/near/pallas_call | solution.py:288
  11.1 0.0 collective-permute-done.rest_1_.rest_5_
  11.1 1.5 %collective-permute-done.1.rest_2_.rest_6_ = bf16[240,128]{1,0:T(8,128)(2,1)S(1)} collective-permute-done((bf16[240,128]{1,0:T(8,128)(2,1)S(1)}, bf16[240,128]{1,0:T(8,128)(2,1)S(1)}, u32[]{:S(2)}, u32[]{:S(2)}) %collective-permute-start.1) | collective-permute-done | bytes 61472 | tf_op jit(solution)/shard_map/ppermute | solution.py:366
  12.6 0.0 collective-permute-done.2.rest_3_.rest_7_
  12.6 0.8 %merge.1.rest_0_ = bf16[768,128]{1,0:T(8,128)(2,1)S(1)} custom-call(s32[3]{0:T(128)} %mo_hbm.5, s32[3]{0:T(128)} %fo_hbm.5, f32[768,128]{1,0:T(8,128)S(1)} %get-tuple-element.14.near_ref, bf16[240,128]{1,0:T(8,128)(2,1)S(1)} %get-tuple-element.15.qp_ref, f32[240,128]{1,0:T(8,128)S(1)} %get-tuple-element.16.am_ref, f32[240,128]{1,0:T(8,128)S(1)} %get-tuple-element.17.pk_ref, ...), custom_call_target="tpu_custom_call" | custom-call | flops 536870912 | bytes 4194304 | tf_op jit(solution)/shard_map/merge/pallas_call | solution.py:288
  13.5 1.4 %collective-permute-start.5 = (bf16[768,128]{1,0:T(8,128)(2,1)S(1)}, bf16[768,128]{1,0:T(8,128)(2,1)S(1)}, u32[]{:S(2)}, u32[]{:S(2)}) collective-permute-start(bf16[768,128]{1,0:T(8,128)(2,1)S(1)} %merge.1.rest_0_), channel_id=1, source_target_pairs={{0,2},{1,3},{2,0},{3,1},{4,6},{5,7},{6,4},{7,5},{8,10},{9,11},{10,... | collective-permute-start | bytes 589832 | tf_op jit(solution)/shard_map/ppermute | solution.py:318
  14.8 0.0 copy-done.2
  14.8 0.0 collective-permute-start.4
  14.8 0.0 collective-permute-done.6.rest_1_
  14.8 0.5 %collective-permute-start.8 = (bf16[192,768]{1,0:T(8,128)(2,1)S(1)}, bf16[192,768]{1,0:T(8,128)(2,1)S(1)}, u32[]{:S(2)}, u32[]{:S(2)}) collective-permute-start(bf16[192,768]{1,0:T(8,128)(2,1)S(1)} %collective-permute-done.6.rest_1_), channel_id=1, source_target_pairs={{0,1},{1,0},{2,3},{3,2},{4,5},{5,4},{6,7},{7,6},{8,9},{9,8},{10,11... | collective-permute-start | bytes 884744 | tf_op jit(solution)/shard_map/ppermute | solution.py:318
  15.3 0.1 collective-permute-start.3
  15.4 3.8 %collective-permute-done.5.rest_0_ = bf16[768,128]{1,0:T(8,128)(2,1)S(1)} collective-permute-done((bf16[768,128]{1,0:T(8,128)(2,1)S(1)}, bf16[768,128]{1,0:T(8,128)(2,1)S(1)}, u32[]{:S(2)}, u32[]{:S(2)}) %collective-permute-start.5) | collective-permute-done | bytes 196640 | tf_op jit(solution)/shard_map/ppermute | solution.py:318
  19.2 0.0 collective-permute-start.7
  19.2 0.0 collective-permute-done.3.rest_1_
  19.2 0.0 collective-permute-done.4.rest_3_
  19.2 0.6 %product.2.x_ref = f32[512,768]{1,0:T(8,128)S(1)} custom-call(bf16[512,768]{1,0:T(8,128)(2,1)S(1)} %copy-done, bf16[768,128]{1,0:T(8,128)(2,1)S(1)} %merge.1.rest_0_, bf16[768,128]{1,0:T(8,128)(2,1)S(1)} %collective-permute-done.3.rest_1_, bf16[192,768]{1,0:T(8,128)(2,1)S(1)} %copy-done.2, bf16[192,768]{1,0:T(8,128)(2,1)S(1)} %collective-permute-done.4.rest_3_), custom_call_target="tpu_custom_call" | custom-call | flops 301989888 | bytes 4194304 | tf_op jit(solution)/shard_map/product/pallas_call | solution.py:288
  19.8 0.4 %product.3.x_ref = f32[512,768]{1,0:T(8,128)S(1)} custom-call(f32[512,768]{1,0:T(8,128)S(1)} %product.2.x_ref, bf16[768,128]{1,0:T(8,128)(2,1)S(1)} %collective-permute-done.5.rest_0_, bf16[192,768]{1,0:T(8,128)(2,1)S(1)} %collective-permute-done.6.rest_1_), custom_call_target="tpu_custom_call" | custom-call | flops 150994944 | bytes 4194304 | tf_op jit(solution)/shard_map/product/pallas_call | solution.py:288
  20.2 0.5 %collective-permute-done.7.rest_0_ = bf16[768,128]{1,0:T(8,128)(2,1)S(1)} collective-permute-done((bf16[768,128]{1,0:T(8,128)(2,1)S(1)}, bf16[768,128]{1,0:T(8,128)(2,1)S(1)}, u32[]{:S(2)}, u32[]{:S(2)}) %collective-permute-start.7) | collective-permute-done | bytes 196640 | tf_op jit(solution)/shard_map/ppermute | solution.py:318
  20.7 0.0 collective-permute-done.8.rest_1_
  20.7 1.4 %output.1 = bf16[192,512]{1,0:T(8,128)(2,1)} custom-call(s32[1]{0:T(128)} %bitcast.place, f32[512,768]{1,0:T(8,128)S(1)} %product.3.x_ref, f32[2,192]{1,0:T(2,128)S(1)} %get-tuple-element.20.gb_ref, bf16[768,128]{1,0:T(8,128)(2,1)S(1)} %collective-permute-done.7.rest_0_, bf16[192,768]{1,0:T(8,128)(2,1)S(1)} %collective-permute-done.8.rest_1_), custom_call_target="tpu_custom_call" | custom-call | flops 150994944 | bytes 4194304 | tf_op jit(solution)/shard_map/output/pallas_call | solution.py:288
  (3 shorter events, 0.0 us)
Async XLA Ops:
  0.0 3.0 %copy-start.1 = (bf16[3,768,192]{1,2,0:T(8,128)(2,1)S(1)}, bf16[3,768,192]{1,2,0:T(8,128)(2,1)}, u32[]{:S(2)}) copy-start(bf16[3,768,192]{1,2,0:T(8,128)(2,1)} %param.8) | copy-start | bytes 2654212
  0.0 3.0 %copy-start = (bf16[512,768]{1,0:T(8,128)(2,1)S(1)}, bf16[512,768]{1,0:T(8,128)(2,1)}, u32[]{:S(2)}) copy-start(bf16[512,768]{1,0:T(8,128)(2,1)} %x_ref.5) | copy-start | bytes 2359300
  0.0 9.4 %copy-start.3 = (f32[192]{0:T(256)S(1)}, f32[192]{0:T(256)}, u32[]{:S(2)}) copy-start(f32[192]{0:T(256)} %param.10) | copy-start | bytes 2308
  0.0 9.4 %copy-start.4 = (f32[192]{0:T(256)S(1)}, f32[192]{0:T(256)}, u32[]{:S(2)}) copy-start(f32[192]{0:T(256)} %param.11) | copy-start | bytes 2308
  0.0 14.8 %collective-permute-start.6 = (bf16[192,768]{1,0:T(8,128)(2,1)}, bf16[192,768]{1,0:T(8,128)(2,1)S(1)}, u32[]{:S(2)}, u32[]{:S(2)}) collective-permute-start(bf16[192,768]{1,0:T(8,128)(2,1)} %rest_2_.1), channel_id=1, source_target_pairs={{0,2},{1,3},{2,0},{3,1},{4,6},{5,7},{6,4},{7,5},{8,10},{9,11},{10,... | collective-permute-start | bytes 884744 | tf_op jit(solution)/shard_map/ppermute | solution.py:318
  3.8 7.3 %collective-permute-start = (bf16[240,128]{1,0:T(8,128)(2,1)S(1)}, bf16[240,128]{1,0:T(8,128)(2,1)S(1)}, u32[]{:S(2)}, u32[]{:S(2)}) collective-permute-start(bf16[240,128]{1,0:T(8,128)(2,1)S(1)} %get-tuple-element.18.rest_0_.rest_4_), channel_id=1, source_target_pairs={{0,4},{4,8},{8,12},{12,0},{1,5},{5,9},{9,13},{13,1},{2,6},{6,10},{... | collective-permute-start | bytes 184328 | tf_op jit(solution)/shard_map/ppermute | solution.py:366
  5.4 7.1 %collective-permute-start.1 = (bf16[240,128]{1,0:T(8,128)(2,1)S(1)}, bf16[240,128]{1,0:T(8,128)(2,1)S(1)}, u32[]{:S(2)}, u32[]{:S(2)}) collective-permute-start(bf16[240,128]{1,0:T(8,128)(2,1)S(1)} %get-tuple-element.18.rest_0_.rest_4_), channel_id=1, source_target_pairs={{0,8},{4,12},{8,0},{12,4},{1,9},{5,13},{9,1},{13,5},{2,10},{6,14},... | collective-permute-start | bytes 184328 | tf_op jit(solution)/shard_map/ppermute | solution.py:366
  8.0 4.6 %collective-permute-start.2 = (bf16[240,128]{1,0:T(8,128)(2,1)S(1)}, bf16[240,128]{1,0:T(8,128)(2,1)S(1)}, u32[]{:S(2)}, u32[]{:S(2)}) collective-permute-start(bf16[240,128]{1,0:T(8,128)(2,1)S(1)} %get-tuple-element.18.rest_0_.rest_4_), channel_id=1, source_target_pairs={{0,12},{4,0},{8,4},{12,8},{1,13},{5,1},{9,5},{13,9},{2,14},{6,2},{... | collective-permute-start | bytes 184328 | tf_op jit(solution)/shard_map/ppermute | solution.py:366
  9.4 5.4 %copy-start.2 = (bf16[192,768]{1,0:T(8,128)(2,1)S(1)}, bf16[192,768]{1,0:T(8,128)(2,1)}, u32[]{:S(2)}) copy-start(bf16[192,768]{1,0:T(8,128)(2,1)} %rest_2_.1) | copy-start | bytes 884740
  13.5 5.7 %collective-permute-start.5 = (bf16[768,128]{1,0:T(8,128)(2,1)S(1)}, bf16[768,128]{1,0:T(8,128)(2,1)S(1)}, u32[]{:S(2)}, u32[]{:S(2)}) collective-permute-start(bf16[768,128]{1,0:T(8,128)(2,1)S(1)} %merge.1.rest_0_), channel_id=1, source_target_pairs={{0,2},{1,3},{2,0},{3,1},{4,6},{5,7},{6,4},{7,5},{8,10},{9,11},{10,... | collective-permute-start | bytes 589832 | tf_op jit(solution)/shard_map/ppermute | solution.py:318
  14.8 4.4 %collective-permute-start.4 = (bf16[192,768]{1,0:T(8,128)(2,1)S(1)}, bf16[192,768]{1,0:T(8,128)(2,1)S(1)}, u32[]{:S(2)}, u32[]{:S(2)}) collective-permute-start(bf16[192,768]{1,0:T(8,128)(2,1)S(1)} %copy-done.2), channel_id=1, source_target_pairs={{0,1},{1,0},{2,3},{3,2},{4,5},{5,4},{6,7},{7,6},{8,9},{9,8},{10,11... | collective-permute-start | bytes 884744 | tf_op jit(solution)/shard_map/ppermute | solution.py:318
  14.8 5.8 %collective-permute-start.8 = (bf16[192,768]{1,0:T(8,128)(2,1)S(1)}, bf16[192,768]{1,0:T(8,128)(2,1)S(1)}, u32[]{:S(2)}, u32[]{:S(2)}) collective-permute-start(bf16[192,768]{1,0:T(8,128)(2,1)S(1)} %collective-permute-done.6.rest_1_), channel_id=1, source_target_pairs={{0,1},{1,0},{2,3},{3,2},{4,5},{5,4},{6,7},{7,6},{8,9},{9,8},{10,11... | collective-permute-start | bytes 884744 | tf_op jit(solution)/shard_map/ppermute | solution.py:318
  15.3 3.9 %collective-permute-start.3 = (bf16[768,128]{1,0:T(8,128)(2,1)S(1)}, bf16[768,128]{1,0:T(8,128)(2,1)S(1)}, u32[]{:S(2)}, u32[]{:S(2)}) collective-permute-start(bf16[768,128]{1,0:T(8,128)(2,1)S(1)} %merge.1.rest_0_), channel_id=1, source_target_pairs={{0,1},{1,0},{2,3},{3,2},{4,5},{5,4},{6,7},{7,6},{8,9},{9,8},{10,11... | collective-permute-start | bytes 589832 | tf_op jit(solution)/shard_map/ppermute | solution.py:318
  19.2 1.4 %collective-permute-start.7 = (bf16[768,128]{1,0:T(8,128)(2,1)S(1)}, bf16[768,128]{1,0:T(8,128)(2,1)S(1)}, u32[]{:S(2)}, u32[]{:S(2)}) collective-permute-start(bf16[768,128]{1,0:T(8,128)(2,1)S(1)} %collective-permute-done.5.rest_0_), channel_id=1, source_target_pairs={{0,1},{1,0},{2,3},{3,2},{4,5},{5,4},{6,7},{7,6},{8,9},{9,8},{10,11... | collective-permute-start | bytes 589832 | tf_op jit(solution)/shard_map/ppermute | solution.py:318

commit v8 on v7

--- a/solution.py
+++ b/solution.py
@@ -31,13 +31,13 @@
 
 
 def project_kernel(
-    mo_hbm, fo_hbm, x_ref, w_ref, lanes_ref, kv_ref, kvp_ref, mo, fo, scr, sems
+    mo_from, fo_from, x_ref, w_ref, lanes_ref, kv_ref, kvp_ref, mo, fo, scr, sems
 ):
     rows = x_ref.shape[0]
     mid, far = rows // R1, rows // R2
     per = mid + far
     half = rows // 2
-    copies = tell(mo_hbm, fo_hbm, mo, fo, sems)
+    copies = tell(mo_from, fo_from, mo, fo, sems)
     k = [w_ref[1, h * HALF : (h + 1) * HALF] for h in range(3)]
     v = [w_ref[2, h * HALF : (h + 1) * HALF] for h in range(3)]
     w = jnp.concatenate([v[0], k[0], k[1], v[1], v[2], k[2]], axis=0)
@@ -92,10 +92,10 @@
     out_ref[...] = lax.broadcasted_iota(jnp.int32, out_ref.shape, 1)
 
 
-def tell(mo_hbm, fo_hbm, mo, fo, sems):
+def tell(mo_from, fo_from, mo, fo, sems):
     copies = [
-        pltpu.make_async_copy(mo_hbm, mo, sems.at[0]),
-        pltpu.make_async_copy(fo_hbm, fo, sems.at[1]),
+        pltpu.make_async_copy(mo_from, mo, sems.at[0]),
+        pltpu.make_async_copy(fo_from, fo, sems.at[1]),
     ]
     for copy in copies:
         copy.start()
@@ -104,8 +104,8 @@
 
 def near_kernel(
     factor,
-    mo_hbm,
-    fo_hbm,
+    mo_from,
+    fo_from,
     kv_ref,
     x_ref,
     w_ref,
@@ -124,7 +124,7 @@
     q_ref,
     sems,
 ):
-    copies = tell(mo_hbm, fo_hbm, mo, fo, sems)
+    copies = tell(mo_from, fo_from, mo, fo, sems)
     gb_ref[0:1] = gain_ref[...]
     gb_ref[1:2] = bias_ref[...]
     rows = kv_ref.shape[0]
@@ -179,10 +179,10 @@
             qp_ref[at] = jnp.where(kept, q_scr[h // 2, picked], 0.0).astype(bf16)
 
 
-def merge_kernel(factor, mid_n, far_n, mo_hbm, fo_hbm, near_ref, qp_ref, am_ref, pk_ref, *rest):
+def merge_kernel(factor, mid_n, far_n, mo_from, fo_from, near_ref, qp_ref, am_ref, pk_ref, *rest):
     mids, fars = rest[:mid_n], rest[mid_n : mid_n + far_n]
     attn_ref, mo, fo, attn_scr, am_scr, pk_scr, sems = rest[mid_n + far_n :]
-    copies = tell(mo_hbm, fo_hbm, mo, fo, sems)
+    copies = tell(mo_from, fo_from, mo, fo, sems)
     rows = near_ref.shape[0] * 2 // 3
     attn_scr[...] = near_ref[...]
     per = qp_ref.shape[0] // 3
@@ -259,24 +259,38 @@
         out_ref[at] = x_ref[at].astype(f32) + part
 
 
-def output_kernel(head_count, place, x_ref, gb_ref, *rest):
-    out_ref, resid_scr = rest[-2:]
-    count = len(rest) // 2 - 1
+def own_kernel(place, x_ref, attn_ref, w_ref, last_ref, out_ref, own_ref, last_own_ref):
+    product_kernel(x_ref, attn_ref, w_ref, out_ref)
+    cols = own_ref.shape[1]
+    for i in range(out_ref.shape[1] // cols):
+
+        @pl.when(place[0] == i)
+        def _():
+            at = slice(i * cols, (i + 1) * cols)
+            own_ref[...] = out_ref[:, at]
+            last_own_ref[...] = last_ref[:, at]
+
+
+def output_kernel(x_ref, own_ref, last_own_ref, gb_ref, attn_ref, w_ref, out_hbm, out_ref, sems):
+    copies = []
     rows, width = x_ref.shape
-    half = rows // 2
-    cols = width // head_count
-    for first in (0, half):
-        at = slice(first, first + half)
-        resid = x_ref[at].astype(f32) + product(first, half, rest[:count], rest[count : 2 * count])
+    step = rows // 4
+    for i in range(4):
+        at = slice(i * step, (i + 1) * step)
+        third = attn_ref[rows + i % 2 * step : rows + (i % 2 + 1) * step]
+        if i > 1:
+            third = swap(third.astype(f32)).astype(bf16)
+        attn = jnp.concatenate([attn_ref[at], third[:, :HALF]], axis=1)
+        resid = x_ref[at] + jnp.dot(attn, w_ref[...], preferred_element_type=f32)
         mean = jnp.sum(resid, axis=1, keepdims=True) / width
         var = jnp.sum(resid * resid, axis=1, keepdims=True) / width - mean * mean
-        resid_scr[at] = (resid - mean) * lax.rsqrt(var + epsilon)
-    for i in range(head_count):
-
-        @pl.when(place[0] == i)
-        def _():
-            mine = resid_scr[:, i * cols : (i + 1) * cols]
-            out_ref[...] = (mine * gb_ref[0:1] + gb_ref[1:2]).T.astype(bf16)
+        mine = own_ref[at] + jnp.dot(attn, last_own_ref[...], preferred_element_type=f32)
+        normed = (mine - mean) * lax.rsqrt(var + epsilon) * gb_ref[0:1] + gb_ref[1:2]
+        out_ref[:, at] = normed.astype(bf16).T
+        copies.append(pltpu.make_async_copy(out_ref.at[:, at], out_hbm.at[:, at], sems.at[i]))
+        copies[i].start()
+    for copy in copies:
+        copy.wait()
 
 
 IN_VMEM = pl.BlockSpec(memory_space=pltpu.VMEM)
@@ -284,12 +298,12 @@
 IN_HBM = pl.BlockSpec(memory_space=pltpu.HBM)
 
 
-def call(kernel, outs, scratch, scalars, far, near, name, flops, limit):
+def call(kernel, outs, scratch, scalars, far, near, name, flops, limit, held=None):
     return pl.pallas_call(
         kernel,
         out_shape=outs,
         in_specs=[IN_SMEM] * len(scalars) + [IN_HBM] * len(far) + [IN_VMEM] * len(near),
-        out_specs=jax.tree.map(lambda _: IN_VMEM, outs),
+        out_specs=jax.tree.map(lambda _: held or IN_VMEM, outs),
         scratch_shapes=scratch,
         compiler_params=pltpu.CompilerParams(vmem_limit_bytes=limit << 20),
         name=name,
@@ -344,8 +358,8 @@
             pltpu.SemaphoreType.DMA((2,)),
         ],
         (),
-        offsets,
-        (x, w_rows, lanes),
+        (),
+        (mid_offset, far_offset, x, w_rows, lanes),
         "project",
         2 * rows * width * 2 * cols,
         24,
@@ -355,12 +369,9 @@
     mid_devs = min(8, seq_count)
 
     def within(step):
-        def partner(i):
-            if False:
-                return i % mid_devs ^ step
-            return (i + step) % mid_devs
-
-        return [(i, i // mid_devs * mid_devs + partner(i)) for i in range(seq_count)]
+        return [
+            (i, i // mid_devs * mid_devs + (i + step) % mid_devs) for i in range(seq_count)
+        ]
 
     if mid_devs == seq_count:
         mids = [kvp] + [lax.ppermute(kvp, "seq", within(s)) for s in range(1, mid_devs)]
@@ -413,8 +424,8 @@
             pltpu.SemaphoreType.DMA((2,)),
         ],
         (),
-        offsets,
-        (near, qp, am, pk, *mids, *(fars or mids)),
+        (),
+        (mid_offset, far_offset, near, qp, am, pk, *mids, *(fars or mids)),
         "merge",
         1 << 29,
         24,
@@ -425,30 +436,44 @@
     else:
         attns = spread(attn)
 
-    resid = x
-    for r in ((0, 1), (2,)) if two_step else ():
-        resid = call(
-            product_kernel,
+    flops = 2 * rows * cols * width
+    resid = call(
+        product_kernel,
+        shape((rows, width), f32),
+        [],
+        (),
+        (),
+        (x, *attns[:-2], *weights[:-2]),
+        "product",
+        (head_count - 2) * flops,
+        24,
+    )
+    resid, own, last_own = call(
+        own_kernel,
+        (
             shape((rows, width), f32),
-            [],
-            (),
-            (),
-            (resid, *(attns[i] for i in r), *(weights[i] for i in r)),
-            "product",
-            len(r) * 2 * rows * cols * width,
-            24,
-        )
-    left = slice(3, None) if two_step else slice(None)
+            shape((rows, cols), f32),
+            shape((cols, cols), bf16),
+        ),
+        [],
+        (lax.axis_index("head").reshape(1),),
+        (),
+        (resid, attns[-2], *weights[-2:]),
+        "own",
+        flops,
+        24,
+    )
     out = call(
-        partial(output_kernel, head_count),
+        output_kernel,
         shape((cols, rows), bf16),
-        [pltpu.VMEM((rows, width), f32)],
-        (lax.axis_index("head").reshape(1),),
-        (),
-        (resid, gb, *attns[left], *weights[left]),
+        [pltpu.VMEM((cols, rows), bf16), pltpu.SemaphoreType.DMA((4,))],
+        (),
+        (),
+        (resid, own, last_own, gb, attns[-1], weights[-1]),
         "output",
-        2 * rows * width * cols,
-        24,
+        flops,
+        24,
+        IN_HBM,
     )
     return out.T
 

time: 22.2 us -> 22 us (level)
  no operation moved by 1% of the time
where the time goes in v8:
time: 22 us; the launch traced here: 21.8 us
  starting transfers between devices  10.5 us (48%)
  waiting for transfers between devices  5.75 us (26%)
  Pallas kernels  5.44 us (25%)
    ppermute x3, starting transfers between devices, local(): lax.ppermute(kvp, 'seq', within(s))  5.56 us
    pallas_call x7, Pallas kernels, call(): pl.pallas_call(kernel, out_shape=outs, in_specs=[IN_SMEM] * len(scalars)...  5.44 us
    ppermute x6, starting transfers between devices, to(): return lax.ppermute(array, 'head', paths[r])  4.93 us
    ppermute x6, waiting for transfers between devices, to(): return lax.ppermute(array, 'head', paths[r])  4.23 us
    ppermute x3, waiting for transfers between devices, local(): lax.ppermute(kvp, 'seq', within(s))  1.52 us
  transfers between devices with their start and end apart: 9, of which 3 were waited for; matrix products, arithmetic and copies ran while one was open for 0% of the time, Pallas kernels for 19%

profile of v8, /device:TPU:0, one launch (start us, length us, event | category | flops | bytes accessed | tf_op | source)
XLA Modules:
  0.0 21.8 jit_solution(6167420626731324890)
XLA Ops:
  0.0 0.0 copy-start.8
  0.0 3.0 %collective-permute-start.6 = (bf16[192,768]{1,0:T(8,128)(2,1)}, bf16[192,768]{1,0:T(8,128)(2,1)S(1)}, u32[]{:S(2)}, u32[]{:S(2)}) collective-permute-start(bf16[192,768]{1,0:T(8,128)(2,1)} %rest_2_.1), channel_id=1, source_target_pairs={{0,2},{1,3},{2,0},{3,1},{4,6},{5,7},{6,4},{7,5},{8,10},{9,11},{10,... | collective-permute-start | bytes 884744 | tf_op jit(solution)/shard_map/ppermute | solution.py:332
  3.1 0.0 copy-done.1
  3.1 0.0 copy-done.3
  3.1 0.0 copy-done.5
  3.1 0.0 copy-start.4
  3.1 0.0 copy-start.6
  3.1 0.7 %project.1 = (bf16[512,384]{1,0:T(8,128)(2,1)S(1)}, bf16[240,128]{1,0:T(8,128)(2,1)S(1)}) custom-call(s32[3]{0:T(128)S(1)} %copy-done.3, s32[3]{0:T(128)S(1)} %copy-done.5, bf16[512,768]{1,0:T(8,128)(2,1)S(1)} %copy-done, bf16[3,192,768]{2,1,0:T(8,128)(2,1)S(1)} %bitcast.5, s32[8,128]{1,0:T(8,128)S(1)} %lanes.1.lanes_ref), custom_call_target="tpu_custom_call" | custom-call | flops 301989888 | bytes 4194304 | tf_op jit(solution)/shard_map/project/pallas_call | solution.py:302
  3.8 1.6 %collective-permute-start = (bf16[240,128]{1,0:T(8,128)(2,1)S(1)}, bf16[240,128]{1,0:T(8,128)(2,1)S(1)}, u32[]{:S(2)}, u32[]{:S(2)}) collective-permute-start(bf16[240,128]{1,0:T(8,128)(2,1)S(1)} %get-tuple-element.21.rest_0_.rest_4_), channel_id=1, source_target_pairs={{0,4},{4,8},{8,12},{12,0},{1,5},{5,9},{9,13},{13,1},{2,6},{6,10},{... | collective-permute-start | bytes 184328 | tf_op jit(solution)/shard_map/ppermute | solution.py:377
  5.4 2.6 %collective-permute-start.1 = (bf16[240,128]{1,0:T(8,128)(2,1)S(1)}, bf16[240,128]{1,0:T(8,128)(2,1)S(1)}, u32[]{:S(2)}, u32[]{:S(2)}) collective-permute-start(bf16[240,128]{1,0:T(8,128)(2,1)S(1)} %get-tuple-element.21.rest_0_.rest_4_), channel_id=1, source_target_pairs={{0,8},{4,12},{8,0},{12,4},{1,9},{5,13},{9,1},{13,5},{2,10},{6,14},... | collective-permute-start | bytes 184328 | tf_op jit(solution)/shard_map/ppermute | solution.py:377
  8.0 1.3 %collective-permute-start.2 = (bf16[240,128]{1,0:T(8,128)(2,1)S(1)}, bf16[240,128]{1,0:T(8,128)(2,1)S(1)}, u32[]{:S(2)}, u32[]{:S(2)}) collective-permute-start(bf16[240,128]{1,0:T(8,128)(2,1)S(1)} %get-tuple-element.21.rest_0_.rest_4_), channel_id=1, source_target_pairs={{0,12},{4,0},{8,4},{12,8},{1,13},{5,1},{9,5},{13,9},{2,14},{6,2},{... | collective-permute-start | bytes 184328 | tf_op jit(solution)/shard_map/ppermute | solution.py:377
  9.3 0.0 copy-done.7
  9.3 1.7 %near.1 = (f32[768,128]{1,0:T(8,128)S(1)}, f32[240,128]{1,0:T(8,128)S(1)}, f32[240,128]{1,0:T(8,128)S(1)}, bf16[240,128]{1,0:T(8,128)(2,1)S(1)}, f32[2,192]{1,0:T(2,128)S(1)}) custom-call(s32[3]{0:T(128)} %mo_from.5, s32[3]{0:T(128)} %fo_from.5, bf16[512,384]{1,0:T(8,128)(2,1)S(1)} %get-tuple-element.16.kv_ref, bf16[512,768]{1,0:T(8,128)(2,1)S(1)} %copy-done, ...), custom_call_target="tpu_custom_call" | custom-call | flops 536870912 | bytes 4194304 | tf_op jit(solution)/shard_map/near/pallas_call | solution.py:302
  11.1 0.0 collective-permute-done.rest_1_.rest_5_
  11.1 1.5 %collective-permute-done.1.rest_2_.rest_6_ = bf16[240,128]{1,0:T(8,128)(2,1)S(1)} collective-permute-done((bf16[240,128]{1,0:T(8,128)(2,1)S(1)}, bf16[240,128]{1,0:T(8,128)(2,1)S(1)}, u32[]{:S(2)}, u32[]{:S(2)}) %collective-permute-start.1) | collective-permute-done | bytes 61472 | tf_op jit(solution)/shard_map/ppermute | solution.py:377
  12.6 0.0 collective-permute-done.2.rest_3_.rest_7_
  12.6 0.0 copy-done.6
  12.6 0.7 %merge.1.rest_0_ = bf16[768,128]{1,0:T(8,128)(2,1)S(1)} custom-call(s32[3]{0:T(128)S(1)} %copy-done.4, s32[3]{0:T(128)S(1)} %copy-done.6, f32[768,128]{1,0:T(8,128)S(1)} %get-tuple-element.17.near_ref, bf16[240,128]{1,0:T(8,128)(2,1)S(1)} %get-tuple-element.18.qp_ref, f32[240,128]{1,0:T(8,128)S(1)} %get-tuple-element.19.am_ref, ...), custom_call_target="tpu_custom_call" | custom-call | flops 536870912 | bytes 4194304 | tf_op jit(solution)/shard_map/merge/pallas_call | solution.py:302
  13.3 1.3 %collective-permute-start.5 = (bf16[768,128]{1,0:T(8,128)(2,1)S(1)}, bf16[768,128]{1,0:T(8,128)(2,1)S(1)}, u32[]{:S(2)}, u32[]{:S(2)}) collective-permute-start(bf16[768,128]{1,0:T(8,128)(2,1)S(1)} %merge.1.rest_0_), channel_id=1, source_target_pairs={{0,2},{1,3},{2,0},{3,1},{4,6},{5,7},{6,4},{7,5},{8,10},{9,11},{10,... | collective-permute-start | bytes 589832 | tf_op jit(solution)/shard_map/ppermute | solution.py:332
  14.7 0.0 collective-permute-start.4
  14.7 0.0 collective-permute-done.6.w_ref
  14.7 0.5 %collective-permute-start.7 = (bf16[192,768]{1,0:T(8,128)(2,1)S(1)}, bf16[192,768]{1,0:T(8,128)(2,1)S(1)}, u32[]{:S(2)}, u32[]{:S(2)}) collective-permute-start(bf16[192,768]{1,0:T(8,128)(2,1)S(1)} %collective-permute-done.6.w_ref), channel_id=1, source_target_pairs={{0,1},{1,0},{2,3},{3,2},{4,5},{5,4},{6,7},{7,6},{8,9},{9,8},{10,11... | collective-permute-start | bytes 884744 | tf_op jit(solution)/shard_map/ppermute | solution.py:332
  15.2 0.1 collective-permute-start.3
  15.3 3.8 %collective-permute-done.5.attn_ref = bf16[768,128]{1,0:T(8,128)(2,1)S(1)} collective-permute-done((bf16[768,128]{1,0:T(8,128)(2,1)S(1)}, bf16[768,128]{1,0:T(8,128)(2,1)S(1)}, u32[]{:S(2)}, u32[]{:S(2)}) %collective-permute-start.5) | collective-permute-done | bytes 196640 | tf_op jit(solution)/shard_map/ppermute | solution.py:332
  19.1 0.0 collective-permute-start.8
  19.1 0.0 collective-permute-done.3.rest_1_
  19.1 0.0 collective-permute-done.4.rest_3_
  19.1 0.6 %product.1.x_ref = f32[512,768]{1,0:T(8,128)S(1)} custom-call(bf16[512,768]{1,0:T(8,128)(2,1)S(1)} %copy-done, bf16[768,128]{1,0:T(8,128)(2,1)S(1)} %merge.1.rest_0_, bf16[768,128]{1,0:T(8,128)(2,1)S(1)} %collective-permute-done.3.rest_1_, bf16[192,768]{1,0:T(8,128)(2,1)S(1)} %copy-done.2, bf16[192,768]{1,0:T(8,128)(2,1)S(1)} %collective-permute-done.4.rest_3_), custom_call_target="tpu_custom_call" | custom-call | flops 301989888 | bytes 4194304 | tf_op jit(solution)/shard_map/product/pallas_call | solution.py:302
  19.7 0.0 collective-permute-done.7.last_ref.w_ref
  19.7 0.4 %own.1 = (f32[512,768]{1,0:T(8,128)S(1)}, f32[512,192]{1,0:T(8,128)S(1)}, bf16[192,192]{1,0:T(8,128)(2,1)S(1)}) custom-call(s32[1]{0:T(128)} %bitcast.place, f32[512,768]{1,0:T(8,128)S(1)} %product.1.x_ref, bf16[768,128]{1,0:T(8,128)(2,1)S(1)} %collective-permute-done.5.attn_ref, bf16[192,768]{1,0:T(8,128)(2,1)S(1)} %collective-permute-done.6.w_ref, ...), custom_call_target="tpu_custom_call" | custom-call | flops 150994944 | bytes 4194304 | tf_op jit(solution)/shard_map/own/pallas_call | solution.py:302
  20.1 0.4 %collective-permute-done.8.attn_ref = bf16[768,128]{1,0:T(8,128)(2,1)S(1)} collective-permute-done((bf16[768,128]{1,0:T(8,128)(2,1)S(1)}, bf16[768,128]{1,0:T(8,128)(2,1)S(1)}, u32[]{:S(2)}, u32[]{:S(2)}) %collective-permute-start.8) | collective-permute-done | bytes 196640 | tf_op jit(solution)/shard_map/ppermute | solution.py:332
  20.5 1.3 %output.1 = bf16[192,512]{1,0:T(8,128)(2,1)} custom-call(f32[512,768]{1,0:T(8,128)S(1)} %get-tuple-element.23.x_ref, f32[512,192]{1,0:T(8,128)S(1)} %get-tuple-element.24.own_ref, bf16[192,192]{1,0:T(8,128)(2,1)S(1)} %get-tuple-element.25.last_own_ref, f32[2,192]{1,0:T(2,128)S(1)} %get-tuple-element.26.gb_ref, ...), custom_call_target="tpu_custom_call" | custom-call | flops 150994944 | bytes 4194304 | tf_op jit(solution)/shard_map/output/pallas_call | solution.py:302
  (11 shorter events, 0.0 us)
Async XLA Ops:
  0.0 3.1 %copy-start.1 = (bf16[3,768,192]{1,2,0:T(8,128)(2,1)S(1)}, bf16[3,768,192]{1,2,0:T(8,128)(2,1)}, u32[]{:S(2)}) copy-start(bf16[3,768,192]{1,2,0:T(8,128)(2,1)} %param.8) | copy-start | bytes 2654212
  0.0 3.1 %copy-start.3 = (s32[3]{0:T(128)S(1)}, s32[3]{0:T(128)}, u32[]{:S(2)}) copy-start(s32[3]{0:T(128)} %mo_from.5) | copy-start | bytes 40
  0.0 3.1 %copy-start.5 = (s32[3]{0:T(128)S(1)}, s32[3]{0:T(128)}, u32[]{:S(2)}) copy-start(s32[3]{0:T(128)} %fo_from.5) | copy-start | bytes 40
  0.0 3.1 %copy-start = (bf16[512,768]{1,0:T(8,128)(2,1)S(1)}, bf16[512,768]{1,0:T(8,128)(2,1)}, u32[]{:S(2)}) copy-start(bf16[512,768]{1,0:T(8,128)(2,1)} %x_ref.5) | copy-start | bytes 2359300
  0.0 9.3 %copy-start.7 = (f32[192]{0:T(256)S(1)}, f32[192]{0:T(256)}, u32[]{:S(2)}) copy-start(f32[192]{0:T(256)} %param.10) | copy-start | bytes 2308
  0.0 9.3 %copy-start.8 = (f32[192]{0:T(256)S(1)}, f32[192]{0:T(256)}, u32[]{:S(2)}) copy-start(f32[192]{0:T(256)} %param.11) | copy-start | bytes 2308
  0.0 14.6 %collective-permute-start.6 = (bf16[192,768]{1,0:T(8,128)(2,1)}, bf16[192,768]{1,0:T(8,128)(2,1)S(1)}, u32[]{:S(2)}, u32[]{:S(2)}) collective-permute-start(bf16[192,768]{1,0:T(8,128)(2,1)} %rest_2_.1), channel_id=1, source_target_pairs={{0,2},{1,3},{2,0},{3,1},{4,6},{5,7},{6,4},{7,5},{8,10},{9,11},{10,... | collective-permute-start | bytes 884744 | tf_op jit(solution)/shard_map/ppermute | solution.py:332
  3.1 9.5 %copy-start.4 = (s32[3]{0:T(128)S(1)}, s32[3]{0:T(128)}, u32[]{:S(2)}) copy-start(s32[3]{0:T(128)} %mo_from.5) | copy-start | bytes 40
  3.1 9.5 %copy-start.6 = (s32[3]{0:T(128)S(1)}, s32[3]{0:T(128)}, u32[]{:S(2)}) copy-start(s32[3]{0:T(128)} %fo_from.5) | copy-start | bytes 40
  3.8 7.3 %collective-permute-start = (bf16[240,128]{1,0:T(8,128)(2,1)S(1)}, bf16[240,128]{1,0:T(8,128)(2,1)S(1)}, u32[]{:S(2)}, u32[]{:S(2)}) collective-permute-start(bf16[240,128]{1,0:T(8,128)(2,1)S(1)} %get-tuple-element.21.rest_0_.rest_4_), channel_id=1, source_target_pairs={{0,4},{4,8},{8,12},{12,0},{1,5},{5,9},{9,13},{13,1},{2,6},{6,10},{... | collective-permute-start | bytes 184328 | tf_op jit(solution)/shard_map/ppermute | solution.py:377
  5.4 7.2 %collective-permute-start.1 = (bf16[240,128]{1,0:T(8,128)(2,1)S(1)}, bf16[240,128]{1,0:T(8,128)(2,1)S(1)}, u32[]{:S(2)}, u32[]{:S(2)}) collective-permute-start(bf16[240,128]{1,0:T(8,128)(2,1)S(1)} %get-tuple-element.21.rest_0_.rest_4_), channel_id=1, source_target_pairs={{0,8},{4,12},{8,0},{12,4},{1,9},{5,13},{9,1},{13,5},{2,10},{6,14},... | collective-permute-start | bytes 184328 | tf_op jit(solution)/shard_map/ppermute | solution.py:377
  8.0 4.6 %collective-permute-start.2 = (bf16[240,128]{1,0:T(8,128)(2,1)S(1)}, bf16[240,128]{1,0:T(8,128)(2,1)S(1)}, u32[]{:S(2)}, u32[]{:S(2)}) collective-permute-start(bf16[240,128]{1,0:T(8,128)(2,1)S(1)} %get-tuple-element.21.rest_0_.rest_4_), channel_id=1, source_target_pairs={{0,12},{4,0},{8,4},{12,8},{1,13},{5,1},{9,5},{13,9},{2,14},{6,2},{... | collective-permute-start | bytes 184328 | tf_op jit(solution)/shard_map/ppermute | solution.py:377
  9.3 5.3 %copy-start.2 = (bf16[192,768]{1,0:T(8,128)(2,1)S(1)}, bf16[192,768]{1,0:T(8,128)(2,1)}, u32[]{:S(2)}) copy-start(bf16[192,768]{1,0:T(8,128)(2,1)} %rest_2_.1) | copy-start | bytes 884740
  13.3 5.7 %collective-permute-start.5 = (bf16[768,128]{1,0:T(8,128)(2,1)S(1)}, bf16[768,128]{1,0:T(8,128)(2,1)S(1)}, u32[]{:S(2)}, u32[]{:S(2)}) collective-permute-start(bf16[768,128]{1,0:T(8,128)(2,1)S(1)} %merge.1.rest_0_), channel_id=1, source_target_pairs={{0,2},{1,3},{2,0},{3,1},{4,6},{5,7},{6,4},{7,5},{8,10},{9,11},{10,... | collective-permute-start | bytes 589832 | tf_op jit(solution)/shard_map/ppermute | solution.py:332
  14.7 4.4 %collective-permute-start.4 = (bf16[192,768]{1,0:T(8,128)(2,1)S(1)}, bf16[192,768]{1,0:T(8,128)(2,1)S(1)}, u32[]{:S(2)}, u32[]{:S(2)}) collective-permute-start(bf16[192,768]{1,0:T(8,128)(2,1)S(1)} %copy-done.2), channel_id=1, source_target_pairs={{0,1},{1,0},{2,3},{3,2},{4,5},{5,4},{6,7},{7,6},{8,9},{9,8},{10,11... | collective-permute-start | bytes 884744 | tf_op jit(solution)/shard_map/ppermute | solution.py:332
  14.7 5.0 %collective-permute-start.7 = (bf16[192,768]{1,0:T(8,128)(2,1)S(1)}, bf16[192,768]{1,0:T(8,128)(2,1)S(1)}, u32[]{:S(2)}, u32[]{:S(2)}) collective-permute-start(bf16[192,768]{1,0:T(8,128)(2,1)S(1)} %collective-permute-done.6.w_ref), channel_id=1, source_target_pairs={{0,1},{1,0},{2,3},{3,2},{4,5},{5,4},{6,7},{7,6},{8,9},{9,8},{10,11... | collective-permute-start | bytes 884744 | tf_op jit(solution)/shard_map/ppermute | solution.py:332
  15.2 3.9 %collective-permute-start.3 = (bf16[768,128]{1,0:T(8,128)(2,1)S(1)}, bf16[768,128]{1,0:T(8,128)(2,1)S(1)}, u32[]{:S(2)}, u32[]{:S(2)}) collective-permute-start(bf16[768,128]{1,0:T(8,128)(2,1)S(1)} %merge.1.rest_0_), channel_id=1, source_target_pairs={{0,1},{1,0},{2,3},{3,2},{4,5},{5,4},{6,7},{7,6},{8,9},{9,8},{10,11... | collective-permute-start | bytes 589832 | tf_op jit(solution)/shard_map/ppermute | solution.py:332
  19.1 1.4 %collective-permute-start.8 = (bf16[768,128]{1,0:T(8,128)(2,1)S(1)}, bf16[768,128]{1,0:T(8,128)(2,1)S(1)}, u32[]{:S(2)}, u32[]{:S(2)}) collective-permute-start(bf16[768,128]{1,0:T(8,128)(2,1)S(1)} %collective-permute-done.5.attn_ref), channel_id=1, source_target_pairs={{0,1},{1,0},{2,3},{3,2},{4,5},{5,4},{6,7},{7,6},{8,9},{9,8},{10,11... | collective-permute-start | bytes 589832 | tf_op jit(solution)/shard_map/ppermute | solution.py:332

commit v9 on v8

--- a/solution.py
+++ b/solution.py
@@ -259,8 +259,9 @@
         out_ref[at] = x_ref[at].astype(f32) + part
 
 
-def own_kernel(place, x_ref, attn_ref, w_ref, last_ref, out_ref, own_ref, last_own_ref):
-    product_kernel(x_ref, attn_ref, w_ref, out_ref)
+def own_kernel(place, last_ref, *refs):
+    out_ref, own_ref, last_own_ref = refs[-3:]
+    product_kernel(*refs[:-3], out_ref)
     cols = own_ref.shape[1]
     for i in range(out_ref.shape[1] // cols):
 
@@ -282,8 +283,9 @@
             third = swap(third.astype(f32)).astype(bf16)
         attn = jnp.concatenate([attn_ref[at], third[:, :HALF]], axis=1)
         resid = x_ref[at] + jnp.dot(attn, w_ref[...], preferred_element_type=f32)
-        mean = jnp.sum(resid, axis=1, keepdims=True) / width
-        var = jnp.sum(resid * resid, axis=1, keepdims=True) / width - mean * mean
+        tiles = [resid[:, j : j + LANES] for j in range(0, width, LANES)]
+        mean = jnp.sum(sum(tiles), axis=1, keepdims=True) / width
+        var = jnp.sum(sum(t * t for t in tiles), axis=1, keepdims=True) / width - mean * mean
         mine = own_ref[at] + jnp.dot(attn, last_own_ref[...], preferred_element_type=f32)
         normed = (mine - mean) * lax.rsqrt(var + epsilon) * gb_ref[0:1] + gb_ref[1:2]
         out_ref[:, at] = normed.astype(bf16).T
@@ -437,17 +439,6 @@
         attns = spread(attn)
 
     flops = 2 * rows * cols * width
-    resid = call(
-        product_kernel,
-        shape((rows, width), f32),
-        [],
-        (),
-        (),
-        (x, *attns[:-2], *weights[:-2]),
-        "product",
-        (head_count - 2) * flops,
-        24,
-    )
     resid, own, last_own = call(
         own_kernel,
         (
@@ -458,9 +449,9 @@
         [],
         (lax.axis_index("head").reshape(1),),
         (),
-        (resid, attns[-2], *weights[-2:]),
+        (weights[-1], x, *attns[:-1], *weights[:-1]),
         "own",
-        flops,
+        (head_count - 1) * flops,
         24,
     )
     out = call(

time: 22 us -> 22 us (level)
    pallas_call x7 -> x6, Pallas kernels: 5.44 us -> 5.3 us  [call(): pl.pallas_call(kernel, out_shape=outs, in_specs=[IN_SMEM] * len(scalars)...]
  transfers between devices with their start and end apart: 9 -> 9, of which waited for: 3 -> 3; matrix products, arithmetic and copies ran while one was open for 0% -> 0% of each run, Pallas kernels for 19% -> 18%
where the time goes in v9:
time: 22 us; the launch traced here: 21.8 us
  starting transfers between devices  10.5 us (48%)
  waiting for transfers between devices  5.91 us (27%)
  Pallas kernels  5.3 us (24%)
    ppermute x3, starting transfers between devices, local(): lax.ppermute(kvp, 'seq', within(s))  5.56 us
    pallas_call x6, Pallas kernels, call(): pl.pallas_call(kernel, out_shape=outs, in_specs=[IN_SMEM] * len(scalars)...  5.3 us
    ppermute x6, starting transfers between devices, to(): return lax.ppermute(array, 'head', paths[r])  4.93 us
    ppermute x6, waiting for transfers between devices, to(): return lax.ppermute(array, 'head', paths[r])  4.39 us
    ppermute x3, waiting for transfers between devices, local(): lax.ppermute(kvp, 'seq', within(s))  1.52 us
  transfers between devices with their start and end apart: 9, of which 3 were waited for; matrix products, arithmetic and copies ran while one was open for 0% of the time, Pallas kernels for 18%

profile of v9, /device:TPU:0, one launch (start us, length us, event | category | flops | bytes accessed | tf_op | source)
XLA Modules:
  0.0 21.8 jit_solution(12891523504580539520)
XLA Ops:
  0.0 0.0 copy-start.8
  0.0 3.0 %collective-permute-start = (bf16[192,768]{1,0:T(8,128)(2,1)}, bf16[192,768]{1,0:T(8,128)(2,1)S(1)}, u32[]{:S(2)}, u32[]{:S(2)}) collective-permute-start(bf16[192,768]{1,0:T(8,128)(2,1)} %refs_4_.1), channel_id=1, source_target_pairs={{0,2},{1,3},{2,0},{3,1},{4,6},{5,7},{6,4},{7,5},{8,10},{9,11},{10,... | collective-permute-start | bytes 884744 | tf_op jit(solution)/shard_map/ppermute | solution.py:334
  3.1 0.0 copy-done.1
  3.1 0.0 copy-done.3
  3.1 0.0 copy-done.5
  3.1 0.0 copy-done
  3.1 0.0 copy-start.4
  3.1 0.0 copy-start.6
  3.1 0.7 %project.1 = (bf16[512,384]{1,0:T(8,128)(2,1)S(1)}, bf16[240,128]{1,0:T(8,128)(2,1)S(1)}) custom-call(s32[3]{0:T(128)S(1)} %copy-done.3, s32[3]{0:T(128)S(1)} %copy-done.5, bf16[512,768]{1,0:T(8,128)(2,1)S(1)} %copy-done, bf16[3,192,768]{2,1,0:T(8,128)(2,1)S(1)} %bitcast.5, s32[8,128]{1,0:T(8,128)S(1)} %lanes.1.lanes_ref), custom_call_target="tpu_custom_call" | custom-call | flops 301989888 | bytes 4194304 | tf_op jit(solution)/shard_map/project/pallas_call | solution.py:304
  3.8 1.6 %collective-permute-start.2 = (bf16[240,128]{1,0:T(8,128)(2,1)S(1)}, bf16[240,128]{1,0:T(8,128)(2,1)S(1)}, u32[]{:S(2)}, u32[]{:S(2)}) collective-permute-start(bf16[240,128]{1,0:T(8,128)(2,1)S(1)} %get-tuple-element.22.rest_0_.rest_4_), channel_id=1, source_target_pairs={{0,4},{4,8},{8,12},{12,0},{1,5},{5,9},{9,13},{13,1},{2,6},{6,10},{... | collective-permute-start | bytes 184328 | tf_op jit(solution)/shard_map/ppermute | solution.py:379
  5.4 2.6 %collective-permute-start.3 = (bf16[240,128]{1,0:T(8,128)(2,1)S(1)}, bf16[240,128]{1,0:T(8,128)(2,1)S(1)}, u32[]{:S(2)}, u32[]{:S(2)}) collective-permute-start(bf16[240,128]{1,0:T(8,128)(2,1)S(1)} %get-tuple-element.22.rest_0_.rest_4_), channel_id=1, source_target_pairs={{0,8},{4,12},{8,0},{12,4},{1,9},{5,13},{9,1},{13,5},{2,10},{6,14},... | collective-permute-start | bytes 184328 | tf_op jit(solution)/shard_map/ppermute | solution.py:379
  8.0 1.3 %collective-permute-start.4 = (bf16[240,128]{1,0:T(8,128)(2,1)S(1)}, bf16[240,128]{1,0:T(8,128)(2,1)S(1)}, u32[]{:S(2)}, u32[]{:S(2)}) collective-permute-start(bf16[240,128]{1,0:T(8,128)(2,1)S(1)} %get-tuple-element.22.rest_0_.rest_4_), channel_id=1, source_target_pairs={{0,12},{4,0},{8,4},{12,8},{1,13},{5,1},{9,5},{13,9},{2,14},{6,2},{... | collective-permute-start | bytes 184328 | tf_op jit(solution)/shard_map/ppermute | solution.py:379
  9.3 0.0 copy-done.7
  9.3 0.0 copy-done.8
  9.3 1.7 %near.1 = (f32[768,128]{1,0:T(8,128)S(1)}, f32[240,128]{1,0:T(8,128)S(1)}, f32[240,128]{1,0:T(8,128)S(1)}, bf16[240,128]{1,0:T(8,128)(2,1)S(1)}, f32[2,192]{1,0:T(2,128)S(1)}) custom-call(s32[3]{0:T(128)} %mo_from.5, s32[3]{0:T(128)} %fo_from.5, bf16[512,384]{1,0:T(8,128)(2,1)S(1)} %get-tuple-element.17.kv_ref, bf16[512,768]{1,0:T(8,128)(2,1)S(1)} %copy-done, ...), custom_call_target="tpu_custom_call" | custom-call | flops 536870912 | bytes 4194304 | tf_op jit(solution)/shard_map/near/pallas_call | solution.py:304
  11.1 0.0 collective-permute-done.2.rest_1_.rest_5_
  11.1 1.5 %collective-permute-done.3.rest_2_.rest_6_ = bf16[240,128]{1,0:T(8,128)(2,1)S(1)} collective-permute-done((bf16[240,128]{1,0:T(8,128)(2,1)S(1)}, bf16[240,128]{1,0:T(8,128)(2,1)S(1)}, u32[]{:S(2)}, u32[]{:S(2)}) %collective-permute-start.3) | collective-permute-done | bytes 61472 | tf_op jit(solution)/shard_map/ppermute | solution.py:379
  12.6 0.0 collective-permute-done.4.rest_3_.rest_7_
  12.6 0.7 %merge.1.refs_1_ = bf16[768,128]{1,0:T(8,128)(2,1)S(1)} custom-call(s32[3]{0:T(128)S(1)} %copy-done.4, s32[3]{0:T(128)S(1)} %copy-done.6, f32[768,128]{1,0:T(8,128)S(1)} %get-tuple-element.18.near_ref, bf16[240,128]{1,0:T(8,128)(2,1)S(1)} %get-tuple-element.19.qp_ref, f32[240,128]{1,0:T(8,128)S(1)} %get-tuple-element.20.am_ref, ...), custom_call_target="tpu_custom_call" | custom-call | flops 536870912 | bytes 4194304 | tf_op jit(solution)/shard_map/merge/pallas_call | solution.py:304
  13.3 1.3 %collective-permute-start.6 = (bf16[768,128]{1,0:T(8,128)(2,1)S(1)}, bf16[768,128]{1,0:T(8,128)(2,1)S(1)}, u32[]{:S(2)}, u32[]{:S(2)}) collective-permute-start(bf16[768,128]{1,0:T(8,128)(2,1)S(1)} %merge.1.refs_1_), channel_id=1, source_target_pairs={{0,2},{1,3},{2,0},{3,1},{4,6},{5,7},{6,4},{7,5},{8,10},{9,11},{10,... | collective-permute-start | bytes 589832 | tf_op jit(solution)/shard_map/ppermute | solution.py:334
  14.7 0.0 collective-permute-start.7
  14.7 0.0 collective-permute-done.refs_6_
  14.7 0.5 %collective-permute-start.1 = (bf16[192,768]{1,0:T(8,128)(2,1)S(1)}, bf16[192,768]{1,0:T(8,128)(2,1)S(1)}, u32[]{:S(2)}, u32[]{:S(2)}) collective-permute-start(bf16[192,768]{1,0:T(8,128)(2,1)S(1)} %collective-permute-done.refs_6_), channel_id=1, source_target_pairs={{0,1},{1,0},{2,3},{3,2},{4,5},{5,4},{6,7},{7,6},{8,9},{9,8},{10,11... | collective-permute-start | bytes 884744 | tf_op jit(solution)/shard_map/ppermute | solution.py:334
  15.2 0.1 collective-permute-start.5
  15.3 3.8 %collective-permute-done.6.refs_3_ = bf16[768,128]{1,0:T(8,128)(2,1)S(1)} collective-permute-done((bf16[768,128]{1,0:T(8,128)(2,1)S(1)}, bf16[768,128]{1,0:T(8,128)(2,1)S(1)}, u32[]{:S(2)}, u32[]{:S(2)}) %collective-permute-start.6) | collective-permute-done | bytes 196640 | tf_op jit(solution)/shard_map/ppermute | solution.py:334
  19.1 0.0 collective-permute-start.8
  19.1 0.0 collective-permute-done.5.refs_2_
  19.1 0.0 collective-permute-done.7.refs_5_
  19.1 0.0 collective-permute-done.1.last_ref.w_ref
  19.1 0.8 %own.1 = (f32[512,768]{1,0:T(8,128)S(1)}, f32[512,192]{1,0:T(8,128)S(1)}, bf16[192,192]{1,0:T(8,128)(2,1)S(1)}) custom-call(s32[1]{0:T(128)} %bitcast.place, bf16[192,768]{1,0:T(8,128)(2,1)S(1)} %collective-permute-done.1.last_ref.w_ref, bf16[512,768]{1,0:T(8,128)(2,1)S(1)} %copy-done, bf16[768,128]{1,0:T(8,128)(2,1)S(1)} %merge.1.refs_1_, ...), custom_call_target="tpu_custom_call" | custom-call | flops 452984832 | bytes 4194304 | tf_op jit(solution)/shard_map/own/pallas_call | solution.py:304
  19.9 0.6 %collective-permute-done.8.attn_ref = bf16[768,128]{1,0:T(8,128)(2,1)S(1)} collective-permute-done((bf16[768,128]{1,0:T(8,128)(2,1)S(1)}, bf16[768,128]{1,0:T(8,128)(2,1)S(1)}, u32[]{:S(2)}, u32[]{:S(2)}) %collective-permute-start.8) | collective-permute-done | bytes 196640 | tf_op jit(solution)/shard_map/ppermute | solution.py:334
  20.5 1.3 %output.1 = bf16[192,512]{1,0:T(8,128)(2,1)} custom-call(f32[512,768]{1,0:T(8,128)S(1)} %get-tuple-element.23.x_ref, f32[512,192]{1,0:T(8,128)S(1)} %get-tuple-element.24.own_ref, bf16[192,192]{1,0:T(8,128)(2,1)S(1)} %get-tuple-element.25.last_own_ref, f32[2,192]{1,0:T(2,128)S(1)} %get-tuple-element.26.gb_ref, ...), custom_call_target="tpu_custom_call" | custom-call | flops 150994944 | bytes 4194304 | tf_op jit(solution)/shard_map/output/pallas_call | solution.py:304
  (10 shorter events, 0.0 us)
Async XLA Ops:
  0.0 3.1 %copy-start.1 = (bf16[3,768,192]{1,2,0:T(8,128)(2,1)S(1)}, bf16[3,768,192]{1,2,0:T(8,128)(2,1)}, u32[]{:S(2)}) copy-start(bf16[3,768,192]{1,2,0:T(8,128)(2,1)} %param.8) | copy-start | bytes 2654212
  0.0 3.1 %copy-start.3 = (s32[3]{0:T(128)S(1)}, s32[3]{0:T(128)}, u32[]{:S(2)}) copy-start(s32[3]{0:T(128)} %mo_from.5) | copy-start | bytes 40
  0.0 3.1 %copy-start.5 = (s32[3]{0:T(128)S(1)}, s32[3]{0:T(128)}, u32[]{:S(2)}) copy-start(s32[3]{0:T(128)} %fo_from.5) | copy-start | bytes 40
  0.0 3.1 %copy-start = (bf16[512,768]{1,0:T(8,128)(2,1)S(1)}, bf16[512,768]{1,0:T(8,128)(2,1)}, u32[]{:S(2)}) copy-start(bf16[512,768]{1,0:T(8,128)(2,1)} %refs_0_.1) | copy-start | bytes 2359300
  0.0 9.3 %copy-start.7 = (f32[192]{0:T(256)S(1)}, f32[192]{0:T(256)}, u32[]{:S(2)}) copy-start(f32[192]{0:T(256)} %param.10) | copy-start | bytes 2308
  0.0 9.3 %copy-start.8 = (f32[192]{0:T(256)S(1)}, f32[192]{0:T(256)}, u32[]{:S(2)}) copy-start(f32[192]{0:T(256)} %param.11) | copy-start | bytes 2308
  0.0 14.6 %collective-permute-start = (bf16[192,768]{1,0:T(8,128)(2,1)}, bf16[192,768]{1,0:T(8,128)(2,1)S(1)}, u32[]{:S(2)}, u32[]{:S(2)}) collective-permute-start(bf16[192,768]{1,0:T(8,128)(2,1)} %refs_4_.1), channel_id=1, source_target_pairs={{0,2},{1,3},{2,0},{3,1},{4,6},{5,7},{6,4},{7,5},{8,10},{9,11},{10,... | collective-permute-start | bytes 884744 | tf_op jit(solution)/shard_map/ppermute | solution.py:334
  3.1 9.5 %copy-start.4 = (s32[3]{0:T(128)S(1)}, s32[3]{0:T(128)}, u32[]{:S(2)}) copy-start(s32[3]{0:T(128)} %mo_from.5) | copy-start | bytes 40
  3.1 9.5 %copy-start.6 = (s32[3]{0:T(128)S(1)}, s32[3]{0:T(128)}, u32[]{:S(2)}) copy-start(s32[3]{0:T(128)} %fo_from.5) | copy-start | bytes 40
  3.8 7.3 %collective-permute-start.2 = (bf16[240,128]{1,0:T(8,128)(2,1)S(1)}, bf16[240,128]{1,0:T(8,128)(2,1)S(1)}, u32[]{:S(2)}, u32[]{:S(2)}) collective-permute-start(bf16[240,128]{1,0:T(8,128)(2,1)S(1)} %get-tuple-element.22.rest_0_.rest_4_), channel_id=1, source_target_pairs={{0,4},{4,8},{8,12},{12,0},{1,5},{5,9},{9,13},{13,1},{2,6},{6,10},{... | collective-permute-start | bytes 184328 | tf_op jit(solution)/shard_map/ppermute | solution.py:379
  5.4 7.2 %collective-permute-start.3 = (bf16[240,128]{1,0:T(8,128)(2,1)S(1)}, bf16[240,128]{1,0:T(8,128)(2,1)S(1)}, u32[]{:S(2)}, u32[]{:S(2)}) collective-permute-start(bf16[240,128]{1,0:T(8,128)(2,1)S(1)} %get-tuple-element.22.rest_0_.rest_4_), channel_id=1, source_target_pairs={{0,8},{4,12},{8,0},{12,4},{1,9},{5,13},{9,1},{13,5},{2,10},{6,14},... | collective-permute-start | bytes 184328 | tf_op jit(solution)/shard_map/ppermute | solution.py:379
  8.0 4.6 %collective-permute-start.4 = (bf16[240,128]{1,0:T(8,128)(2,1)S(1)}, bf16[240,128]{1,0:T(8,128)(2,1)S(1)}, u32[]{:S(2)}, u32[]{:S(2)}) collective-permute-start(bf16[240,128]{1,0:T(8,128)(2,1)S(1)} %get-tuple-element.22.rest_0_.rest_4_), channel_id=1, source_target_pairs={{0,12},{4,0},{8,4},{12,8},{1,13},{5,1},{9,5},{13,9},{2,14},{6,2},{... | collective-permute-start | bytes 184328 | tf_op jit(solution)/shard_map/ppermute | solution.py:379
  9.3 5.3 %copy-start.2 = (bf16[192,768]{1,0:T(8,128)(2,1)S(1)}, bf16[192,768]{1,0:T(8,128)(2,1)}, u32[]{:S(2)}) copy-start(bf16[192,768]{1,0:T(8,128)(2,1)} %refs_4_.1) | copy-start | bytes 884740
  13.3 5.7 %collective-permute-start.6 = (bf16[768,128]{1,0:T(8,128)(2,1)S(1)}, bf16[768,128]{1,0:T(8,128)(2,1)S(1)}, u32[]{:S(2)}, u32[]{:S(2)}) collective-permute-start(bf16[768,128]{1,0:T(8,128)(2,1)S(1)} %merge.1.refs_1_), channel_id=1, source_target_pairs={{0,2},{1,3},{2,0},{3,1},{4,6},{5,7},{6,4},{7,5},{8,10},{9,11},{10,... | collective-permute-start | bytes 589832 | tf_op jit(solution)/shard_map/ppermute | solution.py:334
  14.7 4.4 %collective-permute-start.7 = (bf16[192,768]{1,0:T(8,128)(2,1)S(1)}, bf16[192,768]{1,0:T(8,128)(2,1)S(1)}, u32[]{:S(2)}, u32[]{:S(2)}) collective-permute-start(bf16[192,768]{1,0:T(8,128)(2,1)S(1)} %copy-done.2), channel_id=1, source_target_pairs={{0,1},{1,0},{2,3},{3,2},{4,5},{5,4},{6,7},{7,6},{8,9},{9,8},{10,11... | collective-permute-start | bytes 884744 | tf_op jit(solution)/shard_map/ppermute | solution.py:334
  14.7 4.4 %collective-permute-start.1 = (bf16[192,768]{1,0:T(8,128)(2,1)S(1)}, bf16[192,768]{1,0:T(8,128)(2,1)S(1)}, u32[]{:S(2)}, u32[]{:S(2)}) collective-permute-start(bf16[192,768]{1,0:T(8,128)(2,1)S(1)} %collective-permute-done.refs_6_), channel_id=1, source_target_pairs={{0,1},{1,0},{2,3},{3,2},{4,5},{5,4},{6,7},{7,6},{8,9},{9,8},{10,11... | collective-permute-start | bytes 884744 | tf_op jit(solution)/shard_map/ppermute | solution.py:334
  15.2 3.9 %collective-permute-start.5 = (bf16[768,128]{1,0:T(8,128)(2,1)S(1)}, bf16[768,128]{1,0:T(8,128)(2,1)S(1)}, u32[]{:S(2)}, u32[]{:S(2)}) collective-permute-start(bf16[768,128]{1,0:T(8,128)(2,1)S(1)} %merge.1.refs_1_), channel_id=1, source_target_pairs={{0,1},{1,0},{2,3},{3,2},{4,5},{5,4},{6,7},{7,6},{8,9},{9,8},{10,11... | collective-permute-start | bytes 589832 | tf_op jit(solution)/shard_map/ppermute | solution.py:334
  19.1 1.4 %collective-permute-start.8 = (bf16[768,128]{1,0:T(8,128)(2,1)S(1)}, bf16[768,128]{1,0:T(8,128)(2,1)S(1)}, u32[]{:S(2)}, u32[]{:S(2)}) collective-permute-start(bf16[768,128]{1,0:T(8,128)(2,1)S(1)} %collective-permute-done.6.refs_3_), channel_id=1, source_target_pairs={{0,1},{1,0},{2,3},{3,2},{4,5},{5,4},{6,7},{7,6},{8,9},{9,8},{10,11... | collective-permute-start | bytes 589832 | tf_op jit(solution)/shard_map/ppermute | solution.py:334

commit v10 on v8

--- a/solution.py
+++ b/solution.py
@@ -282,8 +282,9 @@
             third = swap(third.astype(f32)).astype(bf16)
         attn = jnp.concatenate([attn_ref[at], third[:, :HALF]], axis=1)
         resid = x_ref[at] + jnp.dot(attn, w_ref[...], preferred_element_type=f32)
-        mean = jnp.sum(resid, axis=1, keepdims=True) / width
-        var = jnp.sum(resid * resid, axis=1, keepdims=True) / width - mean * mean
+        tiles = [resid[:, j : j + LANES] for j in range(0, width, LANES)]
+        mean = jnp.sum(sum(tiles), axis=1, keepdims=True) / width
+        var = jnp.sum(sum(t * t for t in tiles), axis=1, keepdims=True) / width - mean * mean
         mine = own_ref[at] + jnp.dot(attn, last_own_ref[...], preferred_element_type=f32)
         normed = (mine - mean) * lax.rsqrt(var + epsilon) * gb_ref[0:1] + gb_ref[1:2]
         out_ref[:, at] = normed.astype(bf16).T

time: 22 us -> 22 us (level)
  no operation moved by 1% of the time
where the time goes in v10:
time: 22 us; the launch traced here: 21.8 us
  starting transfers between devices  10.5 us (48%)
  waiting for transfers between devices  5.75 us (26%)
  Pallas kernels  5.44 us (25%)
    ppermute x3, starting transfers between devices, local(): lax.ppermute(kvp, 'seq', within(s))  5.56 us
    pallas_call x7, Pallas kernels, call(): pl.pallas_call(kernel, out_shape=outs, in_specs=[IN_SMEM] * len(scalars)...  5.44 us
    ppermute x6, starting transfers between devices, to(): return lax.ppermute(array, 'head', paths[r])  4.93 us
    ppermute x6, waiting for transfers between devices, to(): return lax.ppermute(array, 'head', paths[r])  4.23 us
    ppermute x3, waiting for transfers between devices, local(): lax.ppermute(kvp, 'seq', within(s))  1.52 us
  transfers between devices with their start and end apart: 9, of which 3 were waited for; matrix products, arithmetic and copies ran while one was open for 0% of the time, Pallas kernels for 19%

profile of v10, /device:TPU:0, one launch (start us, length us, event | category | flops | bytes accessed | tf_op | source)
XLA Modules:
  0.0 21.8 jit_solution(3832964413320222382)
XLA Ops:
  0.0 0.0 copy-start.8
  0.0 3.0 %collective-permute-start.6 = (bf16[192,768]{1,0:T(8,128)(2,1)}, bf16[192,768]{1,0:T(8,128)(2,1)S(1)}, u32[]{:S(2)}, u32[]{:S(2)}) collective-permute-start(bf16[192,768]{1,0:T(8,128)(2,1)} %rest_2_.1), channel_id=1, source_target_pairs={{0,2},{1,3},{2,0},{3,1},{4,6},{5,7},{6,4},{7,5},{8,10},{9,11},{10,... | collective-permute-start | bytes 884744 | tf_op jit(solution)/shard_map/ppermute | solution.py:333
  3.1 0.0 copy-done.1
  3.1 0.0 copy-done.3
  3.1 0.0 copy-done.5
  3.1 0.0 copy-done
  3.1 0.0 copy-start.4
  3.1 0.0 copy-start.6
  3.1 0.7 %project.1 = (bf16[512,384]{1,0:T(8,128)(2,1)S(1)}, bf16[240,128]{1,0:T(8,128)(2,1)S(1)}) custom-call(s32[3]{0:T(128)S(1)} %copy-done.3, s32[3]{0:T(128)S(1)} %copy-done.5, bf16[512,768]{1,0:T(8,128)(2,1)S(1)} %copy-done, bf16[3,192,768]{2,1,0:T(8,128)(2,1)S(1)} %bitcast.5, s32[8,128]{1,0:T(8,128)S(1)} %lanes.1.lanes_ref), custom_call_target="tpu_custom_call" | custom-call | flops 301989888 | bytes 4194304 | tf_op jit(solution)/shard_map/project/pallas_call | solution.py:303
  3.8 1.6 %collective-permute-start = (bf16[240,128]{1,0:T(8,128)(2,1)S(1)}, bf16[240,128]{1,0:T(8,128)(2,1)S(1)}, u32[]{:S(2)}, u32[]{:S(2)}) collective-permute-start(bf16[240,128]{1,0:T(8,128)(2,1)S(1)} %get-tuple-element.21.rest_0_.rest_4_), channel_id=1, source_target_pairs={{0,4},{4,8},{8,12},{12,0},{1,5},{5,9},{9,13},{13,1},{2,6},{6,10},{... | collective-permute-start | bytes 184328 | tf_op jit(solution)/shard_map/ppermute | solution.py:378
  5.4 2.6 %collective-permute-start.1 = (bf16[240,128]{1,0:T(8,128)(2,1)S(1)}, bf16[240,128]{1,0:T(8,128)(2,1)S(1)}, u32[]{:S(2)}, u32[]{:S(2)}) collective-permute-start(bf16[240,128]{1,0:T(8,128)(2,1)S(1)} %get-tuple-element.21.rest_0_.rest_4_), channel_id=1, source_target_pairs={{0,8},{4,12},{8,0},{12,4},{1,9},{5,13},{9,1},{13,5},{2,10},{6,14},... | collective-permute-start | bytes 184328 | tf_op jit(solution)/shard_map/ppermute | solution.py:378
  8.0 1.3 %collective-permute-start.2 = (bf16[240,128]{1,0:T(8,128)(2,1)S(1)}, bf16[240,128]{1,0:T(8,128)(2,1)S(1)}, u32[]{:S(2)}, u32[]{:S(2)}) collective-permute-start(bf16[240,128]{1,0:T(8,128)(2,1)S(1)} %get-tuple-element.21.rest_0_.rest_4_), channel_id=1, source_target_pairs={{0,12},{4,0},{8,4},{12,8},{1,13},{5,1},{9,5},{13,9},{2,14},{6,2},{... | collective-permute-start | bytes 184328 | tf_op jit(solution)/shard_map/ppermute | solution.py:378
  9.3 1.7 %near.1 = (f32[768,128]{1,0:T(8,128)S(1)}, f32[240,128]{1,0:T(8,128)S(1)}, f32[240,128]{1,0:T(8,128)S(1)}, bf16[240,128]{1,0:T(8,128)(2,1)S(1)}, f32[2,192]{1,0:T(2,128)S(1)}) custom-call(s32[3]{0:T(128)} %mo_from.5, s32[3]{0:T(128)} %fo_from.5, bf16[512,384]{1,0:T(8,128)(2,1)S(1)} %get-tuple-element.16.kv_ref, bf16[512,768]{1,0:T(8,128)(2,1)S(1)} %copy-done, ...), custom_call_target="tpu_custom_call" | custom-call | flops 536870912 | bytes 4194304 | tf_op jit(solution)/shard_map/near/pallas_call | solution.py:303
  11.1 0.0 collective-permute-done.rest_1_.rest_5_
  11.1 1.5 %collective-permute-done.1.rest_2_.rest_6_ = bf16[240,128]{1,0:T(8,128)(2,1)S(1)} collective-permute-done((bf16[240,128]{1,0:T(8,128)(2,1)S(1)}, bf16[240,128]{1,0:T(8,128)(2,1)S(1)}, u32[]{:S(2)}, u32[]{:S(2)}) %collective-permute-start.1) | collective-permute-done | bytes 61472 | tf_op jit(solution)/shard_map/ppermute | solution.py:378
  12.6 0.0 collective-permute-done.2.rest_3_.rest_7_
  12.6 0.0 copy-done.4
  12.6 0.7 %merge.1.rest_0_ = bf16[768,128]{1,0:T(8,128)(2,1)S(1)} custom-call(s32[3]{0:T(128)S(1)} %copy-done.4, s32[3]{0:T(128)S(1)} %copy-done.6, f32[768,128]{1,0:T(8,128)S(1)} %get-tuple-element.17.near_ref, bf16[240,128]{1,0:T(8,128)(2,1)S(1)} %get-tuple-element.18.qp_ref, f32[240,128]{1,0:T(8,128)S(1)} %get-tuple-element.19.am_ref, ...), custom_call_target="tpu_custom_call" | custom-call | flops 536870912 | bytes 4194304 | tf_op jit(solution)/shard_map/merge/pallas_call | solution.py:303
  13.3 1.3 %collective-permute-start.5 = (bf16[768,128]{1,0:T(8,128)(2,1)S(1)}, bf16[768,128]{1,0:T(8,128)(2,1)S(1)}, u32[]{:S(2)}, u32[]{:S(2)}) collective-permute-start(bf16[768,128]{1,0:T(8,128)(2,1)S(1)} %merge.1.rest_0_), channel_id=1, source_target_pairs={{0,2},{1,3},{2,0},{3,1},{4,6},{5,7},{6,4},{7,5},{8,10},{9,11},{10,... | collective-permute-start | bytes 589832 | tf_op jit(solution)/shard_map/ppermute | solution.py:333
  14.7 0.0 collective-permute-start.4
  14.7 0.0 collective-permute-done.6.w_ref
  14.7 0.5 %collective-permute-start.7 = (bf16[192,768]{1,0:T(8,128)(2,1)S(1)}, bf16[192,768]{1,0:T(8,128)(2,1)S(1)}, u32[]{:S(2)}, u32[]{:S(2)}) collective-permute-start(bf16[192,768]{1,0:T(8,128)(2,1)S(1)} %collective-permute-done.6.w_ref), channel_id=1, source_target_pairs={{0,1},{1,0},{2,3},{3,2},{4,5},{5,4},{6,7},{7,6},{8,9},{9,8},{10,11... | collective-permute-start | bytes 884744 | tf_op jit(solution)/shard_map/ppermute | solution.py:333
  15.2 0.1 collective-permute-start.3
  15.3 3.8 %collective-permute-done.5.attn_ref = bf16[768,128]{1,0:T(8,128)(2,1)S(1)} collective-permute-done((bf16[768,128]{1,0:T(8,128)(2,1)S(1)}, bf16[768,128]{1,0:T(8,128)(2,1)S(1)}, u32[]{:S(2)}, u32[]{:S(2)}) %collective-permute-start.5) | collective-permute-done | bytes 196640 | tf_op jit(solution)/shard_map/ppermute | solution.py:333
  19.1 0.0 collective-permute-start.8
  19.1 0.0 collective-permute-done.3.rest_1_
  19.1 0.0 collective-permute-done.4.rest_3_
  19.1 0.6 %product.1.x_ref = f32[512,768]{1,0:T(8,128)S(1)} custom-call(bf16[512,768]{1,0:T(8,128)(2,1)S(1)} %copy-done, bf16[768,128]{1,0:T(8,128)(2,1)S(1)} %merge.1.rest_0_, bf16[768,128]{1,0:T(8,128)(2,1)S(1)} %collective-permute-done.3.rest_1_, bf16[192,768]{1,0:T(8,128)(2,1)S(1)} %copy-done.2, bf16[192,768]{1,0:T(8,128)(2,1)S(1)} %collective-permute-done.4.rest_3_), custom_call_target="tpu_custom_call" | custom-call | flops 301989888 | bytes 4194304 | tf_op jit(solution)/shard_map/product/pallas_call | solution.py:303
  19.7 0.0 collective-permute-done.7.last_ref.w_ref
  19.7 0.4 %own.1 = (f32[512,768]{1,0:T(8,128)S(1)}, f32[512,192]{1,0:T(8,128)S(1)}, bf16[192,192]{1,0:T(8,128)(2,1)S(1)}) custom-call(s32[1]{0:T(128)} %bitcast.place, f32[512,768]{1,0:T(8,128)S(1)} %product.1.x_ref, bf16[768,128]{1,0:T(8,128)(2,1)S(1)} %collective-permute-done.5.attn_ref, bf16[192,768]{1,0:T(8,128)(2,1)S(1)} %collective-permute-done.6.w_ref, ...), custom_call_target="tpu_custom_call" | custom-call | flops 150994944 | bytes 4194304 | tf_op jit(solution)/shard_map/own/pallas_call | solution.py:303
  20.1 0.4 %collective-permute-done.8.attn_ref = bf16[768,128]{1,0:T(8,128)(2,1)S(1)} collective-permute-done((bf16[768,128]{1,0:T(8,128)(2,1)S(1)}, bf16[768,128]{1,0:T(8,128)(2,1)S(1)}, u32[]{:S(2)}, u32[]{:S(2)}) %collective-permute-start.8) | collective-permute-done | bytes 196640 | tf_op jit(solution)/shard_map/ppermute | solution.py:333
  20.5 1.3 %output.1 = bf16[192,512]{1,0:T(8,128)(2,1)} custom-call(f32[512,768]{1,0:T(8,128)S(1)} %get-tuple-element.23.x_ref, f32[512,192]{1,0:T(8,128)S(1)} %get-tuple-element.24.own_ref, bf16[192,192]{1,0:T(8,128)(2,1)S(1)} %get-tuple-element.25.last_own_ref, f32[2,192]{1,0:T(2,128)S(1)} %get-tuple-element.26.gb_ref, ...), custom_call_target="tpu_custom_call" | custom-call | flops 150994944 | bytes 4194304 | tf_op jit(solution)/shard_map/output/pallas_call | solution.py:303
  (11 shorter events, 0.0 us)
Async XLA Ops:
  0.0 3.1 %copy-start.1 = (bf16[3,768,192]{1,2,0:T(8,128)(2,1)S(1)}, bf16[3,768,192]{1,2,0:T(8,128)(2,1)}, u32[]{:S(2)}) copy-start(bf16[3,768,192]{1,2,0:T(8,128)(2,1)} %param.8) | copy-start | bytes 2654212
  0.0 3.1 %copy-start.3 = (s32[3]{0:T(128)S(1)}, s32[3]{0:T(128)}, u32[]{:S(2)}) copy-start(s32[3]{0:T(128)} %mo_from.5) | copy-start | bytes 40
  0.0 3.1 %copy-start.5 = (s32[3]{0:T(128)S(1)}, s32[3]{0:T(128)}, u32[]{:S(2)}) copy-start(s32[3]{0:T(128)} %fo_from.5) | copy-start | bytes 40
  0.0 3.1 %copy-start = (bf16[512,768]{1,0:T(8,128)(2,1)S(1)}, bf16[512,768]{1,0:T(8,128)(2,1)}, u32[]{:S(2)}) copy-start(bf16[512,768]{1,0:T(8,128)(2,1)} %x_ref.5) | copy-start | bytes 2359300
  0.0 9.3 %copy-start.7 = (f32[192]{0:T(256)S(1)}, f32[192]{0:T(256)}, u32[]{:S(2)}) copy-start(f32[192]{0:T(256)} %param.10) | copy-start | bytes 2308
  0.0 9.3 %copy-start.8 = (f32[192]{0:T(256)S(1)}, f32[192]{0:T(256)}, u32[]{:S(2)}) copy-start(f32[192]{0:T(256)} %param.11) | copy-start | bytes 2308
  0.0 14.6 %collective-permute-start.6 = (bf16[192,768]{1,0:T(8,128)(2,1)}, bf16[192,768]{1,0:T(8,128)(2,1)S(1)}, u32[]{:S(2)}, u32[]{:S(2)}) collective-permute-start(bf16[192,768]{1,0:T(8,128)(2,1)} %rest_2_.1), channel_id=1, source_target_pairs={{0,2},{1,3},{2,0},{3,1},{4,6},{5,7},{6,4},{7,5},{8,10},{9,11},{10,... | collective-permute-start | bytes 884744 | tf_op jit(solution)/shard_map/ppermute | solution.py:333
  3.1 9.5 %copy-start.4 = (s32[3]{0:T(128)S(1)}, s32[3]{0:T(128)}, u32[]{:S(2)}) copy-start(s32[3]{0:T(128)} %mo_from.5) | copy-start | bytes 40
  3.1 9.5 %copy-start.6 = (s32[3]{0:T(128)S(1)}, s32[3]{0:T(128)}, u32[]{:S(2)}) copy-start(s32[3]{0:T(128)} %fo_from.5) | copy-start | bytes 40
  3.8 7.3 %collective-permute-start = (bf16[240,128]{1,0:T(8,128)(2,1)S(1)}, bf16[240,128]{1,0:T(8,128)(2,1)S(1)}, u32[]{:S(2)}, u32[]{:S(2)}) collective-permute-start(bf16[240,128]{1,0:T(8,128)(2,1)S(1)} %get-tuple-element.21.rest_0_.rest_4_), channel_id=1, source_target_pairs={{0,4},{4,8},{8,12},{12,0},{1,5},{5,9},{9,13},{13,1},{2,6},{6,10},{... | collective-permute-start | bytes 184328 | tf_op jit(solution)/shard_map/ppermute | solution.py:378
  5.4 7.2 %collective-permute-start.1 = (bf16[240,128]{1,0:T(8,128)(2,1)S(1)}, bf16[240,128]{1,0:T(8,128)(2,1)S(1)}, u32[]{:S(2)}, u32[]{:S(2)}) collective-permute-start(bf16[240,128]{1,0:T(8,128)(2,1)S(1)} %get-tuple-element.21.rest_0_.rest_4_), channel_id=1, source_target_pairs={{0,8},{4,12},{8,0},{12,4},{1,9},{5,13},{9,1},{13,5},{2,10},{6,14},... | collective-permute-start | bytes 184328 | tf_op jit(solution)/shard_map/ppermute | solution.py:378
  8.0 4.6 %collective-permute-start.2 = (bf16[240,128]{1,0:T(8,128)(2,1)S(1)}, bf16[240,128]{1,0:T(8,128)(2,1)S(1)}, u32[]{:S(2)}, u32[]{:S(2)}) collective-permute-start(bf16[240,128]{1,0:T(8,128)(2,1)S(1)} %get-tuple-element.21.rest_0_.rest_4_), channel_id=1, source_target_pairs={{0,12},{4,0},{8,4},{12,8},{1,13},{5,1},{9,5},{13,9},{2,14},{6,2},{... | collective-permute-start | bytes 184328 | tf_op jit(solution)/shard_map/ppermute | solution.py:378
  9.3 5.3 %copy-start.2 = (bf16[192,768]{1,0:T(8,128)(2,1)S(1)}, bf16[192,768]{1,0:T(8,128)(2,1)}, u32[]{:S(2)}) copy-start(bf16[192,768]{1,0:T(8,128)(2,1)} %rest_2_.1) | copy-start | bytes 884740
  13.3 5.7 %collective-permute-start.5 = (bf16[768,128]{1,0:T(8,128)(2,1)S(1)}, bf16[768,128]{1,0:T(8,128)(2,1)S(1)}, u32[]{:S(2)}, u32[]{:S(2)}) collective-permute-start(bf16[768,128]{1,0:T(8,128)(2,1)S(1)} %merge.1.rest_0_), channel_id=1, source_target_pairs={{0,2},{1,3},{2,0},{3,1},{4,6},{5,7},{6,4},{7,5},{8,10},{9,11},{10,... | collective-permute-start | bytes 589832 | tf_op jit(solution)/shard_map/ppermute | solution.py:333
  14.7 4.4 %collective-permute-start.4 = (bf16[192,768]{1,0:T(8,128)(2,1)S(1)}, bf16[192,768]{1,0:T(8,128)(2,1)S(1)}, u32[]{:S(2)}, u32[]{:S(2)}) collective-permute-start(bf16[192,768]{1,0:T(8,128)(2,1)S(1)} %copy-done.2), channel_id=1, source_target_pairs={{0,1},{1,0},{2,3},{3,2},{4,5},{5,4},{6,7},{7,6},{8,9},{9,8},{10,11... | collective-permute-start | bytes 884744 | tf_op jit(solution)/shard_map/ppermute | solution.py:333
  14.7 5.0 %collective-permute-start.7 = (bf16[192,768]{1,0:T(8,128)(2,1)S(1)}, bf16[192,768]{1,0:T(8,128)(2,1)S(1)}, u32[]{:S(2)}, u32[]{:S(2)}) collective-permute-start(bf16[192,768]{1,0:T(8,128)(2,1)S(1)} %collective-permute-done.6.w_ref), channel_id=1, source_target_pairs={{0,1},{1,0},{2,3},{3,2},{4,5},{5,4},{6,7},{7,6},{8,9},{9,8},{10,11... | collective-permute-start | bytes 884744 | tf_op jit(solution)/shard_map/ppermute | solution.py:333
  15.2 3.9 %collective-permute-start.3 = (bf16[768,128]{1,0:T(8,128)(2,1)S(1)}, bf16[768,128]{1,0:T(8,128)(2,1)S(1)}, u32[]{:S(2)}, u32[]{:S(2)}) collective-permute-start(bf16[768,128]{1,0:T(8,128)(2,1)S(1)} %merge.1.rest_0_), channel_id=1, source_target_pairs={{0,1},{1,0},{2,3},{3,2},{4,5},{5,4},{6,7},{7,6},{8,9},{9,8},{10,11... | collective-permute-start | bytes 589832 | tf_op jit(solution)/shard_map/ppermute | solution.py:333
  19.1 1.4 %collective-permute-start.8 = (bf16[768,128]{1,0:T(8,128)(2,1)S(1)}, bf16[768,128]{1,0:T(8,128)(2,1)S(1)}, u32[]{:S(2)}, u32[]{:S(2)}) collective-permute-start(bf16[768,128]{1,0:T(8,128)(2,1)S(1)} %collective-permute-done.5.attn_ref), channel_id=1, source_target_pairs={{0,1},{1,0},{2,3},{3,2},{4,5},{5,4},{6,7},{7,6},{8,9},{9,8},{10,11... | collective-permute-start | bytes 589832 | tf_op jit(solution)/shard_map/ppermute | solution.py:333

commit v11 on v8

--- a/solution.py
+++ b/solution.py
@@ -203,6 +203,8 @@
     soft_far = [soften(s, factor) for s in s_far]
     am_mid = [weigh(soft_mid[h][1], kv_mid[h], h) for h in heads]
     am_far = [weigh(soft_far[h][1], kv_far[h], h) for h in heads]
+    for copy in copies:
+        copy.wait()
     out_mid, out_far = [], []
     for h in heads:
         peak_mid = jnp.broadcast_to(soft_mid[h][0], am_mid[h].shape)
@@ -214,8 +216,6 @@
             jnp.exp2((near_peak - top) * factor) * near_am
             + jnp.exp2((peak_mid - top) * factor) * am_mid[h]
         )
-    for copy in copies:
-        copy.wait()
     for h in heads:
         shared = pl.ds(fo[h] // R1, far, stride=R2 // R1)
         also = fo[h] % R1 == mo[h]

time: 22 us -> 22 us (level)
  no operation moved by 1% of the time
where the time goes in v11:
time: 22 us; the launch traced here: 21.9 us
  starting transfers between devices  10.5 us (48%)
  waiting for transfers between devices  5.76 us (26%)
  Pallas kernels  5.47 us (25%)
    ppermute x3, starting transfers between devices, local(): lax.ppermute(kvp, 'seq', within(s))  5.56 us
    pallas_call x7, Pallas kernels, call(): pl.pallas_call(kernel, out_shape=outs, in_specs=[IN_SMEM] * len(scalars)...  5.47 us
    ppermute x6, starting transfers between devices, to(): return lax.ppermute(array, 'head', paths[r])  4.93 us
    ppermute x6, waiting for transfers between devices, to(): return lax.ppermute(array, 'head', paths[r])  4.24 us
    ppermute x3, waiting for transfers between devices, local(): lax.ppermute(kvp, 'seq', within(s))  1.52 us
  transfers between devices with their start and end apart: 9, of which 3 were waited for; matrix products, arithmetic and copies ran while one was open for 0% of the time, Pallas kernels for 19%

profile of v11, /device:TPU:0, one launch (start us, length us, event | category | flops | bytes accessed | tf_op | source)
XLA Modules:
  0.0 21.9 jit_solution(12555593279002636684)
XLA Ops:
  0.0 0.0 copy-start.8
  0.0 3.0 %collective-permute-start.6 = (bf16[192,768]{1,0:T(8,128)(2,1)}, bf16[192,768]{1,0:T(8,128)(2,1)S(1)}, u32[]{:S(2)}, u32[]{:S(2)}) collective-permute-start(bf16[192,768]{1,0:T(8,128)(2,1)} %rest_2_.1), channel_id=1, source_target_pairs={{0,2},{1,3},{2,0},{3,1},{4,6},{5,7},{6,4},{7,5},{8,10},{9,11},{10,... | collective-permute-start | bytes 884744 | tf_op jit(solution)/shard_map/ppermute | solution.py:332
  3.1 0.0 copy-done.1
  3.1 0.0 copy-done.3
  3.1 0.0 copy-done.5
  3.1 0.0 copy-done
  3.1 0.0 copy-start.4
  3.1 0.0 copy-start.6
  3.1 0.7 %project.1 = (bf16[512,384]{1,0:T(8,128)(2,1)S(1)}, bf16[240,128]{1,0:T(8,128)(2,1)S(1)}) custom-call(s32[3]{0:T(128)S(1)} %copy-done.3, s32[3]{0:T(128)S(1)} %copy-done.5, bf16[512,768]{1,0:T(8,128)(2,1)S(1)} %copy-done, bf16[3,192,768]{2,1,0:T(8,128)(2,1)S(1)} %bitcast.5, s32[8,128]{1,0:T(8,128)S(1)} %lanes.1.lanes_ref), custom_call_target="tpu_custom_call" | custom-call | flops 301989888 | bytes 4194304 | tf_op jit(solution)/shard_map/project/pallas_call | solution.py:302
  3.8 1.6 %collective-permute-start = (bf16[240,128]{1,0:T(8,128)(2,1)S(1)}, bf16[240,128]{1,0:T(8,128)(2,1)S(1)}, u32[]{:S(2)}, u32[]{:S(2)}) collective-permute-start(bf16[240,128]{1,0:T(8,128)(2,1)S(1)} %get-tuple-element.21.rest_0_.rest_4_), channel_id=1, source_target_pairs={{0,4},{4,8},{8,12},{12,0},{1,5},{5,9},{9,13},{13,1},{2,6},{6,10},{... | collective-permute-start | bytes 184328 | tf_op jit(solution)/shard_map/ppermute | solution.py:377
  5.4 2.6 %collective-permute-start.1 = (bf16[240,128]{1,0:T(8,128)(2,1)S(1)}, bf16[240,128]{1,0:T(8,128)(2,1)S(1)}, u32[]{:S(2)}, u32[]{:S(2)}) collective-permute-start(bf16[240,128]{1,0:T(8,128)(2,1)S(1)} %get-tuple-element.21.rest_0_.rest_4_), channel_id=1, source_target_pairs={{0,8},{4,12},{8,0},{12,4},{1,9},{5,13},{9,1},{13,5},{2,10},{6,14},... | collective-permute-start | bytes 184328 | tf_op jit(solution)/shard_map/ppermute | solution.py:377
  8.0 1.3 %collective-permute-start.2 = (bf16[240,128]{1,0:T(8,128)(2,1)S(1)}, bf16[240,128]{1,0:T(8,128)(2,1)S(1)}, u32[]{:S(2)}, u32[]{:S(2)}) collective-permute-start(bf16[240,128]{1,0:T(8,128)(2,1)S(1)} %get-tuple-element.21.rest_0_.rest_4_), channel_id=1, source_target_pairs={{0,12},{4,0},{8,4},{12,8},{1,13},{5,1},{9,5},{13,9},{2,14},{6,2},{... | collective-permute-start | bytes 184328 | tf_op jit(solution)/shard_map/ppermute | solution.py:377
  9.3 1.7 %near.1 = (f32[768,128]{1,0:T(8,128)S(1)}, f32[240,128]{1,0:T(8,128)S(1)}, f32[240,128]{1,0:T(8,128)S(1)}, bf16[240,128]{1,0:T(8,128)(2,1)S(1)}, f32[2,192]{1,0:T(2,128)S(1)}) custom-call(s32[3]{0:T(128)} %mo_from.5, s32[3]{0:T(128)} %fo_from.5, bf16[512,384]{1,0:T(8,128)(2,1)S(1)} %get-tuple-element.16.kv_ref, bf16[512,768]{1,0:T(8,128)(2,1)S(1)} %copy-done, ...), custom_call_target="tpu_custom_call" | custom-call | flops 536870912 | bytes 4194304 | tf_op jit(solution)/shard_map/near/pallas_call | solution.py:302
  11.1 0.0 collective-permute-done.rest_1_.rest_5_
  11.1 1.5 %collective-permute-done.1.rest_2_.rest_6_ = bf16[240,128]{1,0:T(8,128)(2,1)S(1)} collective-permute-done((bf16[240,128]{1,0:T(8,128)(2,1)S(1)}, bf16[240,128]{1,0:T(8,128)(2,1)S(1)}, u32[]{:S(2)}, u32[]{:S(2)}) %collective-permute-start.1) | collective-permute-done | bytes 61472 | tf_op jit(solution)/shard_map/ppermute | solution.py:377
  12.6 0.0 collective-permute-done.2.rest_3_.rest_7_
  12.6 0.8 %merge.1.rest_0_ = bf16[768,128]{1,0:T(8,128)(2,1)S(1)} custom-call(s32[3]{0:T(128)S(1)} %copy-done.4, s32[3]{0:T(128)S(1)} %copy-done.6, f32[768,128]{1,0:T(8,128)S(1)} %get-tuple-element.17.near_ref, bf16[240,128]{1,0:T(8,128)(2,1)S(1)} %get-tuple-element.18.qp_ref, f32[240,128]{1,0:T(8,128)S(1)} %get-tuple-element.19.am_ref, ...), custom_call_target="tpu_custom_call" | custom-call | flops 536870912 | bytes 4194304 | tf_op jit(solution)/shard_map/merge/pallas_call | solution.py:302
  13.4 1.3 %collective-permute-start.5 = (bf16[768,128]{1,0:T(8,128)(2,1)S(1)}, bf16[768,128]{1,0:T(8,128)(2,1)S(1)}, u32[]{:S(2)}, u32[]{:S(2)}) collective-permute-start(bf16[768,128]{1,0:T(8,128)(2,1)S(1)} %merge.1.rest_0_), channel_id=1, source_target_pairs={{0,2},{1,3},{2,0},{3,1},{4,6},{5,7},{6,4},{7,5},{8,10},{9,11},{10,... | collective-permute-start | bytes 589832 | tf_op jit(solution)/shard_map/ppermute | solution.py:332
  14.7 0.0 copy-done.2
  14.7 0.0 collective-permute-start.4
  14.7 0.0 collective-permute-done.6.w_ref
  14.7 0.5 %collective-permute-start.7 = (bf16[192,768]{1,0:T(8,128)(2,1)S(1)}, bf16[192,768]{1,0:T(8,128)(2,1)S(1)}, u32[]{:S(2)}, u32[]{:S(2)}) collective-permute-start(bf16[192,768]{1,0:T(8,128)(2,1)S(1)} %collective-permute-done.6.w_ref), channel_id=1, source_target_pairs={{0,1},{1,0},{2,3},{3,2},{4,5},{5,4},{6,7},{7,6},{8,9},{9,8},{10,11... | collective-permute-start | bytes 884744 | tf_op jit(solution)/shard_map/ppermute | solution.py:332
  15.2 0.1 collective-permute-start.3
  15.3 3.8 %collective-permute-done.5.attn_ref = bf16[768,128]{1,0:T(8,128)(2,1)S(1)} collective-permute-done((bf16[768,128]{1,0:T(8,128)(2,1)S(1)}, bf16[768,128]{1,0:T(8,128)(2,1)S(1)}, u32[]{:S(2)}, u32[]{:S(2)}) %collective-permute-start.5) | collective-permute-done | bytes 196640 | tf_op jit(solution)/shard_map/ppermute | solution.py:332
  19.1 0.0 collective-permute-start.8
  19.1 0.0 collective-permute-done.3.rest_1_
  19.1 0.0 collective-permute-done.4.rest_3_
  19.1 0.6 %product.1.x_ref = f32[512,768]{1,0:T(8,128)S(1)} custom-call(bf16[512,768]{1,0:T(8,128)(2,1)S(1)} %copy-done, bf16[768,128]{1,0:T(8,128)(2,1)S(1)} %merge.1.rest_0_, bf16[768,128]{1,0:T(8,128)(2,1)S(1)} %collective-permute-done.3.rest_1_, bf16[192,768]{1,0:T(8,128)(2,1)S(1)} %copy-done.2, bf16[192,768]{1,0:T(8,128)(2,1)S(1)} %collective-permute-done.4.rest_3_), custom_call_target="tpu_custom_call" | custom-call | flops 301989888 | bytes 4194304 | tf_op jit(solution)/shard_map/product/pallas_call | solution.py:302
  19.7 0.0 collective-permute-done.7.last_ref.w_ref
  19.7 0.4 %own.1 = (f32[512,768]{1,0:T(8,128)S(1)}, f32[512,192]{1,0:T(8,128)S(1)}, bf16[192,192]{1,0:T(8,128)(2,1)S(1)}) custom-call(s32[1]{0:T(128)} %bitcast.place, f32[512,768]{1,0:T(8,128)S(1)} %product.1.x_ref, bf16[768,128]{1,0:T(8,128)(2,1)S(1)} %collective-permute-done.5.attn_ref, bf16[192,768]{1,0:T(8,128)(2,1)S(1)} %collective-permute-done.6.w_ref, ...), custom_call_target="tpu_custom_call" | custom-call | flops 150994944 | bytes 4194304 | tf_op jit(solution)/shard_map/own/pallas_call | solution.py:302
  20.1 0.4 %collective-permute-done.8.attn_ref = bf16[768,128]{1,0:T(8,128)(2,1)S(1)} collective-permute-done((bf16[768,128]{1,0:T(8,128)(2,1)S(1)}, bf16[768,128]{1,0:T(8,128)(2,1)S(1)}, u32[]{:S(2)}, u32[]{:S(2)}) %collective-permute-start.8) | collective-permute-done | bytes 196640 | tf_op jit(solution)/shard_map/ppermute | solution.py:332
  20.5 1.3 %output.1 = bf16[192,512]{1,0:T(8,128)(2,1)} custom-call(f32[512,768]{1,0:T(8,128)S(1)} %get-tuple-element.23.x_ref, f32[512,192]{1,0:T(8,128)S(1)} %get-tuple-element.24.own_ref, bf16[192,192]{1,0:T(8,128)(2,1)S(1)} %get-tuple-element.25.last_own_ref, f32[2,192]{1,0:T(2,128)S(1)} %get-tuple-element.26.gb_ref, ...), custom_call_target="tpu_custom_call" | custom-call | flops 150994944 | bytes 4194304 | tf_op jit(solution)/shard_map/output/pallas_call | solution.py:302
  (11 shorter events, 0.0 us)
Async XLA Ops:
  0.0 3.1 %copy-start.1 = (bf16[3,768,192]{1,2,0:T(8,128)(2,1)S(1)}, bf16[3,768,192]{1,2,0:T(8,128)(2,1)}, u32[]{:S(2)}) copy-start(bf16[3,768,192]{1,2,0:T(8,128)(2,1)} %param.8) | copy-start | bytes 2654212
  0.0 3.1 %copy-start.3 = (s32[3]{0:T(128)S(1)}, s32[3]{0:T(128)}, u32[]{:S(2)}) copy-start(s32[3]{0:T(128)} %mo_from.5) | copy-start | bytes 40
  0.0 3.1 %copy-start.5 = (s32[3]{0:T(128)S(1)}, s32[3]{0:T(128)}, u32[]{:S(2)}) copy-start(s32[3]{0:T(128)} %fo_from.5) | copy-start | bytes 40
  0.0 3.1 %copy-start = (bf16[512,768]{1,0:T(8,128)(2,1)S(1)}, bf16[512,768]{1,0:T(8,128)(2,1)}, u32[]{:S(2)}) copy-start(bf16[512,768]{1,0:T(8,128)(2,1)} %x_ref.5) | copy-start | bytes 2359300
  0.0 9.3 %copy-start.7 = (f32[192]{0:T(256)S(1)}, f32[192]{0:T(256)}, u32[]{:S(2)}) copy-start(f32[192]{0:T(256)} %param.10) | copy-start | bytes 2308
  0.0 9.3 %copy-start.8 = (f32[192]{0:T(256)S(1)}, f32[192]{0:T(256)}, u32[]{:S(2)}) copy-start(f32[192]{0:T(256)} %param.11) | copy-start | bytes 2308
  0.0 14.7 %collective-permute-start.6 = (bf16[192,768]{1,0:T(8,128)(2,1)}, bf16[192,768]{1,0:T(8,128)(2,1)S(1)}, u32[]{:S(2)}, u32[]{:S(2)}) collective-permute-start(bf16[192,768]{1,0:T(8,128)(2,1)} %rest_2_.1), channel_id=1, source_target_pairs={{0,2},{1,3},{2,0},{3,1},{4,6},{5,7},{6,4},{7,5},{8,10},{9,11},{10,... | collective-permute-start | bytes 884744 | tf_op jit(solution)/shard_map/ppermute | solution.py:332
  3.1 9.5 %copy-start.4 = (s32[3]{0:T(128)S(1)}, s32[3]{0:T(128)}, u32[]{:S(2)}) copy-start(s32[3]{0:T(128)} %mo_from.5) | copy-start | bytes 40
  3.1 9.5 %copy-start.6 = (s32[3]{0:T(128)S(1)}, s32[3]{0:T(128)}, u32[]{:S(2)}) copy-start(s32[3]{0:T(128)} %fo_from.5) | copy-start | bytes 40
  3.8 7.3 %collective-permute-start = (bf16[240,128]{1,0:T(8,128)(2,1)S(1)}, bf16[240,128]{1,0:T(8,128)(2,1)S(1)}, u32[]{:S(2)}, u32[]{:S(2)}) collective-permute-start(bf16[240,128]{1,0:T(8,128)(2,1)S(1)} %get-tuple-element.21.rest_0_.rest_4_), channel_id=1, source_target_pairs={{0,4},{4,8},{8,12},{12,0},{1,5},{5,9},{9,13},{13,1},{2,6},{6,10},{... | collective-permute-start | bytes 184328 | tf_op jit(solution)/shard_map/ppermute | solution.py:377
  5.4 7.2 %collective-permute-start.1 = (bf16[240,128]{1,0:T(8,128)(2,1)S(1)}, bf16[240,128]{1,0:T(8,128)(2,1)S(1)}, u32[]{:S(2)}, u32[]{:S(2)}) collective-permute-start(bf16[240,128]{1,0:T(8,128)(2,1)S(1)} %get-tuple-element.21.rest_0_.rest_4_), channel_id=1, source_target_pairs={{0,8},{4,12},{8,0},{12,4},{1,9},{5,13},{9,1},{13,5},{2,10},{6,14},... | collective-permute-start | bytes 184328 | tf_op jit(solution)/shard_map/ppermute | solution.py:377
  8.0 4.6 %collective-permute-start.2 = (bf16[240,128]{1,0:T(8,128)(2,1)S(1)}, bf16[240,128]{1,0:T(8,128)(2,1)S(1)}, u32[]{:S(2)}, u32[]{:S(2)}) collective-permute-start(bf16[240,128]{1,0:T(8,128)(2,1)S(1)} %get-tuple-element.21.rest_0_.rest_4_), channel_id=1, source_target_pairs={{0,12},{4,0},{8,4},{12,8},{1,13},{5,1},{9,5},{13,9},{2,14},{6,2},{... | collective-permute-start | bytes 184328 | tf_op jit(solution)/shard_map/ppermute | solution.py:377
  9.3 5.4 %copy-start.2 = (bf16[192,768]{1,0:T(8,128)(2,1)S(1)}, bf16[192,768]{1,0:T(8,128)(2,1)}, u32[]{:S(2)}) copy-start(bf16[192,768]{1,0:T(8,128)(2,1)} %rest_2_.1) | copy-start | bytes 884740
  13.4 5.7 %collective-permute-start.5 = (bf16[768,128]{1,0:T(8,128)(2,1)S(1)}, bf16[768,128]{1,0:T(8,128)(2,1)S(1)}, u32[]{:S(2)}, u32[]{:S(2)}) collective-permute-start(bf16[768,128]{1,0:T(8,128)(2,1)S(1)} %merge.1.rest_0_), channel_id=1, source_target_pairs={{0,2},{1,3},{2,0},{3,1},{4,6},{5,7},{6,4},{7,5},{8,10},{9,11},{10,... | collective-permute-start | bytes 589832 | tf_op jit(solution)/shard_map/ppermute | solution.py:332
  14.7 4.4 %collective-permute-start.4 = (bf16[192,768]{1,0:T(8,128)(2,1)S(1)}, bf16[192,768]{1,0:T(8,128)(2,1)S(1)}, u32[]{:S(2)}, u32[]{:S(2)}) collective-permute-start(bf16[192,768]{1,0:T(8,128)(2,1)S(1)} %copy-done.2), channel_id=1, source_target_pairs={{0,1},{1,0},{2,3},{3,2},{4,5},{5,4},{6,7},{7,6},{8,9},{9,8},{10,11... | collective-permute-start | bytes 884744 | tf_op jit(solution)/shard_map/ppermute | solution.py:332
  14.7 5.0 %collective-permute-start.7 = (bf16[192,768]{1,0:T(8,128)(2,1)S(1)}, bf16[192,768]{1,0:T(8,128)(2,1)S(1)}, u32[]{:S(2)}, u32[]{:S(2)}) collective-permute-start(bf16[192,768]{1,0:T(8,128)(2,1)S(1)} %collective-permute-done.6.w_ref), channel_id=1, source_target_pairs={{0,1},{1,0},{2,3},{3,2},{4,5},{5,4},{6,7},{7,6},{8,9},{9,8},{10,11... | collective-permute-start | bytes 884744 | tf_op jit(solution)/shard_map/ppermute | solution.py:332
  15.2 3.9 %collective-permute-start.3 = (bf16[768,128]{1,0:T(8,128)(2,1)S(1)}, bf16[768,128]{1,0:T(8,128)(2,1)S(1)}, u32[]{:S(2)}, u32[]{:S(2)}) collective-permute-start(bf16[768,128]{1,0:T(8,128)(2,1)S(1)} %merge.1.rest_0_), channel_id=1, source_target_pairs={{0,1},{1,0},{2,3},{3,2},{4,5},{5,4},{6,7},{7,6},{8,9},{9,8},{10,11... | collective-permute-start | bytes 589832 | tf_op jit(solution)/shard_map/ppermute | solution.py:332
  19.1 1.4 %collective-permute-start.8 = (bf16[768,128]{1,0:T(8,128)(2,1)S(1)}, bf16[768,128]{1,0:T(8,128)(2,1)S(1)}, u32[]{:S(2)}, u32[]{:S(2)}) collective-permute-start(bf16[768,128]{1,0:T(8,128)(2,1)S(1)} %collective-permute-done.5.attn_ref), channel_id=1, source_target_pairs={{0,1},{1,0},{2,3},{3,2},{4,5},{5,4},{6,7},{7,6},{8,9},{9,8},{10,11... | collective-permute-start | bytes 589832 | tf_op jit(solution)/shard_map/ppermute | solution.py:332
